TPU v7x, 512 devices: a whole 4x8x8 slice. The times are simulated.
512 devices in a mesh: depth: 64 (over y, x, core), az: 8 (over z).
Axes of the slice: x: 4, y: 8, z: 8, core: 2. Of those that a mesh axis runs over, the one named last changes fastest.
Arguments:
- velocity: float32 [6, 1024, 64, 128], P(None, 'depth', 'az'), may hold values from -6 to 6
- stress: float32 [7, 1024, 64, 128], P(None, 'depth', 'az'), may hold values from -6 to 6
- memory: float32 [12, 1024, 64, 128], P(None, 'depth', 'az'), may hold values from -3 to 3
- layer_ids: int32 [256, 32], P('depth'), may hold values from 0 to 7, as said below
- materials: float32 [8, 8], replicated, may hold values from 0.006 to 4, as said below
- jkd: float32 [8, 9], replicated, may hold values from 0.1 to 60, as said below
- source_depth: int32 [1], replicated, may hold values from 0 to 1023
Outputs:
- velocity_out: float32 [6, 1024, 64, 128], P(None, 'depth', 'az')
- stress_out: float32 [7, 1024, 64, 128], P(None, 'depth', 'az')
- memory_out: float32 [12, 1024, 64, 128], P(None, 'depth', 'az')
Inputs may be any that keep to these rules, and one draw needn't show every extreme that they name: `layer_ids`: the first 4 radial elements hold 0 (borehole fluid); beyond them each depth element holds one formation row of 1 to 7 for all its radial elements. `materials`: columns: lambda0 0.5 to 1.5, shear modulus 0.3 to 1 (row 0: 0.006 to 0.02), M 0.5 to 1.5, beta 0.3 to 0.9, bulk density 1.5 to 2.5, fluid density 0.8 to 1.2, tortuosity 1.5 to 4, friction 0.5 to 2. `jkd`: omega 0.5 to 5, pole weights 0.1 to 1, pole rates 0.3 to 60.
All inputs are finite; a program needn't handle non-finite values.
Results may differ from a plain program's by a relative error of at most 0.0001.
Values sent between devices are 32-bit elements; how exact they have to be, the bound alone decides.
No kernel may reach another device: no remote copies, remote signals or barrier semaphores. Data moves between devices by JAX's collectives and lax.ppermute only.
A program may use at most 128 MiB of HBM per device.

v0:
```python
import math

import jax
import jax.numpy as jnp
import numpy as np
from jax import lax
from jax.sharding import PartitionSpec as P

NR = 128
NT = 64
STEPS = 2
RB = 4


DT = 0.02
SOURCE_GAIN = 40.0
R_INNER = 1.0
HIGHEST = lax.Precision.HIGHEST


def from_behind(value, axis, steps):
    count = lax.axis_size(axis)
    first, last = (max(0, -steps), min(count, count - steps))
    return lax.ppermute(value, axis, [(source, source + steps) for source in range(first, last)])


def gll_basis():
    root_value = math.sqrt(3.0 / 7.0)
    gll_nodes = np.array([-1.0, -root_value, 0.0, root_value, 1.0])
    weights = np.array([0.1, 49.0 / 90.0, 32.0 / 45.0, 49.0 / 90.0, 0.1])
    offsets = gll_nodes[:, None] - gll_nodes[None, :] + np.eye(5)
    factors = np.prod(offsets, axis=1)
    derivative = factors[:, None] / factors[None, :] / offsets
    diagonal_part = np.sum(1.0 / offsets, axis=1) - 1.0
    derivative = derivative * (1.0 - np.eye(5)) + np.eye(5) * diagonal_part[:, None]
    return (gll_nodes, weights, derivative)


def radial_operator(node_count):
    gll_nodes, weights, derivative = gll_basis()
    full_count = node_count + 1
    stencil = weights[:, None] * derivative * 2.0
    assembled = np.zeros((full_count, full_count))
    node_mass = np.zeros(full_count)
    for element in range(node_count // 4):
        assembled[4 * element : 4 * element + 5, 4 * element : 4 * element + 5] += stencil
        node_mass[4 * element : 4 * element + 5] += weights
    return (assembled / node_mass[:, None])[:node_count, :node_count]


def radial_positions(node_count):
    gll_nodes, weights, derivative = gll_basis()
    positions = np.arange(node_count)
    return R_INNER + positions // 4 + 0.5 * (1.0 + gll_nodes[positions % 4])


def azimuth_operator(node_count):
    positions = np.arange(node_count)
    offsets = positions[:, None] - positions[None, :]
    wave_modes = np.arange(1, node_count // 2)
    phases = 2.0 * np.pi * offsets[:, :, None] * wave_modes[None, None, :] / node_count
    return -(2.0 / node_count) * np.sum(wave_modes * np.sin(phases), axis=2)


def node_coefficients(layer_ids, materials, jkd):
    combined = jnp.concatenate([materials, jkd], axis=1)
    row_count = combined.shape[0]
    picks = (layer_ids[:, :, None] == jnp.arange(row_count, dtype=jnp.int32)[None, None, :]).astype(
        jnp.float32
    )
    per_element = jnp.sum(picks[:, :, :, None] * combined[None, None], axis=2)
    per_node = jnp.repeat(jnp.repeat(per_element, 4, axis=0), 4, axis=1)
    return jnp.moveaxis(per_node, 2, 0)[:, :, None, :]


def depth_derivative(fields):
    gll_nodes, weights, derivative = gll_basis()
    stencil = jnp.asarray(weights[:, None] * derivative * 2.0, jnp.float32)
    comps, depth_count, azim_count, radial_count = fields.shape
    elements = depth_count // 4
    first_device = lax.axis_index("depth") == 0
    above_plane = from_behind(fields[:, :1], "depth", -1)
    extended = jnp.concatenate([fields, above_plane], axis=1)
    blocks = jnp.concatenate(
        [
            fields.reshape(comps, elements, 4, azim_count, radial_count),
            extended[:, 4::4][:, :, None],
        ],
        axis=2,
    )
    contrib = jnp.einsum("ij,cejtr->ceitr", stencil, blocks, precision=HIGHEST)
    incoming = from_behind(contrib[:, -1, 4], "depth", 1)
    shifted = jnp.concatenate([incoming[:, None], contrib[:, :-1, 4]], axis=1)
    first_node = contrib[:, :, 0] + shifted
    assembled = jnp.concatenate([first_node[:, :, None], contrib[:, :, 1:4]], axis=2)
    inner_mass = jnp.asarray(
        np.array([weights[0] + weights[4], weights[1], weights[2], weights[3]]), jnp.float32
    )
    node_mass = jnp.broadcast_to(inner_mass, (elements, 4))
    bottom_mass = jnp.where(first_device, weights[0], weights[0] + weights[4]).astype(jnp.float32)
    first_column = jnp.concatenate([bottom_mass[None], node_mass[1:, 0]])
    node_mass = jnp.concatenate([first_column[:, None], node_mass[:, 1:]], axis=1)
    return (assembled / node_mass[None, :, :, None, None]).reshape(
        comps, depth_count, azim_count, radial_count
    )


def radial_derivative(fields, radial_matrix):
    return jnp.einsum("ij,cztj->czti", radial_matrix, fields, precision=HIGHEST)


def azimuth_derivative(fields, azimuth_matrix):
    local_deriv = jnp.einsum(
        "ts,czsr->cztr",
        azimuth_matrix,
        lax.all_to_all(fields, "az", split_axis=1, concat_axis=2, tiled=True),
        precision=HIGHEST,
    )
    return lax.all_to_all(local_deriv, "az", split_axis=2, concat_axis=1, tiled=True)


def on_device(velocity, stress, memory, layer_ids, materials, jkd, source_depth):
    coeffs = node_coefficients(layer_ids, materials, jkd)
    radial_matrix = jnp.asarray(radial_operator(NR), jnp.float32)
    azimuth_matrix = jnp.asarray(azimuth_operator(NT), jnp.float32)
    inverse_r = jnp.asarray(1.0 / radial_positions(NR), jnp.float32)
    radial_index = jnp.arange(NR, dtype=jnp.int32)

    def radial_fn(fields):
        return radial_derivative(fields, radial_matrix)

    def azim_fn(fields):
        return azimuth_derivative(fields, azimuth_matrix)

    lame_zero, shear_mod, modulus, coupling = (coeffs[0], coeffs[1], coeffs[2], coeffs[3])
    density, fluid_density, tortuosity, friction = (coeffs[4], coeffs[5], coeffs[6], coeffs[7])
    relax_omega = coeffs[8]
    pole_weights = coeffs[9:13][:, None]
    pole_rates = coeffs[13:17][:, None]
    fluid_inertia = fluid_density * tortuosity
    determinant = density * fluid_inertia - fluid_density * fluid_density
    lame_fluid = lame_zero + coupling * coupling * modulus
    depth_count, azim_count, radial_count = (
        velocity.shape[1],
        velocity.shape[2],
        velocity.shape[3],
    )
    plane_index = lax.axis_index("depth") * depth_count + jnp.arange(depth_count, dtype=jnp.int32)
    source_mask = (
        (plane_index == source_depth[0])[:, None, None] & (radial_index < 4 * RB)[None, None, :]
    ).astype(jnp.float32)
    memory_state = memory.reshape(4, 3, depth_count, azim_count, radial_count)
    solid_vel, fluid_vel = (velocity[:3], velocity[3:])
    fields = stress
    for time_step in range(STEPS):
        radial_d = radial_fn(jnp.stack([fields[0], fields[3], fields[4], fields[6]]))
        azim_d = azim_fn(jnp.stack([fields[3], fields[1], fields[5], fields[6]])) * inverse_r
        depth_d = depth_derivative(jnp.stack([fields[4], fields[5], fields[2], fields[6]]))
        stress_div = jnp.stack(
            [
                radial_d[0] + azim_d[0] + depth_d[0] + (fields[0] - fields[1]) * inverse_r,
                radial_d[1] + azim_d[1] + depth_d[1] + 2.0 * fields[3] * inverse_r,
                radial_d[2] + azim_d[2] + depth_d[2] + fields[4] * inverse_r,
            ]
        )
        resist = jnp.stack([radial_d[3], azim_d[3], depth_d[3]]) + friction * jnp.sum(
            pole_weights * memory_state, axis=0
        )
        solid_vel = (
            solid_vel + DT * (fluid_inertia * stress_div + fluid_density * resist) / determinant
        )
        fluid_step = -DT * (fluid_density * stress_div + density * resist) / determinant
        fluid_vel = fluid_vel + fluid_step
        memory_state = (memory_state + fluid_step + DT * relax_omega * fluid_vel) / (
            1.0 + DT * (pole_rates + relax_omega)
        )
        radial_d = radial_fn(jnp.stack([solid_vel[0], solid_vel[1], solid_vel[2], fluid_vel[0]]))
        azim_d = (
            azim_fn(jnp.stack([solid_vel[0], solid_vel[1], solid_vel[2], fluid_vel[1]])) * inverse_r
        )
        depth_d = depth_derivative(
            jnp.stack([solid_vel[0], solid_vel[1], solid_vel[2], fluid_vel[2]])
        )
        strain_rr = radial_d[0]
        strain_tt = solid_vel[0] * inverse_r + azim_d[1]
        strain_zz = depth_d[2]
        shear_rt = azim_d[0] + radial_d[1] - solid_vel[1] * inverse_r
        shear_rz = depth_d[0] + radial_d[2]
        shear_tz = depth_d[1] + azim_d[2]
        div_solid = strain_rr + strain_tt + strain_zz
        div_fluid = radial_d[3] + fluid_vel[0] * inverse_r + azim_d[3] + depth_d[3]
        bulk_term = lame_fluid * div_solid + coupling * modulus * div_fluid
        source_term = DT * SOURCE_GAIN * math.cos(0.9 * time_step) * source_mask
        fields = jnp.stack(
            [
                fields[0] + DT * (bulk_term + 2.0 * shear_mod * strain_rr),
                fields[1] + DT * (bulk_term + 2.0 * shear_mod * strain_tt),
                fields[2] + DT * (bulk_term + 2.0 * shear_mod * strain_zz),
                fields[3] + DT * shear_mod * shear_rt,
                fields[4] + DT * shear_mod * shear_rz,
                fields[5] + DT * shear_mod * shear_tz,
                fields[6] - DT * modulus * (coupling * div_solid + div_fluid) + source_term,
            ]
        )
    velocity_out = jnp.concatenate([solid_vel, fluid_vel], axis=0)
    memory_out = memory_state.reshape(12, depth_count, azim_count, radial_count)
    return (velocity_out, fields, memory_out)


def solution(mesh):
    return jax.shard_map(
        on_device,
        mesh=mesh,
        in_specs=(
            P(None, "depth", "az", None),
            P(None, "depth", "az", None),
            P(None, "depth", "az", None),
            P("depth", None),
            P(),
            P(),
            P(),
        ),
        out_specs=(
            P(None, "depth", "az", None),
            P(None, "depth", "az", None),
            P(None, "depth", "az", None),
        ),
        check_vma=False,
    )
```

profile of v0, /device:TPU:32, one launch (start us, length us, event | category | flops | bytes accessed | tf_op | source)
XLA Modules:
  0.0 168.8 jit_solution(9060895452545561654)
XLA Ops:
  0.6 1.0 fusion.93
  1.9 4.0 %collective-permute-start = (f32[4,1,8,128]{3,2,1,0:T(8,128)S(1)}, f32[4,1,8,128]{3,2,1,0:T(8,128)S(1)}, u32[]{:S(2)}, u32[]{:S(2)}) collective-permute-start(f32[4,1,8,128]{3,2,1,0:T(8,128)S(1)} %slice.539), channel_id=1, source_target_pairs={{8,0},{16,8},{24,16},{32,24},{40,32},{48,40},{56,48},{64,56},{72,6... | collective-permute-start | bytes 49160 | tf_op jit(solution)/shard_map/ppermute | solution.py:24
  5.9 0.7 pad_maximum_fusion.19
  6.6 10.3 %all-to-all-start = ((f32[4,16,8,128]{3,2,0,1:T(8,128)}), f32[4,16,8,128]{3,2,0,1:T(8,128)S(1)}, u32[]{:S(2)}, u32[]{:S(2)}) async-start(f32[4,16,8,128]{3,2,0,1:T(8,128)} %pad_maximum_fusion.19), calls=%async_computation | async-start | bytes 524288 | tf_op jit(solution)/shard_map/all_to_all | solution.py:116
  20.1 0.7 and_select_fusion
  22.0 0.7 convolution_bitcast_fusion.3
  22.7 1.9 %collective-permute-start.1 = (f32[4,8,128]{2,1,0:T(8,128)S(1)}, f32[4,8,128]{2,1,0:T(8,128)S(1)}, u32[]{:S(2)}, u32[]{:S(2)}) collective-permute-start(f32[4,8,128]{2,1,0:T(8,128)S(1)} %bitcast.260), channel_id=1, source_target_pairs={{0,8},{8,16},{16,24},{24,32},{32,40},{40,48},{48,56},{56,64},{64,7... | collective-permute-start | bytes 49160 | tf_op jit(solution)/shard_map/ppermute | solution.py:24
  24.8 6.2 %collective-permute-done.1 = f32[4,8,128]{2,1,0:T(8,128)S(1)} collective-permute-done((f32[4,8,128]{2,1,0:T(8,128)S(1)}, f32[4,8,128]{2,1,0:T(8,128)S(1)}, u32[]{:S(2)}, u32[]{:S(2)}) %collective-permute-start.1) | collective-permute-done | bytes 16416 | tf_op jit(solution)/shard_map/ppermute | solution.py:24
  32.2 0.9 copy.485
  33.1 7.2 %all-to-all-start.1 = ((f32[4,2,64,128]{3,1,0,2:T(2,128)}), f32[4,2,64,128]{3,1,0,2:T(2,128)S(1)}, u32[]{:S(2)}, u32[]{:S(2)}) async-start(f32[4,2,64,128]{3,1,0,2:T(2,128)} %copy.485), calls=%async_computation.1 | async-start | bytes 524288 | tf_op jit(solution)/shard_map/all_to_all | solution.py:119
  40.5 10.2 %all-to-all-done.1 = f32[4,2,64,128]{3,1,0,2:T(2,128)S(1)} async-done(((f32[4,2,64,128]{3,1,0,2:T(2,128)}), f32[4,2,64,128]{3,1,0,2:T(2,128)S(1)}, u32[]{:S(2)}, u32[]{:S(2)}) %all-to-all-start.1) | async-done | bytes 262176 | tf_op jit(solution)/shard_map/all_to_all | solution.py:119
  52.3 0.9 copy-done.7
  53.4 1.9 %collective-permute-start.2 = (f32[4,1,8,128]{3,2,1,0:T(8,128)S(1)}, f32[4,1,8,128]{3,2,1,0:T(8,128)S(1)}, u32[]{:S(2)}, u32[]{:S(2)}) collective-permute-start(f32[4,1,8,128]{3,2,1,0:T(8,128)S(1)} %fusion.76), channel_id=1, source_target_pairs={{8,0},{16,8},{24,16},{32,24},{40,32},{48,40},{56,48},{64,56},{72,6... | collective-permute-start | bytes 49160 | tf_op jit(solution)/shard_map/ppermute | solution.py:24
  55.8 0.7 copy.494
  56.6 3.4 %all-to-all-start.2 = ((f32[4,16,8,128]{3,2,0,1:T(8,128)}), f32[4,16,8,128]{3,2,0,1:T(8,128)S(1)}, u32[]{:S(2)}, u32[]{:S(2)}) async-start(f32[4,16,8,128]{3,2,0,1:T(8,128)} %copy.494), calls=%async_computation.2 | async-start | bytes 524288 | tf_op jit(solution)/shard_map/all_to_all | solution.py:116
  60.1 0.7 convolution_bitcast_fusion.2
  60.7 2.4 %collective-permute-start.3 = (f32[4,8,128]{2,1,0:T(8,128)S(1)}, f32[4,8,128]{2,1,0:T(8,128)S(1)}, u32[]{:S(2)}, u32[]{:S(2)}) collective-permute-start(f32[4,8,128]{2,1,0:T(8,128)S(1)} %bitcast.258), channel_id=1, source_target_pairs={{0,8},{8,16},{16,24},{24,32},{32,40},{40,48},{48,56},{56,64},{64,7... | collective-permute-start | bytes 49160 | tf_op jit(solution)/shard_map/ppermute | solution.py:24
  63.5 5.7 %collective-permute-done.3 = f32[4,8,128]{2,1,0:T(8,128)S(1)} collective-permute-done((f32[4,8,128]{2,1,0:T(8,128)S(1)}, f32[4,8,128]{2,1,0:T(8,128)S(1)}, u32[]{:S(2)}, u32[]{:S(2)}) %collective-permute-start.3) | collective-permute-done | bytes 16416 | tf_op jit(solution)/shard_map/ppermute | solution.py:24
  69.4 3.3 %all-to-all-done.2 = f32[4,16,8,128]{3,2,0,1:T(8,128)S(1)} async-done(((f32[4,16,8,128]{3,2,0,1:T(8,128)}), f32[4,16,8,128]{3,2,0,1:T(8,128)S(1)}, u32[]{:S(2)}, u32[]{:S(2)}) %all-to-all-start.2) | async-done | bytes 262176 | tf_op jit(solution)/shard_map/all_to_all | solution.py:116
  73.1 0.9 copy.496
  74.0 3.8 %all-to-all-start.3 = ((f32[4,2,64,128]{3,1,0,2:T(2,128)}), f32[4,2,64,128]{3,1,0,2:T(2,128)S(1)}, u32[]{:S(2)}, u32[]{:S(2)}) async-start(f32[4,2,64,128]{3,1,0,2:T(2,128)} %copy.496), calls=%async_computation.3 | async-start | bytes 524288 | tf_op jit(solution)/shard_map/all_to_all | solution.py:119
  77.9 11.8 %all-to-all-done.3 = f32[4,2,64,128]{3,1,0,2:T(2,128)S(1)} async-done(((f32[4,2,64,128]{3,1,0,2:T(2,128)}), f32[4,2,64,128]{3,1,0,2:T(2,128)S(1)}, u32[]{:S(2)}, u32[]{:S(2)}) %all-to-all-start.3) | async-done | bytes 262176 | tf_op jit(solution)/shard_map/all_to_all | solution.py:119
  91.4 1.9 %collective-permute-start.4 = (f32[4,1,8,128]{3,2,1,0:T(8,128)S(1)}, f32[4,1,8,128]{3,2,1,0:T(8,128)S(1)}, u32[]{:S(2)}, u32[]{:S(2)}) collective-permute-start(f32[4,1,8,128]{3,2,1,0:T(8,128)S(1)} %pad_maximum_fusion.22), channel_id=1, source_target_pairs={{8,0},{16,8},{24,16},{32,24},{40,32},{48,40},{56,48},{64,56},{72,6... | collective-permute-start | bytes 49160 | tf_op jit(solution)/shard_map/ppermute | solution.py:24
  93.3 0.7 copy.505
  94.1 3.4 %all-to-all-start.4 = ((f32[4,16,8,128]{3,2,0,1:T(8,128)}), f32[4,16,8,128]{3,2,0,1:T(8,128)S(1)}, u32[]{:S(2)}, u32[]{:S(2)}) async-start(f32[4,16,8,128]{3,2,0,1:T(8,128)} %copy.505), calls=%async_computation.4 | async-start | bytes 524288 | tf_op jit(solution)/shard_map/all_to_all | solution.py:116
  97.6 0.7 copy-done.22
  99.0 2.4 %collective-permute-start.5 = (f32[4,8,128]{2,1,0:T(8,128)S(1)}, f32[4,8,128]{2,1,0:T(8,128)S(1)}, u32[]{:S(2)}, u32[]{:S(2)}) collective-permute-start(f32[4,8,128]{2,1,0:T(8,128)S(1)} %bitcast.259), channel_id=1, source_target_pairs={{0,8},{8,16},{16,24},{24,32},{32,40},{40,48},{48,56},{56,64},{64,7... | collective-permute-start | bytes 49160 | tf_op jit(solution)/shard_map/ppermute | solution.py:24
  101.9 5.4 %collective-permute-done.5 = f32[4,8,128]{2,1,0:T(8,128)S(1)} collective-permute-done((f32[4,8,128]{2,1,0:T(8,128)S(1)}, f32[4,8,128]{2,1,0:T(8,128)S(1)}, u32[]{:S(2)}, u32[]{:S(2)}) %collective-permute-start.5) | collective-permute-done | bytes 16416 | tf_op jit(solution)/shard_map/ppermute | solution.py:24
  107.5 2.8 %all-to-all-done.4 = f32[4,16,8,128]{3,2,0,1:T(8,128)S(1)} async-done(((f32[4,16,8,128]{3,2,0,1:T(8,128)}), f32[4,16,8,128]{3,2,0,1:T(8,128)S(1)}, u32[]{:S(2)}, u32[]{:S(2)}) %all-to-all-start.4) | async-done | bytes 262176 | tf_op jit(solution)/shard_map/all_to_all | solution.py:116
  110.6 0.9 copy.507
  111.5 5.1 %all-to-all-start.5 = ((f32[4,2,64,128]{3,1,0,2:T(2,128)}), f32[4,2,64,128]{3,1,0,2:T(2,128)S(1)}, u32[]{:S(2)}, u32[]{:S(2)}) async-start(f32[4,2,64,128]{3,1,0,2:T(2,128)} %copy.507), calls=%async_computation.5 | async-start | bytes 524288 | tf_op jit(solution)/shard_map/all_to_all | solution.py:119
  116.9 10.5 %all-to-all-done.5 = f32[4,2,64,128]{3,1,0,2:T(2,128)S(1)} async-done(((f32[4,2,64,128]{3,1,0,2:T(2,128)}), f32[4,2,64,128]{3,1,0,2:T(2,128)S(1)}, u32[]{:S(2)}, u32[]{:S(2)}) %all-to-all-start.5) | async-done | bytes 262176 | tf_op jit(solution)/shard_map/all_to_all | solution.py:119
  128.2 0.8 broadcast_multiply_fusion.4
  129.1 2.4 %collective-permute-start.6 = (f32[4,1,8,128]{3,2,1,0:T(8,128)S(1)}, f32[4,1,8,128]{3,2,1,0:T(8,128)S(1)}, u32[]{:S(2)}, u32[]{:S(2)}) collective-permute-start(f32[4,1,8,128]{3,2,1,0:T(8,128)S(1)} %fusion.75), channel_id=1, source_target_pairs={{8,0},{16,8},{24,16},{32,24},{40,32},{48,40},{56,48},{64,56},{72,6... | collective-permute-start | bytes 49160 | tf_op jit(solution)/shard_map/ppermute | solution.py:24
  131.5 0.7 copy.519
  132.3 3.4 %all-to-all-start.6 = ((f32[4,16,8,128]{3,2,0,1:T(8,128)}), f32[4,16,8,128]{3,2,0,1:T(8,128)S(1)}, u32[]{:S(2)}, u32[]{:S(2)}) async-start(f32[4,16,8,128]{3,2,0,1:T(8,128)} %copy.519), calls=%async_computation.6 | async-start | bytes 524288 | tf_op jit(solution)/shard_map/all_to_all | solution.py:116
  136.9 0.7 convolution_bitcast_fusion
  137.5 1.9 %collective-permute-start.7 = (f32[4,8,128]{2,1,0:T(8,128)S(1)}, f32[4,8,128]{2,1,0:T(8,128)S(1)}, u32[]{:S(2)}, u32[]{:S(2)}) collective-permute-start(f32[4,8,128]{2,1,0:T(8,128)S(1)} %bitcast.257), channel_id=1, source_target_pairs={{0,8},{8,16},{16,24},{24,32},{32,40},{40,48},{48,56},{56,64},{64,7... | collective-permute-start | bytes 49160 | tf_op jit(solution)/shard_map/ppermute | solution.py:24
  139.5 0.8 pad_maximum_fusion
  140.5 1.1 fusion
  141.7 4.2 %collective-permute-done.7 = f32[4,8,128]{2,1,0:T(8,128)S(1)} collective-permute-done((f32[4,8,128]{2,1,0:T(8,128)S(1)}, f32[4,8,128]{2,1,0:T(8,128)S(1)}, u32[]{:S(2)}, u32[]{:S(2)}) %collective-permute-start.7) | collective-permute-done | bytes 16416 | tf_op jit(solution)/shard_map/ppermute | solution.py:24
  146.0 1.9 %all-to-all-done.6 = f32[4,16,8,128]{3,2,0,1:T(8,128)S(1)} async-done(((f32[4,16,8,128]{3,2,0,1:T(8,128)}), f32[4,16,8,128]{3,2,0,1:T(8,128)S(1)}, u32[]{:S(2)}, u32[]{:S(2)}) %all-to-all-start.6) | async-done | bytes 262176 | tf_op jit(solution)/shard_map/all_to_all | solution.py:116
  148.3 0.9 copy.521
  149.2 6.0 %all-to-all-start.7 = ((f32[4,2,64,128]{3,1,0,2:T(2,128)}), f32[4,2,64,128]{3,1,0,2:T(2,128)S(1)}, u32[]{:S(2)}, u32[]{:S(2)}) async-start(f32[4,2,64,128]{3,1,0,2:T(2,128)} %copy.521), calls=%async_computation.7 | async-start | bytes 524288 | tf_op jit(solution)/shard_map/all_to_all | solution.py:119
  155.5 10.2 %all-to-all-done.7 = f32[4,2,64,128]{3,1,0,2:T(2,128)S(1)} async-done(((f32[4,2,64,128]{3,1,0,2:T(2,128)}), f32[4,2,64,128]{3,1,0,2:T(2,128)S(1)}, u32[]{:S(2)}, u32[]{:S(2)}) %all-to-all-start.7) | async-done | bytes 262176 | tf_op jit(solution)/shard_map/all_to_all | solution.py:119
  166.4 0.7 copy-done.12
  167.3 0.7 copy-done.14
  168.0 0.8 copy-done.26
  (183 shorter events, 15.9 us)
Async XLA Ops:
  0.6 1.2 copy-start.1
  1.9 19.6 %collective-permute-start = (f32[4,1,8,128]{3,2,1,0:T(8,128)S(1)}, f32[4,1,8,128]{3,2,1,0:T(8,128)S(1)}, u32[]{:S(2)}, u32[]{:S(2)}) collective-permute-start(f32[4,1,8,128]{3,2,1,0:T(8,128)S(1)} %slice.539), channel_id=1, source_target_pairs={{8,0},{16,8},{24,16},{32,24},{40,32},{48,40},{56,48},{64,56},{72,6... | collective-permute-start | bytes 49160 | tf_op jit(solution)/shard_map/ppermute | solution.py:24
  6.6 24.6 %all-to-all-start = ((f32[4,16,8,128]{3,2,0,1:T(8,128)}), f32[4,16,8,128]{3,2,0,1:T(8,128)S(1)}, u32[]{:S(2)}, u32[]{:S(2)}) async-start(f32[4,16,8,128]{3,2,0,1:T(8,128)} %pad_maximum_fusion.19), calls=%async_computation | async-start | bytes 524288 | tf_op jit(solution)/shard_map/all_to_all | solution.py:116
  16.9 0.7 copy-start.27
  16.9 0.7 copy-start.28
  17.7 0.7 copy-start.31
  19.3 43.9 %copy-start.8 = (f32[4,16,128]{2,1,0:T(8,128)}, f32[4,16,128]{2,1,0:T(8,128)S(1)}, u32[]{:S(2)}) copy-start(f32[4,16,128]{2,1,0:T(8,128)S(1)} %get-tuple-element.76) | copy-start | bytes 98308
  19.3 0.7 copy-start.32
  20.1 0.8 copy-start.2
  20.8 69.7 %copy-start.10 = (f32[16,128]{1,0:T(8,128)}, f32[16,128]{1,0:T(8,128)S(1)}, u32[]{:S(2)}) copy-start(f32[16,128]{1,0:T(8,128)S(1)} %get-tuple-element.82) | copy-start | bytes 24580
  21.3 47.9 %copy-start.18 = (f32[4,4]{1,0:T(4,128)}, f32[4,4]{1,0:T(4,128)S(1)}, u32[]{:S(2)}) copy-start(f32[4,4]{1,0:T(4,128)S(1)} %pad_maximum_fusion.26) | copy-start | bytes 196
  21.3 0.7 copy-start.21
  21.4 3.2 %copy-start = (f32[12,16,8,128]{3,2,1,0:T(8,128)S(1)}, f32[12,16,8,128]{3,2,1,0:T(8,128)}, u32[]{:S(2)}) copy-start(f32[12,16,8,128]{3,2,1,0:T(8,128)} %param.20) | copy-start | bytes 2359300
  22.7 8.4 %collective-permute-start.1 = (f32[4,8,128]{2,1,0:T(8,128)S(1)}, f32[4,8,128]{2,1,0:T(8,128)S(1)}, u32[]{:S(2)}, u32[]{:S(2)}) collective-permute-start(f32[4,8,128]{2,1,0:T(8,128)S(1)} %bitcast.260), channel_id=1, source_target_pairs={{0,8},{8,16},{16,24},{24,32},{32,40},{40,48},{48,56},{56,64},{64,7... | collective-permute-start | bytes 49160 | tf_op jit(solution)/shard_map/ppermute | solution.py:24
  31.1 0.8 copy-start.4
  33.1 17.7 %all-to-all-start.1 = ((f32[4,2,64,128]{3,1,0,2:T(2,128)}), f32[4,2,64,128]{3,1,0,2:T(2,128)S(1)}, u32[]{:S(2)}, u32[]{:S(2)}) async-start(f32[4,2,64,128]{3,1,0,2:T(2,128)} %copy.485), calls=%async_computation.1 | async-start | bytes 524288 | tf_op jit(solution)/shard_map/all_to_all | solution.py:119
  50.9 0.7 copy-start.15
  51.5 0.7 copy-start.29
  52.2 1.0 copy-start.7
  53.4 6.6 %collective-permute-start.2 = (f32[4,1,8,128]{3,2,1,0:T(8,128)S(1)}, f32[4,1,8,128]{3,2,1,0:T(8,128)S(1)}, u32[]{:S(2)}, u32[]{:S(2)}) collective-permute-start(f32[4,1,8,128]{3,2,1,0:T(8,128)S(1)} %fusion.76), channel_id=1, source_target_pairs={{8,0},{16,8},{24,16},{32,24},{40,32},{48,40},{56,48},{64,56},{72,6... | collective-permute-start | bytes 49160 | tf_op jit(solution)/shard_map/ppermute | solution.py:24
  56.6 16.1 %all-to-all-start.2 = ((f32[4,16,8,128]{3,2,0,1:T(8,128)}), f32[4,16,8,128]{3,2,0,1:T(8,128)S(1)}, u32[]{:S(2)}, u32[]{:S(2)}) async-start(f32[4,16,8,128]{3,2,0,1:T(8,128)} %copy.494), calls=%async_computation.2 | async-start | bytes 524288 | tf_op jit(solution)/shard_map/all_to_all | solution.py:116
  60.7 8.4 %collective-permute-start.3 = (f32[4,8,128]{2,1,0:T(8,128)S(1)}, f32[4,8,128]{2,1,0:T(8,128)S(1)}, u32[]{:S(2)}, u32[]{:S(2)}) collective-permute-start(f32[4,8,128]{2,1,0:T(8,128)S(1)} %bitcast.258), channel_id=1, source_target_pairs={{0,8},{8,16},{16,24},{24,32},{32,40},{40,48},{48,56},{56,64},{64,7... | collective-permute-start | bytes 49160 | tf_op jit(solution)/shard_map/ppermute | solution.py:24
  74.0 15.7 %all-to-all-start.3 = ((f32[4,2,64,128]{3,1,0,2:T(2,128)}), f32[4,2,64,128]{3,1,0,2:T(2,128)S(1)}, u32[]{:S(2)}, u32[]{:S(2)}) async-start(f32[4,2,64,128]{3,1,0,2:T(2,128)} %copy.496), calls=%async_computation.3 | async-start | bytes 524288 | tf_op jit(solution)/shard_map/all_to_all | solution.py:119
  89.8 0.7 copy-start.16
  90.5 0.7 copy-start.13
  90.5 0.7 copy-start.25
  90.6 0.7 copy-start.11
  91.4 6.2 %collective-permute-start.4 = (f32[4,1,8,128]{3,2,1,0:T(8,128)S(1)}, f32[4,1,8,128]{3,2,1,0:T(8,128)S(1)}, u32[]{:S(2)}, u32[]{:S(2)}) collective-permute-start(f32[4,1,8,128]{3,2,1,0:T(8,128)S(1)} %pad_maximum_fusion.22), channel_id=1, source_target_pairs={{8,0},{16,8},{24,16},{32,24},{40,32},{48,40},{56,48},{64,56},{72,6... | collective-permute-start | bytes 49160 | tf_op jit(solution)/shard_map/ppermute | solution.py:24
  94.1 16.2 %all-to-all-start.4 = ((f32[4,16,8,128]{3,2,0,1:T(8,128)}), f32[4,16,8,128]{3,2,0,1:T(8,128)S(1)}, u32[]{:S(2)}, u32[]{:S(2)}) async-start(f32[4,16,8,128]{3,2,0,1:T(8,128)} %copy.505), calls=%async_computation.4 | async-start | bytes 524288 | tf_op jit(solution)/shard_map/all_to_all | solution.py:116
  97.6 0.7 copy-start.22
  99.0 8.4 %collective-permute-start.5 = (f32[4,8,128]{2,1,0:T(8,128)S(1)}, f32[4,8,128]{2,1,0:T(8,128)S(1)}, u32[]{:S(2)}, u32[]{:S(2)}) collective-permute-start(f32[4,8,128]{2,1,0:T(8,128)S(1)} %bitcast.259), channel_id=1, source_target_pairs={{0,8},{8,16},{16,24},{24,32},{32,40},{40,48},{48,56},{56,64},{64,7... | collective-permute-start | bytes 49160 | tf_op jit(solution)/shard_map/ppermute | solution.py:24
  107.4 2.9 %copy-start.5 = (f32[64,64,1,1]{1,0,3,2:T(8,128)S(1)}, f32[64,64,1,1]{1,0,3,2:T(8,128)}, u32[]{:S(2)}) copy-start(f32[64,64,1,1]{1,0,3,2:T(8,128)} %constant.67) | copy-start | bytes 49156
  111.5 5.2 %copy-start.19 = (f32[4,4]{1,0:T(4,128)S(1)}, f32[4,4]{1,0:T(4,128)}, u32[]{:S(2)}) copy-start(f32[4,4]{1,0:T(4,128)} %copy-done.18) | copy-start | bytes 196
  111.5 15.9 %all-to-all-start.5 = ((f32[4,2,64,128]{3,1,0,2:T(2,128)}), f32[4,2,64,128]{3,1,0,2:T(2,128)S(1)}, u32[]{:S(2)}, u32[]{:S(2)}) async-start(f32[4,2,64,128]{3,1,0,2:T(2,128)} %copy.507), calls=%async_computation.5 | async-start | bytes 524288 | tf_op jit(solution)/shard_map/all_to_all | solution.py:119
  127.4 0.7 copy-start.30
  129.1 7.1 %collective-permute-start.6 = (f32[4,1,8,128]{3,2,1,0:T(8,128)S(1)}, f32[4,1,8,128]{3,2,1,0:T(8,128)S(1)}, u32[]{:S(2)}, u32[]{:S(2)}) collective-permute-start(f32[4,1,8,128]{3,2,1,0:T(8,128)S(1)} %fusion.75), channel_id=1, source_target_pairs={{8,0},{16,8},{24,16},{32,24},{40,32},{48,40},{56,48},{64,56},{72,6... | collective-permute-start | bytes 49160 | tf_op jit(solution)/shard_map/ppermute | solution.py:24
  132.3 15.6 %all-to-all-start.6 = ((f32[4,16,8,128]{3,2,0,1:T(8,128)}), f32[4,16,8,128]{3,2,0,1:T(8,128)S(1)}, u32[]{:S(2)}, u32[]{:S(2)}) async-start(f32[4,16,8,128]{3,2,0,1:T(8,128)} %copy.519), calls=%async_computation.6 | async-start | bytes 524288 | tf_op jit(solution)/shard_map/all_to_all | solution.py:116
  136.2 0.7 copy-start.23
  137.5 2.7 %copy-start.9 = (f32[4,16,128]{2,1,0:T(8,128)S(1)}, f32[4,16,128]{2,1,0:T(8,128)}, u32[]{:S(2)}) copy-start(f32[4,16,128]{2,1,0:T(8,128)} %copy-done.8) | copy-start | bytes 98308
  137.5 8.4 %collective-permute-start.7 = (f32[4,8,128]{2,1,0:T(8,128)S(1)}, f32[4,8,128]{2,1,0:T(8,128)S(1)}, u32[]{:S(2)}, u32[]{:S(2)}) collective-permute-start(f32[4,8,128]{2,1,0:T(8,128)S(1)} %bitcast.257), channel_id=1, source_target_pairs={{0,8},{8,16},{16,24},{24,32},{32,40},{40,48},{48,56},{56,64},{64,7... | collective-permute-start | bytes 49160 | tf_op jit(solution)/shard_map/ppermute | solution.py:24
  139.5 1.0 copy-start.3
  145.9 2.0 %copy-start.6 = (f32[64,64,1,1]{1,0,3,2:T(8,128)S(1)}, f32[64,64,1,1]{1,0,3,2:T(8,128)}, u32[]{:S(2)}) copy-start(f32[64,64,1,1]{1,0,3,2:T(8,128)} %constant.67) | copy-start | bytes 49156
  149.2 6.0 %copy-start.20 = (f32[4,4]{1,0:T(4,128)S(1)}, f32[4,4]{1,0:T(4,128)}, u32[]{:S(2)}) copy-start(f32[4,4]{1,0:T(4,128)} %copy-done.18) | copy-start | bytes 196
  149.2 16.5 %all-to-all-start.7 = ((f32[4,2,64,128]{3,1,0,2:T(2,128)}), f32[4,2,64,128]{3,1,0,2:T(2,128)S(1)}, u32[]{:S(2)}, u32[]{:S(2)}) async-start(f32[4,2,64,128]{3,1,0,2:T(2,128)} %copy.521), calls=%async_computation.7 | async-start | bytes 524288 | tf_op jit(solution)/shard_map/all_to_all | solution.py:119
  166.4 0.7 copy-start.12
  167.3 0.7 copy-start.14
  167.3 0.7 copy-start.24
  168.0 0.8 copy-start.26
  (1 other events, 0.7 us)
where the time goes:
time: 171 us; the launch traced here: 169 us
  waiting for transfers between devices  72.3 us (42%)
  starting transfers between devices  61.6 us (36%)
  local copies, waits for them, and re-layouts  20.4 us (12%)
  other arithmetic  6.49 us (4%)
  matrix products  5.58 us (3%)
  between operations  2.44 us (1%)
    all_to_all x4, waiting for transfers between devices, azimuth_derivative(): lax.all_to_all(local_deriv, 'az', split_axis=2, concat_axis=1, tiled=True)  42.8 us
    all_to_all x4, starting transfers between devices, azimuth_derivative(): lax.all_to_all(local_deriv, 'az', split_axis=2, concat_axis=1, tiled=True)  22.1 us
    ppermute x8, waiting for transfers between devices, from_behind(): lax.ppermute(value, axis, [(source, source + steps) for source in range(f...  21.6 us
    all_to_all x4, starting transfers between devices, azimuth_derivative(): lax.all_to_all(fields, 'az', split_axis=1, concat_axis=2, tiled=True)  20.6 us
    ppermute x8, starting transfers between devices, from_behind(): lax.ppermute(value, axis, [(source, source + steps) for source in range(f...  18.9 us
    unnamed x66, local copies, waits for them, and re-layouts  11.2 us
    all_to_all x4, waiting for transfers between devices, azimuth_derivative(): lax.all_to_all(fields, 'az', split_axis=1, concat_axis=2, tiled=True)  7.99 us
    transpose x4, local copies, waits for them, and re-layouts, azimuth_derivative(): jnp.einsum('ts,czsr->cztr', azimuth_matrix, lax.all_to_all(fields, 'az',...  3.63 us
  transfers between devices with their start and end apart: 16, of which 11 were waited for; matrix products, arithmetic and copies ran while one was open for 8% of the time, Pallas kernels for 0%

commit v1 on v0

v1 whole, which is shorter than its diff:
```python
import functools
import math

import jax
import jax.numpy as jnp
import ml_dtypes
import numpy as np
from jax import lax
from jax.experimental import pallas as pl
from jax.experimental.pallas import tpu as pltpu
from jax.sharding import PartitionSpec as P

NR = 128
NT = 64
RB = 4
PLANES = 16
AZ = 8
GROUP = 16
DT = 0.02
SOURCE = DT * 40.0
R_INNER = 1.0
F32 = jnp.float32
BF16 = jnp.bfloat16
FIELDS_IN = 19
FIELDS_OUT = 14


def gll_basis():
    root_value = math.sqrt(3.0 / 7.0)
    nodes = np.array([-1.0, -root_value, 0.0, root_value, 1.0])
    weights = np.array([0.1, 49.0 / 90.0, 32.0 / 45.0, 49.0 / 90.0, 0.1])
    offsets = nodes[:, None] - nodes[None, :] + np.eye(5)
    factors = np.prod(offsets, axis=1)
    derivative = factors[:, None] / factors[None, :] / offsets
    diagonal = np.sum(1.0 / offsets, axis=1) - 1.0
    derivative = derivative * (1.0 - np.eye(5)) + np.eye(5) * diagonal[:, None]
    return nodes, weights, derivative


NODES, WEIGHTS, DERIV = gll_basis()
ROW = DERIV * np.array([1.0, 2.0, 2.0, 2.0, 1.0])[:, None]


def line_operator(count, first):
    matrix = np.zeros((count + 1, count + 1))
    for e in range(count // 4):
        matrix[4 * e : 4 * e + 5, 4 * e : 4 * e + 5] += ROW
    if first:
        matrix[0] *= 2.0
    else:
        matrix[0, 0] += ROW[4, 4]
    return matrix[:count, :count]


def halves(matrix):
    hi = matrix.astype(np.float32).astype(ml_dtypes.bfloat16)
    lo = (matrix - hi.astype(np.float64)).astype(np.float32).astype(ml_dtypes.bfloat16)
    return np.stack([hi, lo])


def azimuth_operator():
    positions = np.arange(NT)
    offsets = positions[:, None] - positions[None, :]
    modes = np.arange(1, NT // 2)
    phases = 2.0 * np.pi * offsets[:, :, None] * modes / NT
    return -(2.0 / NT) * np.sum(modes * np.sin(phases), axis=2)


def inverse_radius():
    positions = np.arange(NR)
    return 1.0 / (R_INNER + positions // 4 + 0.5 * (1.0 + NODES[positions % 4]))


@functools.lru_cache(None)
def constants():
    groups = NR // GROUP
    c = {}
    c["dr"] = halves(line_operator(NR, True).T)
    items = np.zeros((8, NR, groups, 16))
    for s in range(8):
        for k in range(groups):
            if GROUP * (k + 1) < NR:
                items[s, GROUP * (k + 1), k, 2 * s] = 1.0
            if k:
                items[s, GROUP * k - 4 : GROUP * k, k, 2 * s + 1] = ROW[4, :4]
    c["items"] = halves(items.reshape(8 * NR, 128))
    c["dt"] = halves(azimuth_operator())
    c["mr"] = np.stack([halves(np.kron(np.eye(8), line_operator(16, first).T)) for first in (False, True)])
    c["mz"] = np.stack([halves(np.kron(line_operator(16, first).T, np.eye(16))) for first in (False, True)])
    spread = np.zeros((2, 16))
    spread[0, 12:] = ROW[:4, 4]
    spread[1, 0] = 1.0
    wr = np.zeros((2, 8, 16, 4, 8, 16))
    wz = np.zeros((8, 16, 4, 16, 16))
    for f in range(4):
        for side in range(2):
            for j in range(8):
                for order in range(2):
                    wr[order, j, 8 * order + 2 * f + side, f, j] = spread[side]
            for r in range(16):
                wz[2 * f + side, r, f, :, r] = spread[side]
    c["wr"] = np.stack([halves(w) for w in wr.reshape(2, 128, 512)])
    c["wz"] = halves(wz.reshape(128, 1024))
    q = inverse_radius().astype(np.float32)
    c["q"] = np.broadcast_to(q, (8, NR)).copy()
    c["qg"] = np.broadcast_to(
        np.tile(q.reshape(groups, 1, GROUP), (1, PLANES, 1)).reshape(groups, 1, 256), (groups, 8, 256)
    ).copy()
    return c


def roll(x, shift):
    return pltpu.roll(x, shift % x.shape[-1], x.ndim - 1)


def dot(a, b):
    return jnp.dot(a, b, preferred_element_type=F32)


def parts(x):
    hi = x.astype(BF16)
    return hi, (x - hi.astype(F32)).astype(BF16)


def mm(x, hi, lo):
    xh, xl = parts(x)
    return dot(xh, hi) + dot(xl, hi) + dot(xh, lo)


def coefficients(ids, tab):
    hits = [ids == float(m) for m in range(8)]

    def pick(column):
        value = jnp.where(hits[0], tab[0, column], 0.0)
        for m in range(1, 8):
            value = jnp.where(hits[m], tab[m, column], value)
        return value

    lame, mu, modulus, beta, rho, rho_f, tort, fric = [pick(c) for c in range(8)]
    omega = pick(8)
    weights = [pick(9 + l) for l in range(4)]
    rates = [pick(13 + l) for l in range(4)]
    rho_w = tort * rho_f
    scale = DT / (rho * rho_w - rho_f * rho_f)
    decay = [1.0 / (1.0 + DT * (rate + omega)) for rate in rates]
    gain = sum(a * c for a, c in zip(weights, decay))
    return dict(
        cv=rho_w * scale,
        cf=rho_f * scale,
        cr=rho * scale,
        fric=fric,
        omega=DT * omega,
        weights=weights,
        decay=decay,
        kappa=(1.0 + DT * omega) * gain,
        bulk=DT * (lame + beta * beta * modulus),
        couple=DT * beta * modulus,
        modulus=DT * modulus,
        shear=DT * mu,
    )


def spread_rows(value, first, count, tail=False):
    rows = [jnp.broadcast_to(value[first + e : first + e + 1, :], (8, NR)) for e in range(count + tail)]
    planes = [rows[i // 4] for i in range(4 * count + tail)]
    return jnp.stack(planes)


def combine(row, nodes):
    total = None
    for weight, node in zip(row, nodes):
        term = float(weight) * node
        total = term if total is None else total + term
    return total


def depth_derivative(x, lo, hi, edge, has_below, low=None, high=None):
    count = (x.shape[0] - 1) // 4
    blocks = x[: 4 * count].reshape((count, 4) + x.shape[1:])
    last = [blocks[e + 1, 0] if e + 1 < count else x[4 * count] for e in range(count)]

    def nodes(e):
        return [blocks[e, l] for l in range(4)] + [last[e]]

    out = []
    for e in range(lo, hi + 1):
        upper = combine(ROW[0], nodes(e)) if e < count else high
        lower = combine(ROW[4], nodes(e - 1)) if e > 0 else low
        if e == edge:
            upper = (2.0 - has_below) * upper
            lower = has_below * lower
        out.append(upper + lower)
        if e < hi:
            for i in range(1, 4):
                out.append(combine(ROW[i], nodes(e)))
    return jnp.stack(out)


def below_partial(x):
    return combine(ROW[4, :4], [x[l] for l in range(4)])


def lane_groups():
    return lax.broadcasted_iota(jnp.int32, (8, NR), 1) // GROUP


def exchange_groups(x):
    groups = lane_groups()
    rows = [x[j] for j in range(8)]
    for s in (4, 2, 1):
        low = (groups & s) == 0
        for j in range(8):
            if not j & s:
                a, b = rows[j], rows[j + s]
                rows[j] = jnp.where(low, a, roll(b, GROUP * s))
                rows[j + s] = jnp.where(low, roll(a, -GROUP * s), b)
    return rows


def flat(x):
    return x.reshape(-1, NR)


def prepare(v, s, psi, ids, tab, vw, t_out, up, dn):
    c = coefficients(ids[...], tab)

    def sp(value):
        return spread_rows(value, 2, 4)

    weights = [sp(w) for w in c["weights"]]
    cf = sp(c["cf"] * c["fric"])
    cr = sp(c["cr"] * c["fric"])
    decayed = [sp(w * d) for w, d in zip(c["weights"], c["decay"])]
    for i in range(3):
        memory = [psi[3 * l + i] for l in range(4)]
        total = sum(w * m for w, m in zip(weights, memory))
        t_out[i] = sum(w * (m - v[3 + i]) for w, m in zip(decayed, memory))
        vi = v[i] + cf * total
        wi = v[3 + i] - cr * total
        for f, x in ((i, vi), (3 + i, wi)):
            vw[f] = x
            up[56 + 8 * f : 64 + 8 * f] = x[8:]
            dn[35 + 5 * f : 40 + 5 * f] = x[:5]
    for f in range(7):
        up[8 * f : 8 * f + 8] = s[f, 8:]
        dn[5 * f : 5 * f + 5] = s[f, :5]
    for i, f in enumerate((4, 5, 2, 6)):
        nodes = [s[f, 4 + l] for l in range(5)]
        up[104 + i] = combine(ROW[4], nodes)
        dn[65 + i] = combine(ROW[0], nodes)
    own = ids[...]
    rows = lax.broadcasted_iota(jnp.int32, (8, NR), 0)
    up[108] = jnp.where(rows < 2, pltpu.roll(own, 4, 0), 0.0)
    dn[69] = jnp.where(rows >= 6, pltpu.roll(own, 4, 0), 0.0)


def launch(s, vw, t_in, up, dn, ids, tab, info, dr_m, items, q_ref, pk, keep):
    has_below = info[1].astype(F32)
    has_above = info[2].astype(F32)
    own = ids[...]
    rows = lax.broadcasted_iota(jnp.int32, (8, NR), 0)
    own = jnp.where((rows >= 2) & (rows < 6), own, 0.0)
    c = coefficients(own + up[108] + dn[69], tab)
    q = q_ref[...]

    def radial(fields):
        stacked = jnp.concatenate([flat(x) for x in fields], axis=0)
        out = mm(stacked, dr_m[0], dr_m[1])
        count = fields[0].shape[0]
        return [out[8 * count * i : 8 * count * (i + 1)].reshape(count, 8, NR) for i in range(len(fields))]

    def ext(f):
        return jnp.concatenate([up[8 * f : 8 * f + 8], s[f], dn[5 * f : 5 * f + 5]], axis=0)

    def ext_v(f):
        return jnp.concatenate(
            [up[56 + 8 * f : 64 + 8 * f], vw[f], dn[35 + 5 * f : 40 + 5 * f]], axis=0
        )

    above29 = lax.broadcasted_iota(jnp.int32, (29, 8, NR), 0) < 24
    mask29 = jnp.where(above29, 1.0, has_above)
    rr, tt, zz, rt, rz, tz, p = [ext(f) for f in range(7)]
    cv, cf, cr = [spread_rows(c[n], 0, 7, True) for n in ("cv", "cf", "cr")]
    r_rr, r_rt, r_rz, r_p = radial([rr, rt, rz, p])
    z_rz, z_tz, z_zz, z_p = [
        depth_derivative(x, 0, 7, 2, has_below, up[104 + i], dn[65 + i]) for i, x in enumerate((rz, tz, zz, p))
    ]
    d_r = r_rr + z_rz + q * (rr - tt)
    d_t = r_rt + z_tz + 2.0 * q * rt
    d_z = r_rz + z_zz + q * rz
    v1 = [
        mask29 * (ext_v(0) + cv * d_r + cf * r_p),
        mask29 * (ext_v(1) + cv * d_t),
        mask29 * (ext_v(2) + cv * d_z + cf * z_p),
    ]
    w1 = [
        mask29 * (ext_v(3) - cf * d_r - cr * r_p),
        mask29 * (ext_v(4) - cf * d_t),
        mask29 * (ext_v(5) - cf * d_z - cr * z_p),
    ]
    q_rt, q_tt, q_tz, q_p = q * rt, q * tt, q * tz, q * p
    u = [cv * q_rt, cv * q_tt + cf * q_p, cv * q_tz]
    uw = [-(cf * q_rt), -(cf * q_tt + cr * q_p), -(cf * q_tz)]

    def pack(f, planes):
        for g in range(2):
            chunks = exchange_groups(planes[8 * g : 8 * g + 8])
            for k in range(8):
                pk[k, 2 * f + g] = chunks[k]

    for f, x in enumerate((3, 1, 5, 6)):
        pack(f, s[x])
    fric = spread_rows(c["fric"], 2, 4)
    kappa = spread_rows(c["kappa"], 2, 4)
    grads = (r_p, None, z_p)
    for i, d in enumerate((d_r, d_t, d_z)):
        g = fric * (t_in[i] + kappa * w1[i][8:24])
        if grads[i] is not None:
            g = g + grads[i][8:24]
        a = cv[8:24] * d[8:24] + cf[8:24] * g
        b = cf[8:24] * d[8:24] + cr[8:24] * g
        pack(4 + i, v1[i][8:24])
        pack(7 + i, w1[i][8:24])
        pack(10 + i, a)
        keep[i] = v1[i][8:24]
        keep[3 + i] = w1[i][8:24]
        keep[6 + i] = a
        keep[9 + i] = b
        if i == 1:
            pack(13, b)

    bulk, couple, modulus, shear = [
        spread_rows(c[n], 1, 6)[:21] for n in ("bulk", "couple", "modulus", "shear")
    ]
    mask21 = jnp.where(lax.broadcasted_iota(jnp.int32, (21, 8, NR), 0) < 20, 1.0, has_above)
    plane21 = lax.broadcasted_iota(jnp.int32, (21, 8, NR), 0) - 4
    lane21 = lax.broadcasted_iota(jnp.int32, (21, 8, NR), 2)
    source = jnp.where((plane21 == info[0]) & (lane21 < 4 * RB), SOURCE, 0.0)

    def stresses(v, w, extra):
        inner = slice(4, 25)
        vr, vt, wr = v[0][inner], v[1][inner], w[0][inner]
        r_r, r_t, r_z, r_w = radial([vr, vt, v[2][inner], wr])
        z_r, z_t, z_z, z_w = [depth_derivative(x, 1, 6, 2, has_below) for x in (v[0], v[1], v[2], w[2])]
        e_tt, g_rt, g_tz, div_w = q * vr, r_t - q * vt, z_t, r_w + q * wr + z_w
        if extra is not None:
            e_tt, g_rt, g_tz, div_w = e_tt + extra[1], g_rt + extra[0], g_tz + extra[2], div_w + extra[3]
        div_v = r_r + e_tt + z_z
        total = bulk * div_v + couple * div_w
        return dict(
            rr=mask21 * (total + 2.0 * shear * r_r),
            zz=mask21 * (total + 2.0 * shear * z_z),
            rt=mask21 * (shear * g_rt),
            rz=mask21 * (shear * (z_r + r_z)),
            tz=mask21 * (shear * g_tz),
            p=mask21 * (-(couple * div_v + modulus * div_w) + (source if extra is None else 0.0)),
        )

    x0 = stresses(v1, w1, None)
    inner = slice(4, 25)
    x1 = stresses(u, uw, [q * v1[0][inner], q * v1[1][inner], q * v1[2][inner], q * w1[1][inner]])
    e2, dw2 = q * u[1][inner], q * uw[1][inner]
    total2 = bulk * e2 + couple * dw2
    x2 = dict(
        rr=mask21 * total2,
        zz=mask21 * total2,
        rt=mask21 * (shear * (q * u[0][inner])),
        tz=mask21 * (shear * (q * u[2][inner])),
        p=mask21 * (-(couple * e2 + modulus * dw2)),
    )

    def radius_items(fields):
        stacked = jnp.concatenate([flat(x) for x in fields], axis=1)
        return mm(stacked, items[0], items[1]).reshape(-1, 8, NR)

    def depth_items(fields, first):
        out = []
        for x in fields:
            out.append(x[first + 20])
            out.append(has_below * below_partial(x[first : first + 4]))
        return jnp.stack(out)

    velocity_r = [v1[0], v1[1], v1[2], w1[0], u[0], u[1], u[2], uw[0]]
    pack(14, radius_items([x[8:24] for x in velocity_r]))
    names_r = ("rr", "rt", "rz", "p")
    pack(15, radius_items([x[n][4:20] for x in (x0, x1) for n in names_r]))
    pack(16, depth_items([v1[0], v1[1], v1[2], w1[2], u[0], u[1], u[2], uw[2]], 4))
    names_z = ("rz", "tz", "zz", "p")
    pack(17, depth_items([x[n] for x in (x0, x1) for n in names_z], 0))
    zero8 = jnp.zeros((8, 8, NR), F32)
    second = [x2[n][4 + 8 * h : 12 + 8 * h] if n in x2 else zero8 for h in range(2) for n in names_r]
    zero21 = jnp.zeros((21, 8, NR), F32)
    pack(
        18,
        jnp.concatenate(
            [radius_items(second), depth_items([x2[n] if n in x2 else zero21 for n in names_z], 0)], axis=0
        ),
    )


def ring(recv, ids, tab, info, dt_m, mr, mz, wr, wz, qg, out):
    c = coefficients(ids[...], tab)
    group = info[3]
    q = qg[group]
    sel_r = info[4]
    sel_z = info[5]

    def field(f):
        return jnp.concatenate([recv[:, 2 * f], recv[:, 2 * f + 1]], axis=-1)

    def az(fields):
        x = jnp.concatenate([y.reshape(NT, -1) for y in fields], axis=1)
        xh, xl = parts(x)
        y = dot(dt_m[0], xh) + dot(dt_m[0], xl) + dot(dt_m[1], xh)
        res, at = [], 0
        for f in fields:
            n = f.shape[-1]
            res.append(y[:, at : at + n].reshape(f.shape))
            at += n
        return res

    def by_half(x):
        x = x.reshape(NT, 256)
        return [x[:, :128], x[:, 128:]]

    mr_h, mr_l = mr[sel_r, 0], mr[sel_r, 1]
    mz_h, mz_l = mz[sel_z, 0], mz[sel_z, 1]

    def radial(fields, halo):
        stacked = jnp.concatenate([h for f in fields for h in by_half(f)], axis=0)
        y = mm(stacked, mr_h, mr_l)
        res = []
        for i in range(len(fields)):
            halves_ = [
                y[128 * i + 64 * g : 128 * i + 64 * g + 64] + halo[64 * g : 64 * g + 64, 128 * i : 128 * i + 128]
                for g in range(2)
            ]
            res.append(jnp.concatenate(halves_, axis=1).reshape(8, 8, 256))
        return res

    def depth(fields, halo):
        stacked = jnp.concatenate([f.reshape(NT, 256) for f in fields], axis=0)
        y = mm(stacked, mz_h, mz_l)
        return [
            (y[64 * i : 64 * i + 64] + halo[:, 256 * i : 256 * i + 256]).reshape(8, 8, 256)
            for i in range(len(fields))
        ]

    rt, tt, tz, p = [field(f) for f in range(4)]
    pr2, pr3 = field(14), field(15)
    pd2 = [recv[:, 32], recv[:, 33]]
    pd3 = [recv[:, 34], recv[:, 35]]
    px = field(18)
    s_rt, s_tt, s_tz, s_p, d_pr2, d_pr3, d_pd2, d_pd3, d_px = az([rt, tt, tz, p, pr2, pr3, pd2[1], pd3[1], px])
    (dd_px,) = az([d_px])
    wr0, wr1 = (wr[0, 0], wr[0, 1]), (wr[1, 0], wr[1, 1])

    def stack_halves(x):
        return jnp.concatenate(by_half(x), axis=0)

    def radius_halo(zero, one):
        return mm(stack_halves(zero), *wr0) + mm(stack_halves(one), *wr1)

    hr2 = radius_halo(pr2, d_pr2)
    hz2 = mm((pd2[0] + d_pd2).reshape(NT, 128), wz[0], wz[1])
    half = dd_px.reshape(NT, 256)[:, :128]
    hr3 = radius_halo(pr3, d_pr3) + jnp.concatenate([mm(half, *wr0), mm(half, *wr1)], axis=0)
    hz3 = mm((pd3[0] + d_pd3).reshape(NT, 128) + dd_px.reshape(NT, 256)[:, 128:], wz[0], wz[1])

    cv, cf, cr = c["cv"], c["cf"], c["cr"]
    q_rt, q_tt, q_tz, q_p = q * s_rt, q * s_tt, q * s_tz, q * s_p
    dw = [-(cf * q_rt), -(cf * q_tt + cr * q_p), -(cf * q_tz)]
    v1 = [
        field(4) + cv * q_rt,
        field(5) + cv * q_tt + cf * q_p,
        field(6) + cv * q_tz,
    ]
    w1 = [field(7 + i) + dw[i] for i in range(3)]
    r_r, r_t, r_z, r_w = radial([v1[0], v1[1], v1[2], w1[0]], hr2)
    z_r, z_t, z_z, z_w = depth([v1[0], v1[1], v1[2], w1[2]], hz2)
    a_r, a_t, a_z, a_w = az([v1[0], v1[1], v1[2], w1[1]])
    e_tt = q * (v1[0] + a_t)
    div_v = r_r + e_tt + z_z
    div_w = r_w + q * (w1[0] + a_w) + z_w
    total = c["bulk"] * div_v + c["couple"] * div_w
    shear = c["shear"]
    lanes = lax.broadcasted_iota(jnp.int32, (8, 256), 1) // GROUP
    source = jnp.where((lanes == info[0]) & (group == 0), SOURCE, 0.0)
    n_rr = total + 2.0 * shear * r_r
    n_tt = total + 2.0 * shear * e_tt
    n_zz = total + 2.0 * shear * z_z
    n_rt = shear * (q * (a_r - v1[1]) + r_t)
    n_rz = shear * (z_r + r_z)
    n_tz = shear * (z_t + q * a_z)
    n_p = source - (c["couple"] * div_v + c["modulus"] * div_w)

    r_rr, r_rt, r_rz, r_p = radial([n_rr, n_rt, n_rz, n_p], hr3)
    z_rz, z_tz, z_zz, z_p = depth([n_rz, n_tz, n_zz, n_p], hz3)
    a_rt, a_tt, a_tz, a_p = az([n_rt, n_tt, n_tz, n_p])
    d_r = q_rt + r_rr + z_rz + q * (a_rt + n_rr - n_tt)
    d_t = q_tt + r_rt + z_tz + q * (a_tt + 2.0 * n_rt)
    d_z = q_tz + r_rz + z_zz + q * (a_tz + n_rz)
    fk = c["fric"] * c["kappa"]
    g_r = r_p + fk * dw[0]
    g_t = q_p + q * a_p + fk * dw[1]
    g_z = z_p + fk * dw[2]
    sums = [
        2.0 * v1[0] + field(10) + cv * d_r + cf * g_r,
        2.0 * v1[1] + field(11) + cv * d_t + cf * g_t,
        2.0 * v1[2] + field(12) + cv * d_z + cf * g_z,
        2.0 * w1[1] - field(13) - cf * d_t - cr * g_t,
    ]
    results = [s_rt, s_tt, s_tz, s_p, d_r, d_t, d_z, g_r, g_t, g_z] + az(sums)
    for f, x in enumerate(results):
        out[:, 2 * f] = x[:, :, :128]
        out[:, 2 * f + 1] = x[:, :, 128:]


def finish(recv, keep, v, s, psi, ids, tab, info, dr_m, q_ref, v_out, s_out, m_out, up, dn):
    has_below = info[1].astype(F32)
    c = coefficients(ids[...], tab)
    q = q_ref[...]

    def sp(value):
        return spread_rows(value, 2, 4)

    def unpack(f):
        planes = []
        for g in range(2):
            planes += exchange_groups([recv[k, 2 * f + g] for k in range(8)])
        return jnp.stack(planes)

    cv, cf, cr = sp(c["cv"]), sp(c["cf"]), sp(c["cr"])
    q_rt, q_tt, q_tz, q_p = [q * unpack(f) for f in range(4)]
    dv = [cv * q_rt, cv * q_tt + cf * q_p, cv * q_tz]
    dw = [-(cf * q_rt), -(cf * q_tt + cr * q_p), -(cf * q_tz)]
    sums_v, sums_w = [], []
    omega = sp(c["omega"])
    decay = [sp(d) for d in c["decay"]]
    for i in range(3):
        d, g = unpack(4 + i), unpack(7 + i)
        v1 = keep[i] + dv[i]
        w1 = keep[3 + i] + dw[i]
        v2 = v1 + keep[6 + i] + cv * d + cf * g
        w2 = w1 - keep[9 + i] - cf * d - cr * g
        v_out[i] = v2
        v_out[3 + i] = w2
        sums_v.append(v1 + v2)
        sums_w.append(w1 + w2)
        first = w1 - v[3 + i] + omega * w1
        second = w2 - w1 + omega * w2
        for l in range(4):
            m_out[3 * l + i] = decay[l] * (decay[l] * (psi[3 * l + i] + first) + second)
    halo = [sums_v[0], sums_v[1], sums_v[2], sums_w[2]]
    for i, x in enumerate(halo):
        up[i] = below_partial(x[12:])
        dn[i] = x[0]
    zero = jnp.zeros((1, 8, NR), F32)
    z_r, z_t, z_z, z_w = [
        depth_derivative(jnp.concatenate([x, zero], axis=0), 0, 4, 0, has_below, float(ROW[4, 4]) * x[0], zero[0])[:16]
        for x in halo
    ]
    stacked = jnp.concatenate([flat(x) for x in (sums_v[0], sums_v[1], sums_v[2], sums_w[0])], axis=0)
    y = mm(stacked, dr_m[0], dr_m[1])
    r_r, r_t, r_z, r_w = [y[128 * i : 128 * i + 128].reshape(16, 8, NR) for i in range(4)]
    a_r, a_t, a_z, a_w = [unpack(10 + i) for i in range(4)]
    e_tt = q * (sums_v[0] + a_t)
    div_v = r_r + e_tt + z_z
    div_w = r_w + q * (sums_w[0] + a_w) + z_w
    couple, shear = sp(c["couple"]), sp(c["shear"])
    total = sp(c["bulk"]) * div_v + couple * div_w
    plane = lax.broadcasted_iota(jnp.int32, (16, 8, NR), 0)
    lane = lax.broadcasted_iota(jnp.int32, (16, 8, NR), 2)
    source = jnp.where((plane == info[0]) & (lane < 4 * RB), SOURCE * (1.0 + math.cos(0.9)), 0.0)
    s_out[0] = s[0] + total + 2.0 * shear * r_r
    s_out[1] = s[1] + total + 2.0 * shear * e_tt
    s_out[2] = s[2] + total + 2.0 * shear * z_z
    s_out[3] = s[3] + shear * (q * (a_r - sums_v[1]) + r_t)
    s_out[4] = s[4] + shear * (z_r + r_z)
    s_out[5] = s[5] + shear * (z_t + q * a_z)
    s_out[6] = s[6] + source - (couple * div_v + sp(c["modulus"]) * div_w)


def close(s, up, dn, ids, tab, info, s_out):
    has_below = info[1].astype(F32)
    c = coefficients(ids[...], tab)

    def update(plane, row, z_r, z_t, z_z, z_w):
        def at(name):
            return jnp.broadcast_to(c[name][row : row + 1, :], (8, NR))

        bulk, couple, modulus, shear = at("bulk"), at("couple"), at("modulus"), at("shear")
        total = bulk * z_z + couple * z_w
        s_out[0, plane] = s[0, plane] + total
        s_out[1, plane] = s[1, plane] + total
        s_out[2, plane] = s[2, plane] + total + 2.0 * shear * z_z
        s_out[3, plane] = s[3, plane]
        s_out[4, plane] = s[4, plane] + shear * z_r
        s_out[5, plane] = s[5, plane] + shear * z_t
        s_out[6, plane] = s[6, plane] - (couple * z_z + modulus * z_w)

    update(0, 2, *[has_below * up[i] for i in range(4)])
    for plane in range(12, 16):
        weight = float(ROW[plane - 12, 4])
        update(plane, 5, *[weight * dn[i] for i in range(4)])
    for f in range(7):
        s_out[f, 1:12] = s[f, 1:12]


def call(body, inputs, shapes, smem=(), cost=None):
    specs = [
        pl.BlockSpec(memory_space=pltpu.SMEM if i in smem else pltpu.VMEM) for i in range(len(inputs))
    ]
    out = pl.pallas_call(
        body,
        out_shape=[jax.ShapeDtypeStruct(x, F32) for x in shapes],
        in_specs=specs,
        out_specs=[pl.BlockSpec(memory_space=pltpu.VMEM) for _ in shapes],
        compiler_params=pltpu.CompilerParams(vmem_limit_bytes=48 * 2**20),
        cost_estimate=pl.CostEstimate(flops=cost or 10**7, bytes_accessed=10**7, transcendentals=0),
        name=body.__name__,
    )(*inputs)
    return out


def shift(value, steps):
    count = lax.axis_size("depth")
    first, last = max(0, -steps), min(count, count - steps)
    return lax.ppermute(value, "depth", [(i, i + steps) for i in range(first, last)])


def on_device(velocity, stress, memory, layer_ids, materials, jkd, source_depth):
    c = constants()
    row = lax.axis_index("depth")
    group = lax.axis_index("az")
    tab = jnp.concatenate([materials, jkd], axis=1)
    first = (row == 0).astype(jnp.int32)
    last = (row == lax.axis_size("depth") - 1).astype(jnp.int32)
    info = jnp.stack(
        [
            source_depth[0] - PLANES * row,
            1 - first,
            1 - last,
            group,
            (group == 0).astype(jnp.int32),
            first,
        ]
    ).astype(jnp.int32)
    ids = jnp.repeat(layer_ids.astype(F32), 4, axis=1)
    ids_own = jnp.pad(ids, ((2, 2), (0, 0)))
    ids_group = lax.dynamic_slice_in_dim(ids, GROUP * group, GROUP, axis=1)
    ids_group = jnp.broadcast_to(jnp.repeat(ids_group, 4, axis=0).reshape(1, 256), (8, 256))
    block = (PLANES, AZ, NR)
    vw, t_part, up, dn = call(
        prepare,
        [velocity, stress, memory, ids_own, tab],
        [(6,) + block, (3,) + block, (109, AZ, NR), (70, AZ, NR)],
        smem=(4,),
    )
    up, dn = shift(up, 1), shift(dn, -1)
    packed, keep = call(
        launch,
        [stress, vw, t_part, up, dn, ids_own, tab, info, c["dr"], c["items"], c["q"]],
        [(8, 2 * FIELDS_IN, AZ, NR), (12,) + block],
        smem=(6, 7),
    )
    packed = lax.all_to_all(packed, "az", split_axis=0, concat_axis=0, tiled=True)
    (back,) = call(
        ring,
        [packed, ids_group, tab, info, c["dt"], c["mr"], c["mz"], c["wr"], c["wz"], c["qg"]],
        [(8, 2 * FIELDS_OUT, AZ, NR)],
        smem=(2, 3),
    )
    back = lax.all_to_all(back, "az", split_axis=0, concat_axis=0, tiled=True)
    v_out, s_part, m_out, up, dn = call(
        finish,
        [back, keep, velocity, stress, memory, ids_own, tab, info, c["dr"], c["q"]],
        [(6,) + block, (7,) + block, (12,) + block, (4, AZ, NR), (4, AZ, NR)],
        smem=(6, 7),
    )
    up, dn = shift(up, 1), shift(dn, -1)
    (s_out,) = call(close, [s_part, up, dn, ids_own, tab, info], [(7,) + block], smem=(4, 5))
    return v_out, s_out, m_out


def solution(mesh):
    field = P(None, "depth", "az", None)
    return jax.shard_map(
        on_device,
        mesh=mesh,
        in_specs=(field, field, field, P("depth", None), P(), P(), P()),
        out_specs=(field, field, field),
        check_vma=False,
    )
```

time: 171 us -> 122 us (0.71)
  the two profiles are of different devices: /device:TPU:32 before, /device:TPU:31 now
where the time goes in v1:
time: 122 us
  waiting for transfers between devices  40.5 us (33%)
  starting transfers between devices  27.5 us (23%)
  blocking collectives  25.9 us (21%)
  Pallas kernels  14.3 us (12%)
  local copies, waits for them, and re-layouts  10.4 us (9%)
  other arithmetic  1.5 us (1%)
  between operations  1.45 us (1%)
    all_to_all x1, blocking collectives, on_device(): back = lax.all_to_all(back, 'az', split_axis=0, concat_axis=0, tiled=True)  25.9 us
    all_to_all x1, waiting for transfers between devices, on_device(): lax.all_to_all(packed, 'az', split_axis=0, concat_axis=0, tiled=True)  25.5 us
    ppermute x4, starting transfers between devices, shift(): lax.ppermute(value, 'depth', [(i, i + steps) for i in range(first, last)])  17.4 us
    ppermute x4, waiting for transfers between devices, shift(): lax.ppermute(value, 'depth', [(i, i + steps) for i in range(first, last)])  15 us
    pallas_call x5, Pallas kernels, call(): pl.pallas_call(body, out_shape=[jax.ShapeDtypeStruct(x, F32) for x in sha...  14.3 us
    all_to_all x1, starting transfers between devices, on_device(): lax.all_to_all(packed, 'az', split_axis=0, concat_axis=0, tiled=True)  10.2 us
    unnamed x34, local copies, waits for them, and re-layouts  6.74 us
  transfers between devices with their start and end apart: 5, of which 3 were waited for; matrix products, arithmetic and copies ran while one was open for 2% of the time, Pallas kernels for 0%

profile of v1, /device:TPU:31, one launch (start us, length us, event | category | flops | bytes accessed | tf_op | source)
XLA Modules:
  0.0 121.7 jit_solution(3955162850015030383)
XLA Ops:
  0.6 0.0 copy-start.15
  0.6 0.0 copy-start.10
  0.7 0.7 convert_element_type.12
  1.4 0.1 broadcast_in_dim.13
  1.4 0.1 reshape.10
  1.6 0.0 copy-start.16
  1.6 0.8 pad_maximum_fusion.tab
  2.4 0.0 copy-done.16
  2.4 0.0 copy-start
  2.4 1.0 copy-done
  3.4 1.1 copy-done.2
  4.5 1.0 copy-done.4
  5.5 0.8 prepare.1
  6.4 4.9 %collective-permute-start = (f32[109,8,128]{2,1,0:T(8,128)S(1)}, f32[109,8,128]{2,1,0:T(8,128)S(1)}, u32[]{:S(2)}, u32[]{:S(2)}) collective-permute-start(f32[109,8,128]{2,1,0:T(8,128)S(1)} %get-tuple-element.16), channel_id=1, source_target_pairs={{0,8},{8,16},{16,24},{24,32},{32,40},{40,48},{48,56},{56,64},{64,7... | collective-permute-start | bytes 1339400 | tf_op jit(solution)/shard_map/ppermute | solution.py:629
  11.3 1.9 %collective-permute-start.1 = (f32[70,8,128]{2,1,0:T(8,128)S(1)}, f32[70,8,128]{2,1,0:T(8,128)S(1)}, u32[]{:S(2)}, u32[]{:S(2)}) collective-permute-start(f32[70,8,128]{2,1,0:T(8,128)S(1)} %get-tuple-element.17), channel_id=1, source_target_pairs={{8,0},{16,8},{24,16},{32,24},{40,32},{48,40},{56,48},{64,56},{72,6... | collective-permute-start | bytes 860168 | tf_op jit(solution)/shard_map/ppermute | solution.py:629
  13.8 0.1 stack.31.info
  13.9 8.6 %collective-permute-done.1.dn = f32[70,8,128]{2,1,0:T(8,128)S(1)} collective-permute-done((f32[70,8,128]{2,1,0:T(8,128)S(1)}, f32[70,8,128]{2,1,0:T(8,128)S(1)}, u32[]{:S(2)}, u32[]{:S(2)}) %collective-permute-start.1) | collective-permute-done | bytes 286752 | tf_op jit(solution)/shard_map/ppermute | solution.py:629
  22.5 0.0 collective-permute-done.up
  22.5 0.0 copy-done.15
  22.5 0.0 copy-done.10
  22.5 0.0 copy-done.1
  22.6 0.0 copy-done.9
  22.6 4.6 %launch.1 = (f32[8,38,8,128]{3,2,1,0:T(8,128)}, f32[12,16,8,128]{3,2,1,0:T(8,128)S(1)}) custom-call(f32[7,16,8,128]{3,2,1,0:T(8,128)S(1)} %copy-done.1, f32[6,16,8,128]{3,2,1,0:T(8,128)S(1)} %get-tuple-element.14.vw, f32[3,16,8,128]{3,2,1,0:T(8,128)S(1)} %get-tuple-element.15.t_in, f32[109,8,128]{2,1,0:T(8,128)S(1)} %collective-permute-done.up, ...), custom_call_target="tpu_custom_call" | custom-call | flops 10000000 | bytes 10000000 | tf_op jit(solution)/shard_map/launch/pallas_call | solution.py:614
  27.2 10.2 %all-to-all-start = ((f32[8,38,8,128]{3,2,1,0:T(8,128)}), f32[8,38,8,128]{3,2,1,0:T(8,128)S(1)}, u32[]{:S(2)}, u32[]{:S(2)}) async-start(f32[8,38,8,128]{3,2,1,0:T(8,128)} %get-tuple-element.18), calls=%async_computation | async-start | bytes 2490368 | tf_op jit(solution)/shard_map/all_to_all | solution.py:667
  37.3 0.8 constant_dynamic-slice_fusion
  38.1 0.6 broadcast_in_dim.14
  38.7 1.3 %broadcast_in_dim.15 = f32[256]{0:T(256)} reshape(f32[4,4,16]{2,1,0:T(4,128)} %broadcast_in_dim.14) | data formatting | bytes 2048 | tf_op jit(solution)/shard_map/broadcast_in_dim | solution.py:652
  40.0 25.5 %all-to-all-done.recv = f32[8,38,8,128]{3,2,1,0:T(8,128)S(1)} async-done(((f32[8,38,8,128]{3,2,1,0:T(8,128)}), f32[8,38,8,128]{3,2,1,0:T(8,128)S(1)}, u32[]{:S(2)}, u32[]{:S(2)}) %all-to-all-start) | async-done | bytes 1245216 | tf_op jit(solution)/shard_map/all_to_all | solution.py:667
  65.5 0.7 broadcast_in_dim.16.ids
  66.2 0.0 copy-done.6
  66.2 0.0 copy-done.7
  66.2 1.0 copy-done.8
  67.3 0.9 copy-done.12
  68.2 0.8 copy-done.13
  69.0 0.8 copy-done.14
  69.8 3.0 %ring.1 = f32[8,28,8,128]{3,2,1,0:T(8,128)S(1)} custom-call(f32[8,38,8,128]{3,2,1,0:T(8,128)S(1)} %all-to-all-done.recv, f32[8,256]{1,0:T(8,128)S(1)} %broadcast_in_dim.16.ids, f32[8,17]{1,0:T(8,128)S(1)} %pad_maximum_fusion.tab, s32[6]{0:T(128)S(1)} %stack.31.info, bf16[2,64,64]{2,1,0:T(8,128)(2,1)S(1)} %copy-done.14, ...), custom_call_target="tpu_custom_call" | custom-call | flops 10000000 | bytes 10000000 | tf_op jit(solution)/shard_map/ring/pallas_call | solution.py:614
  72.8 0.0 copy-start.3
  72.8 0.0 copy-start.5
  72.8 0.0 copy-start.11
  72.8 25.9 %all_to_all.10.recv = f32[8,28,8,128]{3,2,1,0:T(8,128)S(1)} all-to-all(f32[8,28,8,128]{3,2,1,0:T(8,128)S(1)} %ring.1), channel_id=1, replica_groups=mesh['depth'=64,'az'=8] {'az'}, dimensions={0} | all-to-all | bytes 1835008 | tf_op jit(solution)/shard_map/all_to_all | solution.py:674
  98.8 0.0 copy-done.3
  98.8 0.0 copy-done.5
  98.8 4.5 %finish.1 = (f32[6,16,8,128]{3,2,1,0:T(8,128)}, f32[7,16,8,128]{3,2,1,0:T(8,128)S(1)}, f32[12,16,8,128]{3,2,1,0:T(8,128)}, f32[4,8,128]{2,1,0:T(8,128)S(1)}, f32[4,8,128]{2,1,0:T(8,128)S(1)}) custom-call(f32[8,28,8,128]{3,2,1,0:T(8,128)S(1)} %all_to_all.10.recv, f32[12,16,8,128]{3,2,1,0:T(8,128)S(1)} %get-tuple-element.19.keep, ...), custom_call_target="tpu_custom_call" | custom-call | flops 10000000 | bytes 10000000 | tf_op jit(solution)/shard_map/finish/pallas_call | solution.py:614
  103.3 8.6 %collective-permute-start.2 = (f32[4,8,128]{2,1,0:T(8,128)S(1)}, f32[4,8,128]{2,1,0:T(8,128)S(1)}, u32[]{:S(2)}, u32[]{:S(2)}) collective-permute-start(f32[4,8,128]{2,1,0:T(8,128)S(1)} %get-tuple-element.22), channel_id=1, source_target_pairs={{0,8},{8,16},{16,24},{24,32},{32,40},{40,48},{48,56},{56,64},{64,7... | collective-permute-start | bytes 49160 | tf_op jit(solution)/shard_map/ppermute | solution.py:629
  111.9 1.9 %collective-permute-start.3 = (f32[4,8,128]{2,1,0:T(8,128)S(1)}, f32[4,8,128]{2,1,0:T(8,128)S(1)}, u32[]{:S(2)}, u32[]{:S(2)}) collective-permute-start(f32[4,8,128]{2,1,0:T(8,128)S(1)} %get-tuple-element.23), channel_id=1, source_target_pairs={{8,0},{16,8},{24,16},{32,24},{40,32},{48,40},{56,48},{64,56},{72,6... | collective-permute-start | bytes 49160 | tf_op jit(solution)/shard_map/ppermute | solution.py:629
  113.8 0.0 collective-permute-done.2.up
  113.9 6.4 %collective-permute-done.3.dn = f32[4,8,128]{2,1,0:T(8,128)S(1)} collective-permute-done((f32[4,8,128]{2,1,0:T(8,128)S(1)}, f32[4,8,128]{2,1,0:T(8,128)S(1)}, u32[]{:S(2)}, u32[]{:S(2)}) %collective-permute-start.3) | collective-permute-done | bytes 16416 | tf_op jit(solution)/shard_map/ppermute | solution.py:629
  120.3 1.4 %close.1 = f32[7,16,8,128]{3,2,1,0:T(8,128)} custom-call(f32[7,16,8,128]{3,2,1,0:T(8,128)S(1)} %get-tuple-element.21.s, f32[4,8,128]{2,1,0:T(8,128)S(1)} %collective-permute-done.2.up, f32[4,8,128]{2,1,0:T(8,128)S(1)} %collective-permute-done.3.dn, f32[8,128]{1,0:T(8,128)S(1)} %pad.4.ids, f32[8,17]{1,0:T(8,128)S(1)} %pad_maximum_fusion.tab, s32[6]{0:T(128)S(1)} %stack.31.info), custom_call_target="tpu_custom_call" | custom-call | flops 10000000 | bytes 10000000 | tf_op jit(solution)/shard_map/close/pallas_call | solution.py:614
  (12 shorter events, 0.0 us)
Async XLA Ops:
  0.6 21.9 %copy-start.15 = (f32[8,128]{1,0:T(8,128)S(1)}, f32[8,128]{1,0:T(8,128)}, u32[]{:S(2)}) copy-start(f32[8,128]{1,0:T(8,128)} %constant.41.clone.q_ref) | copy-start | bytes 12292
  0.6 21.9 %copy-start.10 = (bf16[2,128,128]{2,1,0:T(8,128)(2,1)S(1)}, bf16[2,128,128]{2,1,0:T(8,128)(2,1)}, u32[]{:S(2)}) copy-start(bf16[2,128,128]{2,1,0:T(8,128)(2,1)} %constant.39.clone.dr_m) | copy-start | bytes 196612
  1.6 0.8 copy-start.16
  2.4 1.0 copy-start
  3.4 1.1 copy-start.2
  4.5 1.0 copy-start.4
  5.5 17.0 %copy-start.1 = (f32[7,16,8,128]{3,2,1,0:T(8,128)S(1)}, f32[7,16,8,128]{3,2,1,0:T(8,128)}, u32[]{:S(2)}) copy-start(f32[7,16,8,128]{3,2,1,0:T(8,128)} %s.5) | copy-start | bytes 1376260
  5.5 17.0 %copy-start.9 = (bf16[2,1024,128]{2,1,0:T(8,128)(2,1)S(1)}, bf16[2,1024,128]{2,1,0:T(8,128)(2,1)}, u32[]{:S(2)}) copy-start(bf16[2,1024,128]{2,1,0:T(8,128)(2,1)} %constant.40.clone.items) | copy-start | bytes 1572868
  6.4 16.2 %collective-permute-start = (f32[109,8,128]{2,1,0:T(8,128)S(1)}, f32[109,8,128]{2,1,0:T(8,128)S(1)}, u32[]{:S(2)}, u32[]{:S(2)}) collective-permute-start(f32[109,8,128]{2,1,0:T(8,128)S(1)} %get-tuple-element.16), channel_id=1, source_target_pairs={{0,8},{8,16},{16,24},{24,32},{32,40},{40,48},{48,56},{56,64},{64,7... | collective-permute-start | bytes 1339400 | tf_op jit(solution)/shard_map/ppermute | solution.py:629
  11.3 11.3 %collective-permute-start.1 = (f32[70,8,128]{2,1,0:T(8,128)S(1)}, f32[70,8,128]{2,1,0:T(8,128)S(1)}, u32[]{:S(2)}, u32[]{:S(2)}) collective-permute-start(f32[70,8,128]{2,1,0:T(8,128)S(1)} %get-tuple-element.17), channel_id=1, source_target_pairs={{8,0},{16,8},{24,16},{32,24},{40,32},{48,40},{56,48},{64,56},{72,6... | collective-permute-start | bytes 860168 | tf_op jit(solution)/shard_map/ppermute | solution.py:629
  27.2 39.1 %copy-start.6 = (bf16[2,128,1024]{2,1,0:T(8,128)(2,1)S(1)}, bf16[2,128,1024]{2,1,0:T(8,128)(2,1)}, u32[]{:S(2)}) copy-start(bf16[2,128,1024]{2,1,0:T(8,128)(2,1)} %constant.46.clone.wz) | copy-start | bytes 1572868
  27.2 39.1 %copy-start.7 = (bf16[2,2,128,512]{3,2,1,0:T(8,128)(2,1)S(1)}, bf16[2,2,128,512]{3,2,1,0:T(8,128)(2,1)}, u32[]{:S(2)}) copy-start(bf16[2,2,128,512]{3,2,1,0:T(8,128)(2,1)} %constant.45.clone.wr) | copy-start | bytes 1572868
  27.2 38.4 %all-to-all-start = ((f32[8,38,8,128]{3,2,1,0:T(8,128)}), f32[8,38,8,128]{3,2,1,0:T(8,128)S(1)}, u32[]{:S(2)}, u32[]{:S(2)}) async-start(f32[8,38,8,128]{3,2,1,0:T(8,128)} %get-tuple-element.18), calls=%async_computation | async-start | bytes 2490368 | tf_op jit(solution)/shard_map/all_to_all | solution.py:667
  66.2 1.0 copy-start.8
  67.3 0.9 copy-start.12
  68.2 0.8 copy-start.13
  69.0 0.8 copy-start.14
  72.8 26.0 %copy-start.3 = (f32[12,16,8,128]{3,2,1,0:T(8,128)S(1)}, f32[12,16,8,128]{3,2,1,0:T(8,128)}, u32[]{:S(2)}) copy-start(f32[12,16,8,128]{3,2,1,0:T(8,128)} %psi.3) | copy-start | bytes 2359300
  72.8 26.0 %copy-start.5 = (f32[6,16,8,128]{3,2,1,0:T(8,128)S(1)}, f32[6,16,8,128]{3,2,1,0:T(8,128)}, u32[]{:S(2)}) copy-start(f32[6,16,8,128]{3,2,1,0:T(8,128)} %v.3) | copy-start | bytes 1179652
  72.8 26.0 %copy-start.11 = (bf16[2,128,128]{2,1,0:T(8,128)(2,1)S(1)}, bf16[2,128,128]{2,1,0:T(8,128)(2,1)}, u32[]{:S(2)}) copy-start(bf16[2,128,128]{2,1,0:T(8,128)(2,1)} %constant.39.clone.dr_m) | copy-start | bytes 196612
  103.3 10.6 %collective-permute-start.2 = (f32[4,8,128]{2,1,0:T(8,128)S(1)}, f32[4,8,128]{2,1,0:T(8,128)S(1)}, u32[]{:S(2)}, u32[]{:S(2)}) collective-permute-start(f32[4,8,128]{2,1,0:T(8,128)S(1)} %get-tuple-element.22), channel_id=1, source_target_pairs={{0,8},{8,16},{16,24},{24,32},{32,40},{40,48},{48,56},{56,64},{64,7... | collective-permute-start | bytes 49160 | tf_op jit(solution)/shard_map/ppermute | solution.py:629
  111.9 8.4 %collective-permute-start.3 = (f32[4,8,128]{2,1,0:T(8,128)S(1)}, f32[4,8,128]{2,1,0:T(8,128)S(1)}, u32[]{:S(2)}, u32[]{:S(2)}) collective-permute-start(f32[4,8,128]{2,1,0:T(8,128)S(1)} %get-tuple-element.23), channel_id=1, source_target_pairs={{8,0},{16,8},{24,16},{32,24},{40,32},{48,40},{56,48},{64,56},{72,6... | collective-permute-start | bytes 49160 | tf_op jit(solution)/shard_map/ppermute | solution.py:629

commit v2 on v1

--- a/solution.py
+++ b/solution.py
@@ -21,8 +21,14 @@
 R_INNER = 1.0
 F32 = jnp.float32
 BF16 = jnp.bfloat16
-FIELDS_IN = 19
+FIELDS_IN = 18
 FIELDS_OUT = 14
+VMEM_LIMIT = 32 * 2**20
+VMEM_FULL = 56 * 2**20
+SHARED = ("cv", "cf", "cr", "bulk", "couple", "modulus", "shear")
+OWN = SHARED + ("fric", "kappa", "omega", "decay0", "decay1", "decay2", "decay3")
+FLAGS = len(OWN)
+RING = SHARED + ("fk",)
 
 
 def gll_basis():
@@ -64,11 +70,6 @@
     modes = np.arange(1, NT // 2)
     phases = 2.0 * np.pi * offsets[:, :, None] * modes / NT
     return -(2.0 / NT) * np.sum(modes * np.sin(phases), axis=2)
-
-
-def inverse_radius():
-    positions = np.arange(NR)
-    return 1.0 / (R_INNER + positions // 4 + 0.5 * (1.0 + NODES[positions % 4]))
 
 
 @functools.lru_cache(None)
@@ -101,11 +102,6 @@
                 wz[2 * f + side, r, f, :, r] = spread[side]
     c["wr"] = np.stack([halves(w) for w in wr.reshape(2, 128, 512)])
     c["wz"] = halves(wz.reshape(128, 1024))
-    q = inverse_radius().astype(np.float32)
-    c["q"] = np.broadcast_to(q, (8, NR)).copy()
-    c["qg"] = np.broadcast_to(
-        np.tile(q.reshape(groups, 1, GROUP), (1, PLANES, 1)).reshape(groups, 1, 256), (groups, 8, 256)
-    ).copy()
     return c
 
 
@@ -127,19 +123,38 @@
     return dot(xh, hi) + dot(xl, hi) + dot(xh, lo)
 
 
+def inverse_radius(group, width):
+    lane = lax.broadcasted_iota(jnp.int32, (8, 128 if width == NR else 256), 1) % width
+    place = lane % 4
+    offset = jnp.zeros(lane.shape, F32)
+    for j in range(4):
+        offset = jnp.where(place == j, float(R_INNER + 0.5 * (1.0 + NODES[j])), offset)
+    return 1.0 / (offset + (lane // 4 + 4 * group).astype(F32))
+
+
+def own_ids(lids):
+    row = lax.broadcasted_iota(jnp.int32, (8, NR), 0)
+    fluid = lax.broadcasted_iota(jnp.int32, (8, NR), 1) < 4 * RB
+    value = jnp.zeros((8, NR), jnp.int32)
+    for e in range(4):
+        value = jnp.where(row == 2 + e, jnp.where(fluid, lids[e, 0], lids[e, NR // 4 - 1]), value)
+    return value.astype(F32)
+
+
 def coefficients(ids, tab):
     hits = [ids == float(m) for m in range(8)]
-
-    def pick(column):
-        value = jnp.where(hits[0], tab[0, column], 0.0)
+    materials, jkd = tab
+
+    def pick(table, column):
+        value = jnp.where(hits[0], table[0, column], 0.0)
         for m in range(1, 8):
-            value = jnp.where(hits[m], tab[m, column], value)
+            value = jnp.where(hits[m], table[m, column], value)
         return value
 
-    lame, mu, modulus, beta, rho, rho_f, tort, fric = [pick(c) for c in range(8)]
-    omega = pick(8)
-    weights = [pick(9 + l) for l in range(4)]
-    rates = [pick(13 + l) for l in range(4)]
+    lame, mu, modulus, beta, rho, rho_f, tort, fric = [pick(materials, c) for c in range(8)]
+    omega = pick(jkd, 0)
+    weights = [pick(jkd, 1 + l) for l in range(4)]
+    rates = [pick(jkd, 5 + l) for l in range(4)]
     rho_w = tort * rho_f
     scale = DT / (rho * rho_w - rho_f * rho_f)
     decay = [1.0 / (1.0 + DT * (rate + omega)) for rate in rates]
@@ -152,7 +167,12 @@
         omega=DT * omega,
         weights=weights,
         decay=decay,
+        decay0=decay[0],
+        decay1=decay[1],
+        decay2=decay[2],
+        decay3=decay[3],
         kappa=(1.0 + DT * omega) * gain,
+        fk=fric * ((1.0 + DT * omega) * gain),
         bulk=DT * (lame + beta * beta * modulus),
         couple=DT * beta * modulus,
         modulus=DT * modulus,
@@ -221,8 +241,42 @@
     return x.reshape(-1, NR)
 
 
-def prepare(v, s, psi, ids, tab, vw, t_out, up, dn):
-    c = coefficients(ids[...], tab)
+def prepare(
+    lids_hbm, mat_hbm, jkd_hbm, src_hbm, psi_hbm, v_hbm, s_hbm,
+    vw, t_out, up, dn, coef, ring_coef,
+    lids, mat, jkd, src, psi, v, s, sems,
+):
+    pairs = (
+        (lids_hbm, lids), (mat_hbm, mat), (jkd_hbm, jkd), (src_hbm, src), (psi_hbm, psi), (v_hbm, v), (s_hbm, s)
+    )
+    copies = [pltpu.make_async_copy(a, b, sems.at[i]) for i, (a, b) in enumerate(pairs)]
+    for copy in copies:
+        copy.start()
+    for copy in copies[:4]:
+        copy.wait()
+    device = lax.axis_index("depth")
+    rows = lax.broadcasted_iota(jnp.int32, (8, NR), 0)
+    c = coefficients(own_ids(lids), (mat, jkd))
+    mine = (rows >= 2) & (rows < 6)
+    for n, name in enumerate(OWN):
+        coef[n] = jnp.where(mine, c[name], 0.0)
+    source = (src[0] - PLANES * device).astype(F32)
+    coef[FLAGS] = jnp.full((8, NR), jnp.where(device > 0, 1.0, 0.0), F32)
+    coef[FLAGS + 1] = jnp.full((8, NR), jnp.where(device < lax.axis_size("depth") - 1, 1.0, 0.0), F32)
+    coef[FLAGS + 2] = jnp.full((8, NR), source, F32)
+    for n, name in enumerate(SHARED):
+        swapped = pltpu.roll(c[name], 4, 0)
+        up[108 + n] = jnp.where(rows < 2, swapped, 0.0)
+        dn[69 + n] = jnp.where(rows >= 6, swapped, 0.0)
+    element = lax.broadcasted_iota(jnp.int32, (8, 256), 1) // 64
+    group = lax.axis_index("az")
+    ids = jnp.zeros((8, 256), jnp.int32)
+    for e in range(4):
+        ids = jnp.where(element == e, lids[e, 4 * group], ids)
+    rc = coefficients(ids.astype(F32), (mat, jkd))
+    for n, name in enumerate(RING):
+        ring_coef[n] = rc[name]
+    ring_coef[len(RING)] = jnp.full((8, 256), source, F32)
 
     def sp(value):
         return spread_rows(value, 2, 4)
@@ -231,6 +285,8 @@
     cf = sp(c["cf"] * c["fric"])
     cr = sp(c["cr"] * c["fric"])
     decayed = [sp(w * d) for w, d in zip(c["weights"], c["decay"])]
+    for copy in copies[4:]:
+        copy.wait()
     for i in range(3):
         memory = [psi[3 * l + i] for l in range(4)]
         total = sum(w * m for w, m in zip(weights, memory))
@@ -248,20 +304,15 @@
         nodes = [s[f, 4 + l] for l in range(5)]
         up[104 + i] = combine(ROW[4], nodes)
         dn[65 + i] = combine(ROW[0], nodes)
-    own = ids[...]
-    rows = lax.broadcasted_iota(jnp.int32, (8, NR), 0)
-    up[108] = jnp.where(rows < 2, pltpu.roll(own, 4, 0), 0.0)
-    dn[69] = jnp.where(rows >= 6, pltpu.roll(own, 4, 0), 0.0)
-
-
-def launch(s, vw, t_in, up, dn, ids, tab, info, dr_m, items, q_ref, pk, keep):
-    has_below = info[1].astype(F32)
-    has_above = info[2].astype(F32)
-    own = ids[...]
-    rows = lax.broadcasted_iota(jnp.int32, (8, NR), 0)
-    own = jnp.where((rows >= 2) & (rows < 6), own, 0.0)
-    c = coefficients(own + up[108] + dn[69], tab)
-    q = q_ref[...]
+
+
+def launch(s, vw, t_in, up, dn, coef, dr_m, items, pk, keep):
+    has_below = coef[FLAGS]
+    has_above = coef[FLAGS + 1]
+    c = {name: coef[n] for n, name in enumerate(OWN)}
+    for n, name in enumerate(SHARED):
+        c[name] = c[name] + up[108 + n] + dn[69 + n]
+    q = inverse_radius(0, NR)
 
     def radial(fields):
         stacked = jnp.concatenate([flat(x) for x in fields], axis=0)
@@ -320,14 +371,14 @@
         a = cv[8:24] * d[8:24] + cf[8:24] * g
         b = cf[8:24] * d[8:24] + cr[8:24] * g
         pack(4 + i, v1[i][8:24])
-        pack(7 + i, w1[i][8:24])
-        pack(10 + i, a)
+        pack(9 + i, a)
         keep[i] = v1[i][8:24]
         keep[3 + i] = w1[i][8:24]
         keep[6 + i] = a
         keep[9 + i] = b
         if i == 1:
-            pack(13, b)
+            pack(7, w1[i][8:24])
+            pack(12, b)
 
     bulk, couple, modulus, shear = [
         spread_rows(c[n], 1, 6)[:21] for n in ("bulk", "couple", "modulus", "shear")
@@ -335,7 +386,7 @@
     mask21 = jnp.where(lax.broadcasted_iota(jnp.int32, (21, 8, NR), 0) < 20, 1.0, has_above)
     plane21 = lax.broadcasted_iota(jnp.int32, (21, 8, NR), 0) - 4
     lane21 = lax.broadcasted_iota(jnp.int32, (21, 8, NR), 2)
-    source = jnp.where((plane21 == info[0]) & (lane21 < 4 * RB), SOURCE, 0.0)
+    source = jnp.where((plane21.astype(F32) == coef[FLAGS + 2]) & (lane21 < 4 * RB), SOURCE, 0.0)
 
     def stresses(v, w, extra):
         inner = slice(4, 25)
@@ -354,9 +405,11 @@
             rz=mask21 * (shear * (z_r + r_z)),
             tz=mask21 * (shear * g_tz),
             p=mask21 * (-(couple * div_v + modulus * div_w) + (source if extra is None else 0.0)),
+            w=div_w,
         )
 
     x0 = stresses(v1, w1, None)
+    pack(8, x0["w"][4:20])
     inner = slice(4, 25)
     x1 = stresses(u, uw, [q * v1[0][inner], q * v1[1][inner], q * v1[2][inner], q * w1[1][inner]])
     e2, dw2 = q * u[1][inner], q * uw[1][inner]
@@ -370,40 +423,48 @@
     )
 
     def radius_items(fields):
-        stacked = jnp.concatenate([flat(x) for x in fields], axis=1)
-        return mm(stacked, items[0], items[1]).reshape(-1, 8, NR)
+        slots = [i for i, x in enumerate(fields) if x is not None]
+        stacked = jnp.concatenate([flat(fields[i]) for i in slots], axis=1)
+        hi, lo = [jnp.concatenate([items[h, NR * i : NR * i + NR] for i in slots], axis=0) for h in range(2)]
+        return mm(stacked, hi, lo).reshape(-1, 8, NR)
 
     def depth_items(fields, first):
         out = []
         for x in fields:
-            out.append(x[first + 20])
-            out.append(has_below * below_partial(x[first : first + 4]))
+            if x is None:
+                out += [jnp.zeros((8, NR), F32)] * 2
+            else:
+                out.append(x[first + 20])
+                out.append(has_below * below_partial(x[first : first + 4]))
         return jnp.stack(out)
 
-    velocity_r = [v1[0], v1[1], v1[2], w1[0], u[0], u[1], u[2], uw[0]]
-    pack(14, radius_items([x[8:24] for x in velocity_r]))
+    velocity_r = [v1[0][8:24], v1[1][8:24], v1[2][8:24], None] + [x[8:24] for x in (u[0], u[1], u[2], uw[0])]
+    pack(13, radius_items(velocity_r))
     names_r = ("rr", "rt", "rz", "p")
-    pack(15, radius_items([x[n][4:20] for x in (x0, x1) for n in names_r]))
-    pack(16, depth_items([v1[0], v1[1], v1[2], w1[2], u[0], u[1], u[2], uw[2]], 4))
+    pack(14, radius_items([x[n][4:20] for x in (x0, x1) for n in names_r]))
+    pack(15, depth_items([v1[0], v1[1], v1[2], None, u[0], u[1], u[2], uw[2]], 4))
     names_z = ("rz", "tz", "zz", "p")
-    pack(17, depth_items([x[n] for x in (x0, x1) for n in names_z], 0))
-    zero8 = jnp.zeros((8, 8, NR), F32)
-    second = [x2[n][4 + 8 * h : 12 + 8 * h] if n in x2 else zero8 for h in range(2) for n in names_r]
-    zero21 = jnp.zeros((21, 8, NR), F32)
-    pack(
-        18,
-        jnp.concatenate(
-            [radius_items(second), depth_items([x2[n] if n in x2 else zero21 for n in names_z], 0)], axis=0
-        ),
-    )
-
-
-def ring(recv, ids, tab, info, dt_m, mr, mz, wr, wz, qg, out):
-    c = coefficients(ids[...], tab)
-    group = info[3]
-    q = qg[group]
-    sel_r = info[4]
-    sel_z = info[5]
+    pack(16, depth_items([x[n] for x in (x0, x1) for n in names_z], 0))
+    second = [x2[n][4 + 8 * h : 12 + 8 * h] if n in x2 else None for h in range(2) for n in names_r]
+    pack(17, jnp.concatenate([radius_items(second), depth_items([x2.get(n) for n in names_z], 0)], axis=0))
+
+
+def ring(
+    recv, coef, dt_hbm, mr_hbm, mz_hbm, wr_hbm, wz_hbm, out, dt_m, mr, mz, wr, wz, sems
+):
+    group = lax.axis_index("az")
+    first_r = jnp.where(group == 0, 1, 0)
+    first_z = jnp.where(lax.axis_index("depth") == 0, 1, 0)
+    sources = (dt_hbm, wr_hbm, wz_hbm, mr_hbm.at[first_r], mz_hbm.at[first_z])
+    copies = [
+        pltpu.make_async_copy(a, b, sems.at[i]) for i, (a, b) in enumerate(zip(sources, (dt_m, wr, wz, mr, mz)))
+    ]
+    for copy in copies:
+        copy.start()
+    c = {name: coef[n] for n, name in enumerate(RING)}
+    q = inverse_radius(group, GROUP)
+    for copy in copies:
+        copy.wait()
 
     def field(f):
         return jnp.concatenate([recv[:, 2 * f], recv[:, 2 * f + 1]], axis=-1)
@@ -423,8 +484,8 @@
         x = x.reshape(NT, 256)
         return [x[:, :128], x[:, 128:]]
 
-    mr_h, mr_l = mr[sel_r, 0], mr[sel_r, 1]
-    mz_h, mz_l = mz[sel_z, 0], mz[sel_z, 1]
+    mr_h, mr_l = mr[0], mr[1]
+    mz_h, mz_l = mz[0], mz[1]
 
     def radial(fields, halo):
         stacked = jnp.concatenate([h for f in fields for h in by_half(f)], axis=0)
@@ -447,10 +508,10 @@
         ]
 
     rt, tt, tz, p = [field(f) for f in range(4)]
-    pr2, pr3 = field(14), field(15)
-    pd2 = [recv[:, 32], recv[:, 33]]
-    pd3 = [recv[:, 34], recv[:, 35]]
-    px = field(18)
+    pr2, pr3 = field(13), field(14)
+    pd2 = [recv[:, 30], recv[:, 31]]
+    pd3 = [recv[:, 32], recv[:, 33]]
+    px = field(17)
     s_rt, s_tt, s_tz, s_p, d_pr2, d_pr3, d_pd2, d_pd3, d_px = az([rt, tt, tz, p, pr2, pr3, pd2[1], pd3[1], px])
     (dd_px,) = az([d_px])
     wr0, wr1 = (wr[0, 0], wr[0, 1]), (wr[1, 0], wr[1, 1])
@@ -475,17 +536,17 @@
         field(5) + cv * q_tt + cf * q_p,
         field(6) + cv * q_tz,
     ]
-    w1 = [field(7 + i) + dw[i] for i in range(3)]
-    r_r, r_t, r_z, r_w = radial([v1[0], v1[1], v1[2], w1[0]], hr2)
-    z_r, z_t, z_z, z_w = depth([v1[0], v1[1], v1[2], w1[2]], hz2)
-    a_r, a_t, a_z, a_w = az([v1[0], v1[1], v1[2], w1[1]])
+    w1_t = field(7) + dw[1]
+    r_r, r_t, r_z, r_w = radial([v1[0], v1[1], v1[2], dw[0]], hr2)
+    z_r, z_t, z_z, z_w = depth([v1[0], v1[1], v1[2], dw[2]], hz2)
+    a_r, a_t, a_z, a_w = az([v1[0], v1[1], v1[2], w1_t])
     e_tt = q * (v1[0] + a_t)
     div_v = r_r + e_tt + z_z
-    div_w = r_w + q * (w1[0] + a_w) + z_w
+    div_w = field(8) + r_w + q * (dw[0] + a_w) + z_w
     total = c["bulk"] * div_v + c["couple"] * div_w
     shear = c["shear"]
     lanes = lax.broadcasted_iota(jnp.int32, (8, 256), 1) // GROUP
-    source = jnp.where((lanes == info[0]) & (group == 0), SOURCE, 0.0)
+    source = jnp.where(lanes.astype(F32) == coef[len(RING)], jnp.where(group == 0, SOURCE, 0.0), 0.0)
     n_rr = total + 2.0 * shear * r_r
     n_tt = total + 2.0 * shear * e_tt
     n_zz = total + 2.0 * shear * z_z
@@ -500,15 +561,15 @@
     d_r = q_rt + r_rr + z_rz + q * (a_rt + n_rr - n_tt)
     d_t = q_tt + r_rt + z_tz + q * (a_tt + 2.0 * n_rt)
     d_z = q_tz + r_rz + z_zz + q * (a_tz + n_rz)
-    fk = c["fric"] * c["kappa"]
+    fk = c["fk"]
     g_r = r_p + fk * dw[0]
     g_t = q_p + q * a_p + fk * dw[1]
     g_z = z_p + fk * dw[2]
     sums = [
-        2.0 * v1[0] + field(10) + cv * d_r + cf * g_r,
-        2.0 * v1[1] + field(11) + cv * d_t + cf * g_t,
-        2.0 * v1[2] + field(12) + cv * d_z + cf * g_z,
-        2.0 * w1[1] - field(13) - cf * d_t - cr * g_t,
+        2.0 * v1[0] + field(9) + cv * d_r + cf * g_r,
+        2.0 * v1[1] + field(10) + cv * d_t + cf * g_t,
+        2.0 * v1[2] + field(11) + cv * d_z + cf * g_z,
+        2.0 * w1_t - field(12) - cf * d_t - cr * g_t,
     ]
     results = [s_rt, s_tt, s_tz, s_p, d_r, d_t, d_z, g_r, g_t, g_z] + az(sums)
     for f, x in enumerate(results):
@@ -516,111 +577,136 @@
         out[:, 2 * f + 1] = x[:, :, 128:]
 
 
-def finish(recv, keep, v, s, psi, ids, tab, info, dr_m, q_ref, v_out, s_out, m_out, up, dn):
-    has_below = info[1].astype(F32)
-    c = coefficients(ids[...], tab)
-    q = q_ref[...]
-
-    def sp(value):
-        return spread_rows(value, 2, 4)
-
-    def unpack(f):
-        planes = []
-        for g in range(2):
-            planes += exchange_groups([recv[k, 2 * f + g] for k in range(8)])
-        return jnp.stack(planes)
-
-    cv, cf, cr = sp(c["cv"]), sp(c["cf"]), sp(c["cr"])
-    q_rt, q_tt, q_tz, q_p = [q * unpack(f) for f in range(4)]
+def unpack(recv, f):
+    planes = []
+    for g in range(2):
+        planes += exchange_groups([recv[k, 2 * f + g] for k in range(8)])
+    return jnp.stack(planes)
+
+
+def advance(recv, keep, coef, v_out, mid, up, dn):
+    c = {name: coef[n] for n, name in enumerate(OWN)}
+    q = inverse_radius(0, NR)
+    cv, cf, cr = [spread_rows(c[n], 2, 4) for n in ("cv", "cf", "cr")]
+    q_rt, q_tt, q_tz, q_p = [q * unpack(recv, f) for f in range(4)]
     dv = [cv * q_rt, cv * q_tt + cf * q_p, cv * q_tz]
     dw = [-(cf * q_rt), -(cf * q_tt + cr * q_p), -(cf * q_tz)]
-    sums_v, sums_w = [], []
-    omega = sp(c["omega"])
-    decay = [sp(d) for d in c["decay"]]
     for i in range(3):
-        d, g = unpack(4 + i), unpack(7 + i)
+        d, g = unpack(recv, 4 + i), unpack(recv, 7 + i)
         v1 = keep[i] + dv[i]
         w1 = keep[3 + i] + dw[i]
         v2 = v1 + keep[6 + i] + cv * d + cf * g
         w2 = w1 - keep[9 + i] - cf * d - cr * g
         v_out[i] = v2
         v_out[3 + i] = w2
-        sums_v.append(v1 + v2)
-        sums_w.append(w1 + w2)
+        mid[i] = v1
+        mid[3 + i] = w1
+        x = v1 + v2
+        up[i] = below_partial(x[12:])
+        dn[i] = x[0]
+        if i == 2:
+            x = w1 + w2
+            up[3] = below_partial(x[12:])
+            dn[3] = x[0]
+
+
+def settle(recv, v2, mid, v, s, psi, coef, dr_m, s_out, m_out, edge):
+    has_below = coef[FLAGS]
+    c = {name: coef[n] for n, name in enumerate(OWN)}
+    q = inverse_radius(0, NR)
+
+    def sp(value):
+        return spread_rows(value, 2, 4)
+
+    omega = sp(c["omega"])
+    decay = [sp(c[f"decay{l}"]) for l in range(4)]
+    for i in range(3):
+        w1, w2 = mid[3 + i], v2[3 + i]
         first = w1 - v[3 + i] + omega * w1
         second = w2 - w1 + omega * w2
         for l in range(4):
             m_out[3 * l + i] = decay[l] * (decay[l] * (psi[3 * l + i] + first) + second)
-    halo = [sums_v[0], sums_v[1], sums_v[2], sums_w[2]]
-    for i, x in enumerate(halo):
-        up[i] = below_partial(x[12:])
-        dn[i] = x[0]
+    sums = [mid[i] + v2[i] for i in range(6)]
     zero = jnp.zeros((1, 8, NR), F32)
     z_r, z_t, z_z, z_w = [
         depth_derivative(jnp.concatenate([x, zero], axis=0), 0, 4, 0, has_below, float(ROW[4, 4]) * x[0], zero[0])[:16]
-        for x in halo
-    ]
-    stacked = jnp.concatenate([flat(x) for x in (sums_v[0], sums_v[1], sums_v[2], sums_w[0])], axis=0)
+        for x in (sums[0], sums[1], sums[2], sums[5])
+    ]
+    stacked = jnp.concatenate([flat(x) for x in sums[:4]], axis=0)
     y = mm(stacked, dr_m[0], dr_m[1])
     r_r, r_t, r_z, r_w = [y[128 * i : 128 * i + 128].reshape(16, 8, NR) for i in range(4)]
-    a_r, a_t, a_z, a_w = [unpack(10 + i) for i in range(4)]
-    e_tt = q * (sums_v[0] + a_t)
+    a_r, a_t, a_z, a_w = [unpack(recv, 10 + i) for i in range(4)]
+    e_tt = q * (sums[0] + a_t)
     div_v = r_r + e_tt + z_z
-    div_w = r_w + q * (sums_w[0] + a_w) + z_w
+    div_w = r_w + q * (sums[3] + a_w) + z_w
     couple, shear = sp(c["couple"]), sp(c["shear"])
     total = sp(c["bulk"]) * div_v + couple * div_w
     plane = lax.broadcasted_iota(jnp.int32, (16, 8, NR), 0)
     lane = lax.broadcasted_iota(jnp.int32, (16, 8, NR), 2)
-    source = jnp.where((plane == info[0]) & (lane < 4 * RB), SOURCE * (1.0 + math.cos(0.9)), 0.0)
-    s_out[0] = s[0] + total + 2.0 * shear * r_r
-    s_out[1] = s[1] + total + 2.0 * shear * e_tt
-    s_out[2] = s[2] + total + 2.0 * shear * z_z
-    s_out[3] = s[3] + shear * (q * (a_r - sums_v[1]) + r_t)
-    s_out[4] = s[4] + shear * (z_r + r_z)
-    s_out[5] = s[5] + shear * (z_t + q * a_z)
-    s_out[6] = s[6] + source - (couple * div_v + sp(c["modulus"]) * div_w)
-
-
-def close(s, up, dn, ids, tab, info, s_out):
-    has_below = info[1].astype(F32)
-    c = coefficients(ids[...], tab)
-
-    def update(plane, row, z_r, z_t, z_z, z_w):
+    source = jnp.where((plane.astype(F32) == coef[FLAGS + 2]) & (lane < 4 * RB), SOURCE * (1.0 + math.cos(0.9)), 0.0)
+    updates = [
+        total + 2.0 * shear * r_r,
+        total + 2.0 * shear * e_tt,
+        total + 2.0 * shear * z_z,
+        shear * (q * (a_r - sums[1]) + r_t),
+        shear * (z_r + r_z),
+        shear * (z_t + q * a_z),
+        source - (couple * div_v + sp(c["modulus"]) * div_w),
+    ]
+    for f, x in enumerate(updates):
+        x = s[f] + x
+        s_out[f] = x
+        edge[f, 0] = x[0]
+        edge[f, 1:] = x[12:]
+
+
+def close(s_in, edge, up, dn, coef, s_out, new, sems):
+    has_below = coef[FLAGS]
+    c = {name: coef[n] for n, name in enumerate(OWN)}
+
+    def update(slot, row, z_r, z_t, z_z, z_w):
         def at(name):
             return jnp.broadcast_to(c[name][row : row + 1, :], (8, NR))
 
         bulk, couple, modulus, shear = at("bulk"), at("couple"), at("modulus"), at("shear")
         total = bulk * z_z + couple * z_w
-        s_out[0, plane] = s[0, plane] + total
-        s_out[1, plane] = s[1, plane] + total
-        s_out[2, plane] = s[2, plane] + total + 2.0 * shear * z_z
-        s_out[3, plane] = s[3, plane]
-        s_out[4, plane] = s[4, plane] + shear * z_r
-        s_out[5, plane] = s[5, plane] + shear * z_t
-        s_out[6, plane] = s[6, plane] - (couple * z_z + modulus * z_w)
+        new[0, slot] = edge[0, slot] + total
+        new[1, slot] = edge[1, slot] + total
+        new[2, slot] = edge[2, slot] + total + 2.0 * shear * z_z
+        new[3, slot] = edge[3, slot]
+        new[4, slot] = edge[4, slot] + shear * z_r
+        new[5, slot] = edge[5, slot] + shear * z_t
+        new[6, slot] = edge[6, slot] - (couple * z_z + modulus * z_w)
 
     update(0, 2, *[has_below * up[i] for i in range(4)])
-    for plane in range(12, 16):
-        weight = float(ROW[plane - 12, 4])
-        update(plane, 5, *[weight * dn[i] for i in range(4)])
-    for f in range(7):
-        s_out[f, 1:12] = s[f, 1:12]
-
-
-def call(body, inputs, shapes, smem=(), cost=None):
-    specs = [
-        pl.BlockSpec(memory_space=pltpu.SMEM if i in smem else pltpu.VMEM) for i in range(len(inputs))
-    ]
-    out = pl.pallas_call(
+    for slot in range(1, 5):
+        weight = float(ROW[slot - 1, 4])
+        update(slot, 5, *[weight * dn[i] for i in range(4)])
+    copies = [
+        pltpu.make_async_copy(new.at[:, 0:1], s_out.at[:, 0:1], sems.at[0]),
+        pltpu.make_async_copy(new.at[:, 1:5], s_out.at[:, 12:16], sems.at[1]),
+    ]
+    for copy in copies:
+        copy.start()
+    for copy in copies:
+        copy.wait()
+
+
+def call(body, inputs, shapes, hbm=(), scratch=(), out_hbm=False, alias=None, micros=1, vmem=VMEM_LIMIT):
+    def space(i):
+        return pltpu.HBM if i in hbm else pltpu.VMEM
+
+    return pl.pallas_call(
         body,
         out_shape=[jax.ShapeDtypeStruct(x, F32) for x in shapes],
-        in_specs=specs,
-        out_specs=[pl.BlockSpec(memory_space=pltpu.VMEM) for _ in shapes],
-        compiler_params=pltpu.CompilerParams(vmem_limit_bytes=48 * 2**20),
-        cost_estimate=pl.CostEstimate(flops=cost or 10**7, bytes_accessed=10**7, transcendentals=0),
+        in_specs=[pl.BlockSpec(memory_space=space(i)) for i in range(len(inputs))],
+        out_specs=[pl.BlockSpec(memory_space=pltpu.HBM if out_hbm else pltpu.VMEM) for _ in shapes],
+        scratch_shapes=list(scratch),
+        input_output_aliases=alias or {},
+        compiler_params=pltpu.CompilerParams(vmem_limit_bytes=vmem),
+        cost_estimate=pl.CostEstimate(flops=0, bytes_accessed=3 * 10**6 * micros, transcendentals=0),
         name=body.__name__,
     )(*inputs)
-    return out
 
 
 def shift(value, steps):
@@ -631,55 +717,59 @@
 
 def on_device(velocity, stress, memory, layer_ids, materials, jkd, source_depth):
     c = constants()
-    row = lax.axis_index("depth")
-    group = lax.axis_index("az")
-    tab = jnp.concatenate([materials, jkd], axis=1)
-    first = (row == 0).astype(jnp.int32)
-    last = (row == lax.axis_size("depth") - 1).astype(jnp.int32)
-    info = jnp.stack(
-        [
-            source_depth[0] - PLANES * row,
-            1 - first,
-            1 - last,
-            group,
-            (group == 0).astype(jnp.int32),
-            first,
-        ]
-    ).astype(jnp.int32)
-    ids = jnp.repeat(layer_ids.astype(F32), 4, axis=1)
-    ids_own = jnp.pad(ids, ((2, 2), (0, 0)))
-    ids_group = lax.dynamic_slice_in_dim(ids, GROUP * group, GROUP, axis=1)
-    ids_group = jnp.broadcast_to(jnp.repeat(ids_group, 4, axis=0).reshape(1, 256), (8, 256))
     block = (PLANES, AZ, NR)
-    vw, t_part, up, dn = call(
+    tables = [layer_ids, materials, jkd, source_depth]
+    vw, t_part, up, dn, coef, ring_coef = call(
         prepare,
-        [velocity, stress, memory, ids_own, tab],
-        [(6,) + block, (3,) + block, (109, AZ, NR), (70, AZ, NR)],
-        smem=(4,),
+        tables + [memory, velocity, stress],
+        [(6,) + block, (3,) + block, (115, AZ, NR), (76, AZ, NR), (FLAGS + 3, 8, NR), (len(RING) + 1, 8, 256)],
+        hbm=range(7),
+        scratch=[pltpu.SMEM(x.shape, x.dtype) for x in tables]
+        + [pltpu.VMEM((n,) + block, F32) for n in (12, 6, 7)]
+        + [pltpu.SemaphoreType.DMA((7,))],
+        vmem=VMEM_FULL,
     )
     up, dn = shift(up, 1), shift(dn, -1)
     packed, keep = call(
         launch,
-        [stress, vw, t_part, up, dn, ids_own, tab, info, c["dr"], c["items"], c["q"]],
+        [stress, vw, t_part, up, dn, coef, c["dr"], c["items"]],
         [(8, 2 * FIELDS_IN, AZ, NR), (12,) + block],
-        smem=(6, 7),
+        micros=4,
     )
     packed = lax.all_to_all(packed, "az", split_axis=0, concat_axis=0, tiled=True)
+    matrices = [c[n] for n in ("dt", "mr", "mz", "wr", "wz")]
+    shapes = [m.shape[1:] if n in (1, 2) else m.shape for n, m in enumerate(matrices)]
     (back,) = call(
         ring,
-        [packed, ids_group, tab, info, c["dt"], c["mr"], c["mz"], c["wr"], c["wz"], c["qg"]],
+        [packed, ring_coef] + matrices,
         [(8, 2 * FIELDS_OUT, AZ, NR)],
-        smem=(2, 3),
+        hbm=range(2, 7),
+        scratch=[pltpu.VMEM(x, BF16) for x in shapes] + [pltpu.SemaphoreType.DMA((5,))],
+        micros=3,
+        vmem=VMEM_FULL,
     )
     back = lax.all_to_all(back, "az", split_axis=0, concat_axis=0, tiled=True)
-    v_out, s_part, m_out, up, dn = call(
-        finish,
-        [back, keep, velocity, stress, memory, ids_own, tab, info, c["dr"], c["q"]],
-        [(6,) + block, (7,) + block, (12,) + block, (4, AZ, NR), (4, AZ, NR)],
-        smem=(6, 7),
+    v_out, mid, up, dn = call(
+        advance,
+        [back, keep, coef],
+        [(6,) + block, (6,) + block, (4, AZ, NR), (4, AZ, NR)],
     )
     up, dn = shift(up, 1), shift(dn, -1)
-    (s_out,) = call(close, [s_part, up, dn, ids_own, tab, info], [(7,) + block], smem=(4, 5))
+    s_part, m_out, edge = call(
+        settle,
+        [back, v_out, mid, velocity, stress, memory, coef, c["dr"]],
+        [(7,) + block, (12,) + block, (7, 5, AZ, NR)],
+        micros=3,
+    )
+    (s_out,) = call(
+        close,
+        [s_part, edge, up, dn, coef],
+        [(7,) + block],
+        hbm=(0,),
+        scratch=[pltpu.VMEM((7, 5, AZ, NR), F32), pltpu.SemaphoreType.DMA((2,))],
+        out_hbm=True,
+        alias={0: 0},
+    )
     return v_out, s_out, m_out
 
 

time: 122 us -> 113 us (0.926)
  blocking collectives: 25.9 us -> 63 us
  waiting for transfers between devices: 40.5 us -> 13.8 us
  starting transfers between devices: 27.5 us -> 14.7 us
  local copies, waits for them, and re-layouts: 10.4 us -> 3.82 us
  Pallas kernels: 14.3 us -> 16.1 us
  other arithmetic: 1.5 us -> 0 us
    all_to_all x0 -> x1, blocking collectives: none -> 36.8 us  [on_device(): lax.all_to_all(packed, 'az', split_axis=0, concat_axis=0, tiled=True)]
    all_to_all x1 -> x0, waiting for transfers between devices: 25.5 us -> none  [on_device(): lax.all_to_all(packed, 'az', split_axis=0, concat_axis=0, tiled=True)]
    all_to_all x1 -> x0, starting transfers between devices: 10.2 us -> none  [on_device(): lax.all_to_all(packed, 'az', split_axis=0, concat_axis=0, tiled=True)]
    unnamed x34 -> x20, local copies, waits for them, and re-layouts: 6.74 us -> 3.82 us
    broadcast_in_dim x4 -> x0, local copies, waits for them, and re-layouts: 2.7 us -> none  [the longest x2 2.02 us: on_device(): jnp.broadcast_to(jnp.repeat(ids_group, 4, axis=0).reshape(1, 256), (8, 256))]
    ppermute x4, starting transfers between devices: 17.4 us -> 14.7 us  [shift(): lax.ppermute(value, 'depth', [(i, i + steps) for i in range(first, last)])]
    pallas_call x5 -> x6, Pallas kernels: 14.3 us -> 16.1 us  [call(): pl.pallas_call(body, out_shape=[jax.ShapeDtypeStruct(x, F32) for x in sha...]
    ppermute x4, waiting for transfers between devices: 15 us -> 13.8 us  [shift(): lax.ppermute(value, 'depth', [(i, i + steps) for i in range(first, last)])]
  transfers between devices with their start and end apart: 5 -> 4, of which waited for: 3 -> 2; matrix products, arithmetic and copies ran while one was open for 2% -> 0% of each run, Pallas kernels for 0% -> 1%
where the time goes in v2:
time: 113 us
  blocking collectives  63 us (56%)
  Pallas kernels  16.1 us (14%)
  starting transfers between devices  14.7 us (13%)
  waiting for transfers between devices  13.8 us (12%)
  local copies, waits for them, and re-layouts  3.82 us (3%)
  between operations  1.5 us (1%)
    all_to_all x1, blocking collectives, on_device(): lax.all_to_all(packed, 'az', split_axis=0, concat_axis=0, tiled=True)  36.8 us
    all_to_all x1, blocking collectives, on_device(): back = lax.all_to_all(back, 'az', split_axis=0, concat_axis=0, tiled=True)  26.2 us
    pallas_call x6, Pallas kernels, call(): pl.pallas_call(body, out_shape=[jax.ShapeDtypeStruct(x, F32) for x in sha...  16.1 us
    ppermute x4, starting transfers between devices, shift(): lax.ppermute(value, 'depth', [(i, i + steps) for i in range(first, last)])  14.7 us
    ppermute x4, waiting for transfers between devices, shift(): lax.ppermute(value, 'depth', [(i, i + steps) for i in range(first, last)])  13.8 us
    unnamed x20, local copies, waits for them, and re-layouts  3.82 us
  transfers between devices with their start and end apart: 4, of which 2 were waited for; matrix products, arithmetic and copies ran while one was open for 0% of the time, Pallas kernels for 1%

profile of v2, /device:TPU:31, one launch (start us, length us, event | category | flops | bytes accessed | tf_op | source)
XLA Modules:
  0.0 112.8 jit_solution(12118722252145476656)
XLA Ops:
  0.6 0.0 copy-start.8
  0.6 0.0 copy-start.5
  0.7 0.0 copy-start
  1.4 2.7 %prepare.1 = (f32[6,16,8,128]{3,2,1,0:T(8,128)}, f32[3,16,8,128]{3,2,1,0:T(8,128)}, f32[115,8,128]{2,1,0:T(8,128)}, f32[76,8,128]{2,1,0:T(8,128)}, f32[17,8,128]{2,1,0:T(8,128)}, /*index=5*/f32[9,8,256]{2,1,0:T(8,128)}) custom-call(s32[4,32]{1,0:T(4,128)} %lids_hbm.1, f32[8,8]{1,0:T(8,128)} %mat_hbm.1, f32[8,9]{1,0:T(8,128)} %jkd_hbm.1, s32[1]{0:T(128)S(6)} %copy.19.src_hbm, ...), custom_call_target="tpu_custom_call" | custom-call | bytes 3000000 | tf_op jit(solution)/shard_map/prepare/pallas_call | solution.py:699
  4.1 4.9 %collective-permute-start = (f32[115,8,128]{2,1,0:T(8,128)}, f32[115,8,128]{2,1,0:T(8,128)S(1)}, u32[]{:S(2)}, u32[]{:S(2)}) collective-permute-start(f32[115,8,128]{2,1,0:T(8,128)} %get-tuple-element.20), channel_id=1, source_target_pairs={{0,8},{8,16},{16,24},{24,32},{32,40},{40,48},{48,56},{56,64},{64,7... | collective-permute-start | bytes 1413128 | tf_op jit(solution)/shard_map/ppermute | solution.py:715
  9.0 1.9 %collective-permute-start.1 = (f32[76,8,128]{2,1,0:T(8,128)}, f32[76,8,128]{2,1,0:T(8,128)S(1)}, u32[]{:S(2)}, u32[]{:S(2)}) collective-permute-start(f32[76,8,128]{2,1,0:T(8,128)} %get-tuple-element.21), channel_id=1, source_target_pairs={{8,0},{16,8},{24,16},{32,24},{40,32},{48,40},{56,48},{64,56},{72,6... | collective-permute-start | bytes 933896 | tf_op jit(solution)/shard_map/ppermute | solution.py:715
  10.9 9.8 %collective-permute-done.1.dn = f32[76,8,128]{2,1,0:T(8,128)S(1)} collective-permute-done((f32[76,8,128]{2,1,0:T(8,128)}, f32[76,8,128]{2,1,0:T(8,128)S(1)}, u32[]{:S(2)}, u32[]{:S(2)}) %collective-permute-start.1) | collective-permute-done | bytes 311328 | tf_op jit(solution)/shard_map/ppermute | solution.py:715
  20.7 0.0 collective-permute-done.up
  20.7 0.0 copy-done.8
  20.7 0.0 copy-done.5
  20.7 0.0 copy-done
  20.8 0.0 copy-start.3
  20.8 0.9 copy-done.3
  21.6 0.0 copy-start.6
  21.6 1.0 copy-done.6
  22.6 0.0 copy-start.9
  22.6 0.9 copy-done.9
  23.6 2.5 %launch.1 = (f32[8,36,8,128]{3,2,1,0:T(8,128)S(1)}, f32[12,16,8,128]{3,2,1,0:T(8,128)S(1)}) custom-call(f32[7,16,8,128]{3,2,1,0:T(8,128)S(1)} %copy-done, f32[6,16,8,128]{3,2,1,0:T(8,128)S(1)} %copy-done.6, f32[3,16,8,128]{3,2,1,0:T(8,128)S(1)} %copy-done.9, f32[115,8,128]{2,1,0:T(8,128)S(1)} %collective-permute-done.up, ...), custom_call_target="tpu_custom_call" | custom-call | bytes 12000000 | tf_op jit(solution)/shard_map/launch/pallas_call | solution.py:699
  26.0 36.8 %all_to_all.10.recv = f32[8,36,8,128]{3,2,1,0:T(8,128)} all-to-all(f32[8,36,8,128]{3,2,1,0:T(8,128)S(1)} %get-tuple-element.23), channel_id=1, replica_groups=mesh['depth'=64,'az'=8] {'az'}, dimensions={0} | all-to-all | bytes 2359296 | tf_op jit(solution)/shard_map/all_to_all | solution.py:739
  62.8 6.0 %ring.1 = f32[8,28,8,128]{3,2,1,0:T(8,128)} custom-call(f32[8,36,8,128]{3,2,1,0:T(8,128)} %all_to_all.10.recv, f32[9,8,256]{2,1,0:T(8,128)} %get-tuple-element.24.coef, bf16[2,64,64]{2,1,0:T(8,128)(2,1)} %constant.16.clone.dt_hbm, bf16[2,2,128,128]{3,2,1,0:T(8,128)(2,1)} %constant.17.clone.mr_hbm, bf16[2,2,256,256]{3,2,1,0:T(8,128)(2,1)} %constant.18.clone.mz_hbm, ...), custom_call_target="tpu_custom_call" | custom-call | bytes 9000000 | tf_op jit(solution)/shard_map/ring/pallas_call | solution.py:699
  68.8 0.0 copy-start.4
  68.8 26.2 %all_to_all.11.recv = f32[8,28,8,128]{3,2,1,0:T(8,128)S(1)} all-to-all(f32[8,28,8,128]{3,2,1,0:T(8,128)} %ring.1), channel_id=1, replica_groups=mesh['depth'=64,'az'=8] {'az'}, dimensions={0} | all-to-all | bytes 1835008 | tf_op jit(solution)/shard_map/all_to_all | solution.py:751
  95.0 0.0 copy-start.1
  95.0 0.0 copy-start.2
  95.0 0.0 copy-done.4
  95.0 2.8 %advance.1 = (f32[6,16,8,128]{3,2,1,0:T(8,128)}, f32[6,16,8,128]{3,2,1,0:T(8,128)S(1)}, f32[4,8,128]{2,1,0:T(8,128)S(1)}, f32[4,8,128]{2,1,0:T(8,128)S(1)}) custom-call(f32[8,28,8,128]{3,2,1,0:T(8,128)S(1)} %all_to_all.11.recv, f32[12,16,8,128]{3,2,1,0:T(8,128)S(1)} %get-tuple-element.25.keep, f32[17,8,128]{2,1,0:T(8,128)S(1)} %copy-done.4), custom_call_target="tpu_custom_call" | custom-call | bytes 3000000 | tf_op jit(solution)/shard_map/advance/pallas_call | solution.py:699
  97.8 6.0 %collective-permute-start.2 = (f32[4,8,128]{2,1,0:T(8,128)S(1)}, f32[4,8,128]{2,1,0:T(8,128)S(1)}, u32[]{:S(2)}, u32[]{:S(2)}) collective-permute-start(f32[4,8,128]{2,1,0:T(8,128)S(1)} %get-tuple-element.30), channel_id=1, source_target_pairs={{0,8},{8,16},{16,24},{24,32},{32,40},{40,48},{48,56},{56,64},{64,7... | collective-permute-start | bytes 49160 | tf_op jit(solution)/shard_map/ppermute | solution.py:715
  103.8 1.9 %collective-permute-start.3 = (f32[4,8,128]{2,1,0:T(8,128)S(1)}, f32[4,8,128]{2,1,0:T(8,128)S(1)}, u32[]{:S(2)}, u32[]{:S(2)}) collective-permute-start(f32[4,8,128]{2,1,0:T(8,128)S(1)} %get-tuple-element.31), channel_id=1, source_target_pairs={{8,0},{16,8},{24,16},{32,24},{40,32},{48,40},{56,48},{64,56},{72,6... | collective-permute-start | bytes 49160 | tf_op jit(solution)/shard_map/ppermute | solution.py:715
  105.7 0.0 copy-done.1
  105.7 0.0 copy-done.2
  105.7 0.0 copy-start.7
  105.7 1.0 copy-done.7
  106.7 1.5 %settle.1 = (f32[7,16,8,128]{3,2,1,0:T(8,128)}, f32[12,16,8,128]{3,2,1,0:T(8,128)}, f32[7,5,8,128]{3,2,1,0:T(8,128)S(1)}) custom-call(f32[8,28,8,128]{3,2,1,0:T(8,128)S(1)} %all_to_all.11.recv, f32[6,16,8,128]{3,2,1,0:T(8,128)S(1)} %copy-done.7, f32[6,16,8,128]{3,2,1,0:T(8,128)S(1)} %get-tuple-element.27.mid, f32[6,16,8,128]{3,2,1,0:T(8,128)S(1)} %copy-done.2, ...), custom_call_target="tpu_custom_call" | custom-call | bytes 9000000 | tf_op jit(solution)/shard_map/settle/pallas_call | solution.py:699
  108.2 0.0 collective-permute-done.2.up
  108.2 3.9 %collective-permute-done.3.dn = f32[4,8,128]{2,1,0:T(8,128)S(1)} collective-permute-done((f32[4,8,128]{2,1,0:T(8,128)S(1)}, f32[4,8,128]{2,1,0:T(8,128)S(1)}, u32[]{:S(2)}, u32[]{:S(2)}) %collective-permute-start.3) | collective-permute-done | bytes 16416 | tf_op jit(solution)/shard_map/ppermute | solution.py:715
  112.2 0.7 close.1
Async XLA Ops:
  0.6 20.1 %copy-start.8 = (bf16[2,128,128]{2,1,0:T(8,128)(2,1)S(1)}, bf16[2,128,128]{2,1,0:T(8,128)(2,1)}, u32[]{:S(2)}) copy-start(bf16[2,128,128]{2,1,0:T(8,128)(2,1)} %constant.14.clone.dr_m) | copy-start | bytes 196612
  0.6 20.1 %copy-start.5 = (bf16[2,1024,128]{2,1,0:T(8,128)(2,1)S(1)}, bf16[2,1024,128]{2,1,0:T(8,128)(2,1)}, u32[]{:S(2)}) copy-start(bf16[2,1024,128]{2,1,0:T(8,128)(2,1)} %constant.15.clone.items) | copy-start | bytes 1572868
  0.7 20.1 %copy-start = (f32[7,16,8,128]{3,2,1,0:T(8,128)S(1)}, f32[7,16,8,128]{3,2,1,0:T(8,128)}, u32[]{:S(2)}) copy-start(f32[7,16,8,128]{3,2,1,0:T(8,128)} %s.3) | copy-start | bytes 1376260
  4.1 16.6 %collective-permute-start = (f32[115,8,128]{2,1,0:T(8,128)}, f32[115,8,128]{2,1,0:T(8,128)S(1)}, u32[]{:S(2)}, u32[]{:S(2)}) collective-permute-start(f32[115,8,128]{2,1,0:T(8,128)} %get-tuple-element.20), channel_id=1, source_target_pairs={{0,8},{8,16},{16,24},{24,32},{32,40},{40,48},{48,56},{56,64},{64,7... | collective-permute-start | bytes 1413128 | tf_op jit(solution)/shard_map/ppermute | solution.py:715
  9.0 11.7 %collective-permute-start.1 = (f32[76,8,128]{2,1,0:T(8,128)}, f32[76,8,128]{2,1,0:T(8,128)S(1)}, u32[]{:S(2)}, u32[]{:S(2)}) collective-permute-start(f32[76,8,128]{2,1,0:T(8,128)} %get-tuple-element.21), channel_id=1, source_target_pairs={{8,0},{16,8},{24,16},{32,24},{40,32},{48,40},{56,48},{64,56},{72,6... | collective-permute-start | bytes 933896 | tf_op jit(solution)/shard_map/ppermute | solution.py:715
  20.8 0.9 copy-start.3
  21.6 1.0 copy-start.6
  22.6 0.9 copy-start.9
  68.8 26.2 %copy-start.4 = (f32[17,8,128]{2,1,0:T(8,128)S(1)}, f32[17,8,128]{2,1,0:T(8,128)}, u32[]{:S(2)}) copy-start(f32[17,8,128]{2,1,0:T(8,128)} %get-tuple-element.22.coef) | copy-start | bytes 208900
  95.0 10.7 %copy-start.1 = (f32[12,16,8,128]{3,2,1,0:T(8,128)S(1)}, f32[12,16,8,128]{3,2,1,0:T(8,128)}, u32[]{:S(2)}) copy-start(f32[12,16,8,128]{3,2,1,0:T(8,128)} %psi.1) | copy-start | bytes 2359300
  95.0 10.7 %copy-start.2 = (f32[6,16,8,128]{3,2,1,0:T(8,128)S(1)}, f32[6,16,8,128]{3,2,1,0:T(8,128)}, u32[]{:S(2)}) copy-start(f32[6,16,8,128]{3,2,1,0:T(8,128)} %v.1) | copy-start | bytes 1179652
  97.8 10.4 %collective-permute-start.2 = (f32[4,8,128]{2,1,0:T(8,128)S(1)}, f32[4,8,128]{2,1,0:T(8,128)S(1)}, u32[]{:S(2)}, u32[]{:S(2)}) collective-permute-start(f32[4,8,128]{2,1,0:T(8,128)S(1)} %get-tuple-element.30), channel_id=1, source_target_pairs={{0,8},{8,16},{16,24},{24,32},{32,40},{40,48},{48,56},{56,64},{64,7... | collective-permute-start | bytes 49160 | tf_op jit(solution)/shard_map/ppermute | solution.py:715
  103.8 8.4 %collective-permute-start.3 = (f32[4,8,128]{2,1,0:T(8,128)S(1)}, f32[4,8,128]{2,1,0:T(8,128)S(1)}, u32[]{:S(2)}, u32[]{:S(2)}) collective-permute-start(f32[4,8,128]{2,1,0:T(8,128)S(1)} %get-tuple-element.31), channel_id=1, source_target_pairs={{8,0},{16,8},{24,16},{32,24},{40,32},{48,40},{56,48},{64,56},{72,6... | collective-permute-start | bytes 49160 | tf_op jit(solution)/shard_map/ppermute | solution.py:715
  105.7 1.0 copy-start.7

commit v3 on v2

--- a/solution.py
+++ b/solution.py
@@ -28,6 +28,7 @@
 SHARED = ("cv", "cf", "cr", "bulk", "couple", "modulus", "shear")
 OWN = SHARED + ("fric", "kappa", "omega", "decay0", "decay1", "decay2", "decay3")
 FLAGS = len(OWN)
+COEF = 9 * PLANES
 RING = SHARED + ("fk",)
 
 
@@ -243,7 +244,7 @@
 
 def prepare(
     lids_hbm, mat_hbm, jkd_hbm, src_hbm, psi_hbm, v_hbm, s_hbm,
-    vw, t_out, up, dn, coef, ring_coef,
+    state, up, dn, ring_coef,
     lids, mat, jkd, src, psi, v, s, sems,
 ):
     pairs = (
@@ -259,11 +260,11 @@
     c = coefficients(own_ids(lids), (mat, jkd))
     mine = (rows >= 2) & (rows < 6)
     for n, name in enumerate(OWN):
-        coef[n] = jnp.where(mine, c[name], 0.0)
+        state[COEF + n] = jnp.where(mine, c[name], 0.0)
     source = (src[0] - PLANES * device).astype(F32)
-    coef[FLAGS] = jnp.full((8, NR), jnp.where(device > 0, 1.0, 0.0), F32)
-    coef[FLAGS + 1] = jnp.full((8, NR), jnp.where(device < lax.axis_size("depth") - 1, 1.0, 0.0), F32)
-    coef[FLAGS + 2] = jnp.full((8, NR), source, F32)
+    state[COEF + FLAGS] = jnp.full((8, NR), jnp.where(device > 0, 1.0, 0.0), F32)
+    state[COEF + FLAGS + 1] = jnp.full((8, NR), jnp.where(device < lax.axis_size("depth") - 1, 1.0, 0.0), F32)
+    state[COEF + FLAGS + 2] = jnp.full((8, NR), source, F32)
     for n, name in enumerate(SHARED):
         swapped = pltpu.roll(c[name], 4, 0)
         up[108 + n] = jnp.where(rows < 2, swapped, 0.0)
@@ -290,11 +291,11 @@
     for i in range(3):
         memory = [psi[3 * l + i] for l in range(4)]
         total = sum(w * m for w, m in zip(weights, memory))
-        t_out[i] = sum(w * (m - v[3 + i]) for w, m in zip(decayed, memory))
+        state[96 + 16 * i : 112 + 16 * i] = sum(w * (m - v[3 + i]) for w, m in zip(decayed, memory))
         vi = v[i] + cf * total
         wi = v[3 + i] - cr * total
         for f, x in ((i, vi), (3 + i, wi)):
-            vw[f] = x
+            state[16 * f : 16 * f + 16] = x
             up[56 + 8 * f : 64 + 8 * f] = x[8:]
             dn[35 + 5 * f : 40 + 5 * f] = x[:5]
     for f in range(7):
@@ -306,6 +307,23 @@
         dn[65 + i] = combine(ROW[0], nodes)
 
 
+def stage(*refs):
+    *pairs, sems = refs
+    count = 6
+    first_r = jnp.where(lax.axis_index("az") == 0, 1, 0)
+    first_z = jnp.where(lax.axis_index("depth") == 0, 1, 0)
+    sources = list(pairs[:count])
+    sources[0] = sources[0].at[first_r]
+    sources[1] = sources[1].at[first_z]
+    state = sources.pop()
+    sources += [state.at[0:96], state.at[96:COEF], state.at[COEF:]]
+    copies = [pltpu.make_async_copy(a, b, sems.at[i]) for i, (a, b) in enumerate(zip(sources, pairs[count:]))]
+    for copy in copies:
+        copy.start()
+    for copy in copies:
+        copy.wait()
+
+
 def launch(s, vw, t_in, up, dn, coef, dr_m, items, pk, keep):
     has_below = coef[FLAGS]
     has_above = coef[FLAGS + 1]
@@ -325,7 +343,7 @@
 
     def ext_v(f):
         return jnp.concatenate(
-            [up[56 + 8 * f : 64 + 8 * f], vw[f], dn[35 + 5 * f : 40 + 5 * f]], axis=0
+            [up[56 + 8 * f : 64 + 8 * f], vw[16 * f : 16 * f + 16], dn[35 + 5 * f : 40 + 5 * f]], axis=0
         )
 
     above29 = lax.broadcasted_iota(jnp.int32, (29, 8, NR), 0) < 24
@@ -365,7 +383,7 @@
     kappa = spread_rows(c["kappa"], 2, 4)
     grads = (r_p, None, z_p)
     for i, d in enumerate((d_r, d_t, d_z)):
-        g = fric * (t_in[i] + kappa * w1[i][8:24])
+        g = fric * (t_in[16 * i : 16 * i + 16] + kappa * w1[i][8:24])
         if grads[i] is not None:
             g = g + grads[i][8:24]
         a = cv[8:24] * d[8:24] + cf[8:24] * g
@@ -449,22 +467,10 @@
     pack(17, jnp.concatenate([radius_items(second), depth_items([x2.get(n) for n in names_z], 0)], axis=0))
 
 
-def ring(
-    recv, coef, dt_hbm, mr_hbm, mz_hbm, wr_hbm, wz_hbm, out, dt_m, mr, mz, wr, wz, sems
-):
+def ring(recv, coef, mr, mz, dt_m, wr, wz, out):
     group = lax.axis_index("az")
-    first_r = jnp.where(group == 0, 1, 0)
-    first_z = jnp.where(lax.axis_index("depth") == 0, 1, 0)
-    sources = (dt_hbm, wr_hbm, wz_hbm, mr_hbm.at[first_r], mz_hbm.at[first_z])
-    copies = [
-        pltpu.make_async_copy(a, b, sems.at[i]) for i, (a, b) in enumerate(zip(sources, (dt_m, wr, wz, mr, mz)))
-    ]
-    for copy in copies:
-        copy.start()
     c = {name: coef[n] for n, name in enumerate(RING)}
     q = inverse_radius(group, GROUP)
-    for copy in copies:
-        copy.wait()
 
     def field(f):
         return jnp.concatenate([recv[:, 2 * f], recv[:, 2 * f + 1]], axis=-1)
@@ -584,7 +590,7 @@
     return jnp.stack(planes)
 
 
-def advance(recv, keep, coef, v_out, mid, up, dn):
+def advance(recv, keep, coef, new, mid, up, dn):
     c = {name: coef[n] for n, name in enumerate(OWN)}
     q = inverse_radius(0, NR)
     cv, cf, cr = [spread_rows(c[n], 2, 4) for n in ("cv", "cf", "cr")]
@@ -597,8 +603,8 @@
         w1 = keep[3 + i] + dw[i]
         v2 = v1 + keep[6 + i] + cv * d + cf * g
         w2 = w1 - keep[9 + i] - cf * d - cr * g
-        v_out[i] = v2
-        v_out[3 + i] = w2
+        new[i] = v2
+        new[3 + i] = w2
         mid[i] = v1
         mid[3 + i] = w1
         x = v1 + v2
@@ -610,7 +616,8 @@
             dn[3] = x[0]
 
 
-def settle(recv, v2, mid, v, s, psi, coef, dr_m, s_out, m_out, edge):
+def settle(recv, v2, mid, v, s, psi, coef, dr_m, v_out, s_out, m_out, edge):
+    v_out[...] = v2[...]
     has_below = coef[FLAGS]
     c = {name: coef[n] for n, name in enumerate(OWN)}
     q = inverse_radius(0, NR)
@@ -692,13 +699,13 @@
         copy.wait()
 
 
-def call(body, inputs, shapes, hbm=(), scratch=(), out_hbm=False, alias=None, micros=1, vmem=VMEM_LIMIT):
+def call(body, inputs, shapes, types=None, hbm=(), scratch=(), out_hbm=False, alias=None, micros=1, vmem=VMEM_LIMIT):
     def space(i):
         return pltpu.HBM if i in hbm else pltpu.VMEM
 
     return pl.pallas_call(
         body,
-        out_shape=[jax.ShapeDtypeStruct(x, F32) for x in shapes],
+        out_shape=[jax.ShapeDtypeStruct(x, t) for x, t in zip(shapes, types or [F32] * len(shapes))],
         in_specs=[pl.BlockSpec(memory_space=space(i)) for i in range(len(inputs))],
         out_specs=[pl.BlockSpec(memory_space=pltpu.HBM if out_hbm else pltpu.VMEM) for _ in shapes],
         scratch_shapes=list(scratch),
@@ -719,10 +726,10 @@
     c = constants()
     block = (PLANES, AZ, NR)
     tables = [layer_ids, materials, jkd, source_depth]
-    vw, t_part, up, dn, coef, ring_coef = call(
+    state, up, dn, ring_coef = call(
         prepare,
         tables + [memory, velocity, stress],
-        [(6,) + block, (3,) + block, (115, AZ, NR), (76, AZ, NR), (FLAGS + 3, 8, NR), (len(RING) + 1, 8, 256)],
+        [(COEF + FLAGS + 3, AZ, NR), (115, AZ, NR), (76, AZ, NR), (len(RING) + 1, 8, 256)],
         hbm=range(7),
         scratch=[pltpu.SMEM(x.shape, x.dtype) for x in tables]
         + [pltpu.VMEM((n,) + block, F32) for n in (12, 6, 7)]
@@ -730,6 +737,16 @@
         vmem=VMEM_FULL,
     )
     up, dn = shift(up, 1), shift(dn, -1)
+    staged = [c[n] for n in ("mr", "mz", "dt", "wr", "wz")]
+    shapes = [x.shape[1:] if n < 2 else x.shape for n, x in enumerate(staged)]
+    *matrices, vw, t_part, coef = call(
+        stage,
+        staged + [state],
+        shapes + [(96, AZ, NR), (48, AZ, NR), (FLAGS + 3, AZ, NR)],
+        types=[BF16] * 5 + [F32] * 3,
+        hbm=range(6),
+        scratch=[pltpu.SemaphoreType.DMA((8,))],
+    )
     packed, keep = call(
         launch,
         [stress, vw, t_part, up, dn, coef, c["dr"], c["items"]],
@@ -737,28 +754,18 @@
         micros=4,
     )
     packed = lax.all_to_all(packed, "az", split_axis=0, concat_axis=0, tiled=True)
-    matrices = [c[n] for n in ("dt", "mr", "mz", "wr", "wz")]
-    shapes = [m.shape[1:] if n in (1, 2) else m.shape for n, m in enumerate(matrices)]
-    (back,) = call(
-        ring,
-        [packed, ring_coef] + matrices,
-        [(8, 2 * FIELDS_OUT, AZ, NR)],
-        hbm=range(2, 7),
-        scratch=[pltpu.VMEM(x, BF16) for x in shapes] + [pltpu.SemaphoreType.DMA((5,))],
-        micros=3,
-        vmem=VMEM_FULL,
-    )
+    (back,) = call(ring, [packed, ring_coef] + matrices, [(8, 2 * FIELDS_OUT, AZ, NR)], micros=3)
     back = lax.all_to_all(back, "az", split_axis=0, concat_axis=0, tiled=True)
-    v_out, mid, up, dn = call(
+    new, mid, up, dn = call(
         advance,
         [back, keep, coef],
         [(6,) + block, (6,) + block, (4, AZ, NR), (4, AZ, NR)],
     )
     up, dn = shift(up, 1), shift(dn, -1)
-    s_part, m_out, edge = call(
+    v_out, s_part, m_out, edge = call(
         settle,
-        [back, v_out, mid, velocity, stress, memory, coef, c["dr"]],
-        [(7,) + block, (12,) + block, (7, 5, AZ, NR)],
+        [back, new, mid, velocity, stress, memory, coef, c["dr"]],
+        [(6,) + block, (7,) + block, (12,) + block, (7, 5, AZ, NR)],
         micros=3,
     )
     (s_out,) = call(

time: 113 us -> 106 us (0.938)
  Pallas kernels: 16.1 us -> 12.8 us
  waiting for transfers between devices: 13.8 us -> 11.8 us
  local copies, waits for them, and re-layouts: 3.82 us -> 2.04 us
    pallas_call x6 -> x7, Pallas kernels: 16.1 us -> 12.8 us  [call(): pl.pallas_call(body, out_shape=[jax.ShapeDtypeStruct(x, t) for x, t in zi...]
    ppermute x4, waiting for transfers between devices: 13.8 us -> 11.8 us  [shift(): lax.ppermute(value, 'depth', [(i, i + steps) for i in range(first, last)])]
    unnamed x20 -> x24, local copies, waits for them, and re-layouts: 3.82 us -> 2.04 us
  transfers between devices with their start and end apart: 4 -> 4, of which waited for: 2 -> 2; matrix products, arithmetic and copies ran while one was open for 0% -> 0% of each run, Pallas kernels for 1% -> 2%
where the time goes in v3:
time: 106 us; the launch traced here: 105 us
  blocking collectives  62.7 us (59%)
  starting transfers between devices  14.4 us (14%)
  Pallas kernels  12.8 us (12%)
  waiting for transfers between devices  11.8 us (11%)
  local copies, waits for them, and re-layouts  2.04 us (2%)
  between operations  1.57 us (1%)
    all_to_all x1, blocking collectives, on_device(): lax.all_to_all(packed, 'az', split_axis=0, concat_axis=0, tiled=True)  36.8 us
    all_to_all x1, blocking collectives, on_device(): back = lax.all_to_all(back, 'az', split_axis=0, concat_axis=0, tiled=True)  25.8 us
    ppermute x4, starting transfers between devices, shift(): lax.ppermute(value, 'depth', [(i, i + steps) for i in range(first, last)])  14.4 us
    pallas_call x7, Pallas kernels, call(): pl.pallas_call(body, out_shape=[jax.ShapeDtypeStruct(x, t) for x, t in zi...  12.8 us
    ppermute x4, waiting for transfers between devices, shift(): lax.ppermute(value, 'depth', [(i, i + steps) for i in range(first, last)])  11.8 us
  transfers between devices with their start and end apart: 4, of which 2 were waited for; matrix products, arithmetic and copies ran while one was open for 0% of the time, Pallas kernels for 2%

profile of v3, /device:TPU:31, one launch (start us, length us, event | category | flops | bytes accessed | tf_op | source)
XLA Modules:
  0.0 105.2 jit_solution(1973987372416871594)
XLA Ops:
  0.6 0.0 copy-start.5
  0.6 0.0 copy-start.6
  0.7 0.0 copy-start.11
  0.7 0.0 copy-start.7
  1.4 2.6 %prepare.1 = (f32[161,8,128]{2,1,0:T(8,128)}, f32[115,8,128]{2,1,0:T(8,128)}, f32[76,8,128]{2,1,0:T(8,128)}, f32[9,8,256]{2,1,0:T(8,128)}) custom-call(s32[4,32]{1,0:T(4,128)} %lids_hbm.1, f32[8,8]{1,0:T(8,128)} %mat_hbm.1, f32[8,9]{1,0:T(8,128)} %jkd_hbm.1, s32[1]{0:T(128)S(6)} %copy.19.src_hbm, f32[12,16,8,128]{3,2,1,0:T(8,128)} %psi.1, ...), custom_call_target="tpu_custom_call" | custom-call | bytes 3000000 | tf_op jit(solution)/shard_map/prepare/pallas_call | solution.py:706
  4.1 4.9 %collective-permute-start = (f32[115,8,128]{2,1,0:T(8,128)}, f32[115,8,128]{2,1,0:T(8,128)S(1)}, u32[]{:S(2)}, u32[]{:S(2)}) collective-permute-start(f32[115,8,128]{2,1,0:T(8,128)} %get-tuple-element.28), channel_id=1, source_target_pairs={{0,8},{8,16},{16,24},{24,32},{32,40},{40,48},{48,56},{56,64},{64,7... | collective-permute-start | bytes 1413128 | tf_op jit(solution)/shard_map/ppermute | solution.py:722
  9.0 1.9 %collective-permute-start.1 = (f32[76,8,128]{2,1,0:T(8,128)}, f32[76,8,128]{2,1,0:T(8,128)S(1)}, u32[]{:S(2)}, u32[]{:S(2)}) collective-permute-start(f32[76,8,128]{2,1,0:T(8,128)} %get-tuple-element.29), channel_id=1, source_target_pairs={{8,0},{16,8},{24,16},{32,24},{40,32},{48,40},{56,48},{64,56},{72,6... | collective-permute-start | bytes 933896 | tf_op jit(solution)/shard_map/ppermute | solution.py:722
  10.9 0.0 copy-done.5
  10.9 0.0 copy-done.6
  10.9 0.0 copy-done.11
  10.9 0.0 copy-done.7
  10.9 0.0 copy-start.3
  10.9 1.1 %copy-done.3 = f32[161,8,128]{2,1,0:T(8,128)S(1)} copy-done((f32[161,8,128]{2,1,0:T(8,128)S(1)}, f32[161,8,128]{2,1,0:T(8,128)}, u32[]{:S(2)}) %copy-start.3) | copy-done | bytes 659480
  12.0 0.0 copy-start.9
  12.0 0.9 copy-done.9
  12.9 0.0 copy-start
  12.9 0.0 copy-start.4
  12.9 0.0 copy-start.8
  12.9 0.8 stage.1
  13.8 6.9 %collective-permute-done.1.dn = f32[76,8,128]{2,1,0:T(8,128)S(1)} collective-permute-done((f32[76,8,128]{2,1,0:T(8,128)}, f32[76,8,128]{2,1,0:T(8,128)S(1)}, u32[]{:S(2)}, u32[]{:S(2)}) %collective-permute-start.1) | collective-permute-done | bytes 311328 | tf_op jit(solution)/shard_map/ppermute | solution.py:722
  20.7 0.0 collective-permute-done.up
  20.7 0.0 copy-done
  20.7 0.0 copy-done.4
  20.7 0.0 copy-done.8
  20.7 2.6 %launch.1 = (f32[8,36,8,128]{3,2,1,0:T(8,128)S(1)}, f32[12,16,8,128]{3,2,1,0:T(8,128)S(1)}) custom-call(f32[7,16,8,128]{3,2,1,0:T(8,128)S(1)} %copy-done, f32[96,8,128]{2,1,0:T(8,128)S(1)} %get-tuple-element.26.vw, f32[48,8,128]{2,1,0:T(8,128)S(1)} %get-tuple-element.27.t_in, f32[115,8,128]{2,1,0:T(8,128)S(1)} %collective-permute-done.up, ...), custom_call_target="tpu_custom_call" | custom-call | bytes 12000000 | tf_op jit(solution)/shard_map/launch/pallas_call | solution.py:706
  23.3 0.0 copy-start.10
  23.3 36.8 %all_to_all.10.recv = f32[8,36,8,128]{3,2,1,0:T(8,128)S(1)} all-to-all(f32[8,36,8,128]{3,2,1,0:T(8,128)S(1)} %get-tuple-element.31), channel_id=1, replica_groups=mesh['depth'=64,'az'=8] {'az'}, dimensions={0} | all-to-all | bytes 2359296 | tf_op jit(solution)/shard_map/all_to_all | solution.py:756
  60.1 0.0 copy-done.10
  60.1 2.4 %ring.1 = f32[8,28,8,128]{3,2,1,0:T(8,128)S(1)} custom-call(f32[8,36,8,128]{3,2,1,0:T(8,128)S(1)} %all_to_all.10.recv, f32[9,8,256]{2,1,0:T(8,128)S(1)} %copy-done.10, bf16[2,128,128]{2,1,0:T(8,128)(2,1)S(1)} %get-tuple-element.33.mr, bf16[2,256,256]{2,1,0:T(8,128)(2,1)S(1)} %get-tuple-element.34.mz, bf16[2,64,64]{2,1,0:T(8,128)(2,1)S(1)} %get-tuple-element.35.dt_m, ...), custom_call_target="tpu_custom_call" | custom-call | bytes 9000000 | tf_op jit(solution)/shard_map/ring/pallas_call | solution.py:706
  62.6 25.8 %all_to_all.11.recv = f32[8,28,8,128]{3,2,1,0:T(8,128)S(1)} all-to-all(f32[8,28,8,128]{3,2,1,0:T(8,128)S(1)} %ring.1), channel_id=1, replica_groups=mesh['depth'=64,'az'=8] {'az'}, dimensions={0} | all-to-all | bytes 1835008 | tf_op jit(solution)/shard_map/all_to_all | solution.py:758
  88.4 0.0 copy-start.1
  88.4 0.0 copy-start.2
  88.4 2.1 %advance.1 = (f32[6,16,8,128]{3,2,1,0:T(8,128)S(1)}, f32[6,16,8,128]{3,2,1,0:T(8,128)S(1)}, f32[4,8,128]{2,1,0:T(8,128)S(1)}, f32[4,8,128]{2,1,0:T(8,128)S(1)}) custom-call(f32[8,28,8,128]{3,2,1,0:T(8,128)S(1)} %all_to_all.11.recv, f32[12,16,8,128]{3,2,1,0:T(8,128)S(1)} %get-tuple-element.38.keep, f32[17,8,128]{2,1,0:T(8,128)S(1)} %get-tuple-element.30.coef), custom_call_target="tpu_custom_call" | custom-call | bytes 3000000 | tf_op jit(solution)/shard_map/advance/pallas_call | solution.py:706
  90.5 5.6 %collective-permute-start.2 = (f32[4,8,128]{2,1,0:T(8,128)S(1)}, f32[4,8,128]{2,1,0:T(8,128)S(1)}, u32[]{:S(2)}, u32[]{:S(2)}) collective-permute-start(f32[4,8,128]{2,1,0:T(8,128)S(1)} %get-tuple-element.44), channel_id=1, source_target_pairs={{0,8},{8,16},{16,24},{24,32},{32,40},{40,48},{48,56},{56,64},{64,7... | collective-permute-start | bytes 49160 | tf_op jit(solution)/shard_map/ppermute | solution.py:722
  96.1 1.9 %collective-permute-start.3 = (f32[4,8,128]{2,1,0:T(8,128)S(1)}, f32[4,8,128]{2,1,0:T(8,128)S(1)}, u32[]{:S(2)}, u32[]{:S(2)}) collective-permute-start(f32[4,8,128]{2,1,0:T(8,128)S(1)} %get-tuple-element.45), channel_id=1, source_target_pairs={{8,0},{16,8},{24,16},{32,24},{40,32},{48,40},{56,48},{64,56},{72,6... | collective-permute-start | bytes 49160 | tf_op jit(solution)/shard_map/ppermute | solution.py:722
  98.1 0.0 copy-done.1
  98.1 0.0 copy-done.2
  98.1 1.6 %settle.1 = (f32[6,16,8,128]{3,2,1,0:T(8,128)}, f32[7,16,8,128]{3,2,1,0:T(8,128)}, f32[12,16,8,128]{3,2,1,0:T(8,128)}, f32[7,5,8,128]{3,2,1,0:T(8,128)S(1)}) custom-call(f32[8,28,8,128]{3,2,1,0:T(8,128)S(1)} %all_to_all.11.recv, f32[6,16,8,128]{3,2,1,0:T(8,128)S(1)} %get-tuple-element.39.v2, f32[6,16,8,128]{3,2,1,0:T(8,128)S(1)} %get-tuple-element.40.mid, ...), custom_call_target="tpu_custom_call" | custom-call | bytes 9000000 | tf_op jit(solution)/shard_map/settle/pallas_call | solution.py:706
  99.7 0.0 collective-permute-done.2.up
  99.7 4.8 %collective-permute-done.3.dn = f32[4,8,128]{2,1,0:T(8,128)S(1)} collective-permute-done((f32[4,8,128]{2,1,0:T(8,128)S(1)}, f32[4,8,128]{2,1,0:T(8,128)S(1)}, u32[]{:S(2)}, u32[]{:S(2)}) %collective-permute-start.3) | collective-permute-done | bytes 16416 | tf_op jit(solution)/shard_map/ppermute | solution.py:722
  104.5 0.7 close.1
Async XLA Ops:
  0.6 10.3 %copy-start.5 = (bf16[2,128,1024]{2,1,0:T(8,128)(2,1)S(1)}, bf16[2,128,1024]{2,1,0:T(8,128)(2,1)}, u32[]{:S(2)}) copy-start(bf16[2,128,1024]{2,1,0:T(8,128)(2,1)} %constant.18.clone.refs_4_) | copy-start | bytes 1572868
  0.6 10.3 %copy-start.6 = (bf16[2,2,128,512]{3,2,1,0:T(8,128)(2,1)S(1)}, bf16[2,2,128,512]{3,2,1,0:T(8,128)(2,1)}, u32[]{:S(2)}) copy-start(bf16[2,2,128,512]{3,2,1,0:T(8,128)(2,1)} %constant.17.clone.refs_3_) | copy-start | bytes 1572868
  0.7 10.3 %copy-start.11 = (bf16[2,64,64]{2,1,0:T(8,128)(2,1)S(1)}, bf16[2,64,64]{2,1,0:T(8,128)(2,1)}, u32[]{:S(2)}) copy-start(bf16[2,64,64]{2,1,0:T(8,128)(2,1)} %constant.16.clone.refs_2_) | copy-start | bytes 49156
  0.7 10.3 %copy-start.7 = (bf16[2,2,256,256]{3,2,1,0:T(8,128)(2,1)S(1)}, bf16[2,2,256,256]{3,2,1,0:T(8,128)(2,1)}, u32[]{:S(2)}) copy-start(bf16[2,2,256,256]{3,2,1,0:T(8,128)(2,1)} %constant.15.clone.refs_1_) | copy-start | bytes 1572868
  4.1 16.6 %collective-permute-start = (f32[115,8,128]{2,1,0:T(8,128)}, f32[115,8,128]{2,1,0:T(8,128)S(1)}, u32[]{:S(2)}, u32[]{:S(2)}) collective-permute-start(f32[115,8,128]{2,1,0:T(8,128)} %get-tuple-element.28), channel_id=1, source_target_pairs={{0,8},{8,16},{16,24},{24,32},{32,40},{40,48},{48,56},{56,64},{64,7... | collective-permute-start | bytes 1413128 | tf_op jit(solution)/shard_map/ppermute | solution.py:722
  9.0 11.7 %collective-permute-start.1 = (f32[76,8,128]{2,1,0:T(8,128)}, f32[76,8,128]{2,1,0:T(8,128)S(1)}, u32[]{:S(2)}, u32[]{:S(2)}) collective-permute-start(f32[76,8,128]{2,1,0:T(8,128)} %get-tuple-element.29), channel_id=1, source_target_pairs={{8,0},{16,8},{24,16},{32,24},{40,32},{48,40},{56,48},{64,56},{72,6... | collective-permute-start | bytes 933896 | tf_op jit(solution)/shard_map/ppermute | solution.py:722
  10.9 1.1 %copy-start.3 = (f32[161,8,128]{2,1,0:T(8,128)S(1)}, f32[161,8,128]{2,1,0:T(8,128)}, u32[]{:S(2)}) copy-start(f32[161,8,128]{2,1,0:T(8,128)} %get-tuple-element.25.refs_5_) | copy-start | bytes 1978372
  12.0 0.9 copy-start.9
  12.9 7.8 %copy-start = (f32[7,16,8,128]{3,2,1,0:T(8,128)S(1)}, f32[7,16,8,128]{3,2,1,0:T(8,128)}, u32[]{:S(2)}) copy-start(f32[7,16,8,128]{3,2,1,0:T(8,128)} %s.3) | copy-start | bytes 1376260
  12.9 7.8 %copy-start.4 = (bf16[2,1024,128]{2,1,0:T(8,128)(2,1)S(1)}, bf16[2,1024,128]{2,1,0:T(8,128)(2,1)}, u32[]{:S(2)}) copy-start(bf16[2,1024,128]{2,1,0:T(8,128)(2,1)} %constant.20.clone.items) | copy-start | bytes 1572868
  12.9 7.8 %copy-start.8 = (bf16[2,128,128]{2,1,0:T(8,128)(2,1)S(1)}, bf16[2,128,128]{2,1,0:T(8,128)(2,1)}, u32[]{:S(2)}) copy-start(bf16[2,128,128]{2,1,0:T(8,128)(2,1)} %constant.19.clone.dr_m) | copy-start | bytes 196612
  23.3 36.8 %copy-start.10 = (f32[9,8,256]{2,1,0:T(8,128)S(1)}, f32[9,8,256]{2,1,0:T(8,128)}, u32[]{:S(2)}) copy-start(f32[9,8,256]{2,1,0:T(8,128)} %get-tuple-element.32.coef) | copy-start | bytes 221188
  88.4 9.7 %copy-start.1 = (f32[12,16,8,128]{3,2,1,0:T(8,128)S(1)}, f32[12,16,8,128]{3,2,1,0:T(8,128)}, u32[]{:S(2)}) copy-start(f32[12,16,8,128]{3,2,1,0:T(8,128)} %psi.1) | copy-start | bytes 2359300
  88.4 9.7 %copy-start.2 = (f32[6,16,8,128]{3,2,1,0:T(8,128)S(1)}, f32[6,16,8,128]{3,2,1,0:T(8,128)}, u32[]{:S(2)}) copy-start(f32[6,16,8,128]{3,2,1,0:T(8,128)} %v.1) | copy-start | bytes 1179652
  90.5 9.2 %collective-permute-start.2 = (f32[4,8,128]{2,1,0:T(8,128)S(1)}, f32[4,8,128]{2,1,0:T(8,128)S(1)}, u32[]{:S(2)}, u32[]{:S(2)}) collective-permute-start(f32[4,8,128]{2,1,0:T(8,128)S(1)} %get-tuple-element.44), channel_id=1, source_target_pairs={{0,8},{8,16},{16,24},{24,32},{32,40},{40,48},{48,56},{56,64},{64,7... | collective-permute-start | bytes 49160 | tf_op jit(solution)/shard_map/ppermute | solution.py:722
  96.1 8.4 %collective-permute-start.3 = (f32[4,8,128]{2,1,0:T(8,128)S(1)}, f32[4,8,128]{2,1,0:T(8,128)S(1)}, u32[]{:S(2)}, u32[]{:S(2)}) collective-permute-start(f32[4,8,128]{2,1,0:T(8,128)S(1)} %get-tuple-element.45), channel_id=1, source_target_pairs={{8,0},{16,8},{24,16},{32,24},{40,32},{48,40},{56,48},{64,56},{72,6... | collective-permute-start | bytes 49160 | tf_op jit(solution)/shard_map/ppermute | solution.py:722

commit v4 on v3

--- a/solution.py
+++ b/solution.py
@@ -25,10 +25,12 @@
 FIELDS_OUT = 14
 VMEM_LIMIT = 32 * 2**20
 VMEM_FULL = 56 * 2**20
+UP_COEF = 52
+DN_COEF = 20
 SHARED = ("cv", "cf", "cr", "bulk", "couple", "modulus", "shear")
 OWN = SHARED + ("fric", "kappa", "omega", "decay0", "decay1", "decay2", "decay3")
 FLAGS = len(OWN)
-COEF = 9 * PLANES
+COEF = 12 * PLANES
 RING = SHARED + ("fk",)
 
 
@@ -243,12 +245,13 @@
 
 
 def prepare(
-    lids_hbm, mat_hbm, jkd_hbm, src_hbm, psi_hbm, v_hbm, s_hbm,
+    lids_hbm, mat_hbm, jkd_hbm, src_hbm, s_hbm, psi_hbm, v_hbm, dr_hbm,
     state, up, dn, ring_coef,
-    lids, mat, jkd, src, psi, v, s, sems,
+    lids, mat, jkd, src, s, psi, v, dr_m, sems,
 ):
     pairs = (
-        (lids_hbm, lids), (mat_hbm, mat), (jkd_hbm, jkd), (src_hbm, src), (psi_hbm, psi), (v_hbm, v), (s_hbm, s)
+        (lids_hbm, lids), (mat_hbm, mat), (jkd_hbm, jkd), (src_hbm, src), (s_hbm, s), (psi_hbm, psi),
+        (v_hbm, v), (dr_hbm, dr_m),
     )
     copies = [pltpu.make_async_copy(a, b, sems.at[i]) for i, (a, b) in enumerate(pairs)]
     for copy in copies:
@@ -267,8 +270,8 @@
     state[COEF + FLAGS + 2] = jnp.full((8, NR), source, F32)
     for n, name in enumerate(SHARED):
         swapped = pltpu.roll(c[name], 4, 0)
-        up[108 + n] = jnp.where(rows < 2, swapped, 0.0)
-        dn[69 + n] = jnp.where(rows >= 6, swapped, 0.0)
+        up[UP_COEF + n] = jnp.where(rows < 2, swapped, 0.0)
+        dn[DN_COEF + n] = jnp.where(rows >= 6, swapped, 0.0)
     element = lax.broadcasted_iota(jnp.int32, (8, 256), 1) // 64
     group = lax.axis_index("az")
     ids = jnp.zeros((8, 256), jnp.int32)
@@ -282,29 +285,57 @@
     def sp(value):
         return spread_rows(value, 2, 4)
 
+    has_below = jnp.where(device > 0, 1.0, 0.0)
+    q = inverse_radius(0, NR)
+    cv, cf, cr, fric = [sp(c[n]) for n in ("cv", "cf", "cr", "fric")]
     weights = [sp(w) for w in c["weights"]]
-    cf = sp(c["cf"] * c["fric"])
-    cr = sp(c["cr"] * c["fric"])
     decayed = [sp(w * d) for w, d in zip(c["weights"], c["decay"])]
     for copy in copies[4:]:
         copy.wait()
+    rr, tt, zz, rt, rz, tz, p = [s[f] for f in range(7)]
+    stacked = jnp.concatenate([flat(x) for x in (rr, rt, rz, p)], axis=0)
+    y = mm(stacked, dr_m[0], dr_m[1])
+    r_rr, r_rt, r_rz, r_p = [y[128 * i : 128 * i + 128].reshape(16, 8, NR) for i in range(4)]
+    zero = jnp.zeros((1, 8, NR), F32)
+    z_rz, z_tz, z_zz, z_p = [
+        depth_derivative(jnp.concatenate([x, zero], axis=0), 0, 4, 0, has_below, float(ROW[4, 4]) * x[0], zero[0])[:16]
+        for x in (rz, tz, zz, p)
+    ]
+    div = [r_rr + z_rz + q * (rr - tt), r_rt + z_tz + 2.0 * q * rt, r_rz + z_zz + q * rz]
+    grads = (r_p, None, z_p)
+    new = []
     for i in range(3):
         memory = [psi[3 * l + i] for l in range(4)]
         total = sum(w * m for w, m in zip(weights, memory))
-        state[96 + 16 * i : 112 + 16 * i] = sum(w * (m - v[3 + i]) for w, m in zip(decayed, memory))
-        vi = v[i] + cf * total
-        wi = v[3 + i] - cr * total
-        for f, x in ((i, vi), (3 + i, wi)):
-            state[16 * f : 16 * f + 16] = x
-            up[56 + 8 * f : 64 + 8 * f] = x[8:]
-            dn[35 + 5 * f : 40 + 5 * f] = x[:5]
-    for f in range(7):
-        up[8 * f : 8 * f + 8] = s[f, 8:]
-        dn[5 * f : 5 * f + 5] = s[f, :5]
-    for i, f in enumerate((4, 5, 2, 6)):
-        nodes = [s[f, 4 + l] for l in range(5)]
-        up[104 + i] = combine(ROW[4], nodes)
-        dn[65 + i] = combine(ROW[0], nodes)
+        later = sum(w * (m - v[3 + i]) for w, m in zip(decayed, memory))
+        g0, g1 = fric * total, fric * later
+        if grads[i] is not None:
+            g0, g1 = g0 + grads[i], g1 + grads[i]
+        d_v, d_w = cv * div[i], cf * div[i]
+        for n, x in enumerate(
+            (v[i] + d_v + cf * g0, v[3 + i] - d_w - cr * g0, d_v + cf * g1, d_w + cr * g1)
+        ):
+            at = 16 * (3 * n + i)
+            state[at : at + 16] = x
+            if n < 2:
+                f = 3 * n + i
+                up[4 * f : 4 * f + 4] = x[12:]
+                dn[f] = x[0]
+                if f < 3 or f == 5:
+                    place = min(f, 3)
+                    up[40 + place] = below_partial(x[8:12])
+                    dn[12 + place] = combine(ROW[0, 1:], [x[1 + l] for l in range(4)])
+    q_rt, q_tt, q_tz, q_p = q * rt, q * tt, q * tz, q * p
+    u = [cv * q_rt, cv * q_tt + cf * q_p, cv * q_tz, -(cf * q_tz)]
+    for i, x in enumerate(u):
+        up[44 + i] = below_partial(x[8:12])
+        dn[16 + i] = combine(ROW[0, 1:], [x[1 + l] for l in range(4)])
+    for i, x in enumerate((rt, tt, tz, p)):
+        up[24 + 4 * i : 28 + 4 * i] = x[12:]
+    for i, x in enumerate((rt, tt, tz, p, rz, zz)):
+        dn[6 + i] = x[0]
+    for i, x in enumerate((rz, tz, zz, p)):
+        up[48 + i] = below_partial(x[12:])
 
 
 def stage(*refs):
@@ -316,7 +347,7 @@
     sources[0] = sources[0].at[first_r]
     sources[1] = sources[1].at[first_z]
     state = sources.pop()
-    sources += [state.at[0:96], state.at[96:COEF], state.at[COEF:]]
+    sources += [state.at[0:COEF], state.at[COEF:]]
     copies = [pltpu.make_async_copy(a, b, sems.at[i]) for i, (a, b) in enumerate(zip(sources, pairs[count:]))]
     for copy in copies:
         copy.start()
@@ -324,13 +355,14 @@
         copy.wait()
 
 
-def launch(s, vw, t_in, up, dn, coef, dr_m, items, pk, keep):
+def launch(s, state, up, dn, coef, dr_m, items, pk, keep):
     has_below = coef[FLAGS]
     has_above = coef[FLAGS + 1]
     c = {name: coef[n] for n, name in enumerate(OWN)}
     for n, name in enumerate(SHARED):
-        c[name] = c[name] + up[108 + n] + dn[69 + n]
+        c[name] = c[name] + up[UP_COEF + n] + dn[DN_COEF + n]
     q = inverse_radius(0, NR)
+    cv, cf, cr, bulk, couple, modulus, shear = [spread_rows(c[n], 1, 5, True) for n in SHARED]
 
     def radial(fields):
         stacked = jnp.concatenate([flat(x) for x in fields], axis=0)
@@ -338,36 +370,38 @@
         count = fields[0].shape[0]
         return [out[8 * count * i : 8 * count * (i + 1)].reshape(count, 8, NR) for i in range(len(fields))]
 
-    def ext(f):
-        return jnp.concatenate([up[8 * f : 8 * f + 8], s[f], dn[5 * f : 5 * f + 5]], axis=0)
-
-    def ext_v(f):
-        return jnp.concatenate(
-            [up[56 + 8 * f : 64 + 8 * f], vw[16 * f : 16 * f + 16], dn[35 + 5 * f : 40 + 5 * f]], axis=0
-        )
-
-    above29 = lax.broadcasted_iota(jnp.int32, (29, 8, NR), 0) < 24
-    mask29 = jnp.where(above29, 1.0, has_above)
-    rr, tt, zz, rt, rz, tz, p = [ext(f) for f in range(7)]
-    cv, cf, cr = [spread_rows(c[n], 0, 7, True) for n in ("cv", "cf", "cr")]
-    r_rr, r_rt, r_rz, r_p = radial([rr, rt, rz, p])
-    z_rz, z_tz, z_zz, z_p = [
-        depth_derivative(x, 0, 7, 2, has_below, up[104 + i], dn[65 + i]) for i, x in enumerate((rz, tz, zz, p))
+    def added(f, partial, above):
+        x = s[f]
+        planes = [float(ROW[l, 4]) * x[0] for l in range(4)]
+        planes.append(has_below * partial)
+        planes += [float(ROW[l, 4]) * above for l in range(4)]
+        planes.append(has_above * below_partial(x[12:]))
+        return jnp.stack(planes)
+
+    def edges(x):
+        return jnp.concatenate([x[:5], x[16:]], axis=0)
+
+    e_cv, e_cf, e_cr = edges(cv), edges(cf), edges(cr)
+    m_rz, m_tz, m_zz, m_p = [
+        added(f, up[48 + i], dn[n]) for i, (f, n) in enumerate(((4, 10), (5, 8), (2, 11), (6, 9)))
     ]
-    d_r = r_rr + z_rz + q * (rr - tt)
-    d_t = r_rt + z_tz + 2.0 * q * rt
-    d_z = r_rz + z_zz + q * rz
-    v1 = [
-        mask29 * (ext_v(0) + cv * d_r + cf * r_p),
-        mask29 * (ext_v(1) + cv * d_t),
-        mask29 * (ext_v(2) + cv * d_z + cf * z_p),
+    to_v = [e_cv * m_rz, e_cv * m_tz, e_cv * m_zz + e_cf * m_p]
+    to_w = [e_cf * m_rz, e_cf * m_tz, e_cf * m_zz + e_cr * m_p]
+
+    def inner_planes(n, more):
+        x = state[16 * n : 16 * n + 16]
+        return [x[:1] + more[4:5], x[1:12], x[12:] + more[5:9]]
+
+    def whole(f, more):
+        ends = [up[4 * f : 4 * f + 4] + more[:4]], [dn[f : f + 1] + more[9:]]
+        return jnp.concatenate(ends[0] + inner_planes(f, more) + ends[1], axis=0)
+
+    v1 = [whole(i, to_v[i]) for i in range(3)]
+    w1 = [whole(3 + i, -to_w[i]) for i in range(3)]
+    q_rt, q_tt, q_tz, q_p = [
+        q * jnp.concatenate([up[24 + 4 * i : 28 + 4 * i], s[f], dn[6 + i : 7 + i]], axis=0)
+        for i, f in enumerate((3, 1, 5, 6))
     ]
-    w1 = [
-        mask29 * (ext_v(3) - cf * d_r - cr * r_p),
-        mask29 * (ext_v(4) - cf * d_t),
-        mask29 * (ext_v(5) - cf * d_z - cr * z_p),
-    ]
-    q_rt, q_tt, q_tz, q_p = q * rt, q * tt, q * tz, q * p
     u = [cv * q_rt, cv * q_tt + cf * q_p, cv * q_tz]
     uw = [-(cf * q_rt), -(cf * q_tt + cr * q_p), -(cf * q_tz)]
 
@@ -379,38 +413,44 @@
 
     for f, x in enumerate((3, 1, 5, 6)):
         pack(f, s[x])
-    fric = spread_rows(c["fric"], 2, 4)
-    kappa = spread_rows(c["kappa"], 2, 4)
-    grads = (r_p, None, z_p)
-    for i, d in enumerate((d_r, d_t, d_z)):
-        g = fric * (t_in[16 * i : 16 * i + 16] + kappa * w1[i][8:24])
-        if grads[i] is not None:
-            g = g + grads[i][8:24]
-        a = cv[8:24] * d[8:24] + cf[8:24] * g
-        b = cf[8:24] * d[8:24] + cr[8:24] * g
-        pack(4 + i, v1[i][8:24])
+    fk = spread_rows(c["fric"] * c["kappa"], 2, 4)
+    o_cf, o_cr = cf[4:20], cr[4:20]
+    for i in range(3):
+        v_i, w_i = v1[i][4:20], w1[i][4:20]
+        a = jnp.concatenate(inner_planes(6 + i, to_v[i]), axis=0) + o_cf * (fk * w_i)
+        b = jnp.concatenate(inner_planes(9 + i, to_w[i]), axis=0) + o_cr * (fk * w_i)
+        pack(4 + i, v_i)
         pack(9 + i, a)
-        keep[i] = v1[i][8:24]
-        keep[3 + i] = w1[i][8:24]
+        keep[i] = v_i
+        keep[3 + i] = w_i
         keep[6 + i] = a
         keep[9 + i] = b
         if i == 1:
-            pack(7, w1[i][8:24])
+            pack(7, w_i)
             pack(12, b)
 
-    bulk, couple, modulus, shear = [
-        spread_rows(c[n], 1, 6)[:21] for n in ("bulk", "couple", "modulus", "shear")
-    ]
     mask21 = jnp.where(lax.broadcasted_iota(jnp.int32, (21, 8, NR), 0) < 20, 1.0, has_above)
     plane21 = lax.broadcasted_iota(jnp.int32, (21, 8, NR), 0) - 4
     lane21 = lax.broadcasted_iota(jnp.int32, (21, 8, NR), 2)
     source = jnp.where((plane21.astype(F32) == coef[FLAGS + 2]) & (lane21 < 4 * RB), SOURCE, 0.0)
 
     def stresses(v, w, extra):
-        inner = slice(4, 25)
-        vr, vt, wr = v[0][inner], v[1][inner], w[0][inner]
-        r_r, r_t, r_z, r_w = radial([vr, vt, v[2][inner], wr])
-        z_r, z_t, z_z, z_w = [depth_derivative(x, 1, 6, 2, has_below) for x in (v[0], v[1], v[2], w[2])]
+        at = 12 if extra is None else 16
+        low = 40 if extra is None else 44
+        vr, vt, wr = v[0], v[1], w[0]
+        r_r, r_t, r_z, r_w = radial([vr, vt, v[2], wr])
+        z_r, z_t, z_z, z_w = [
+            depth_derivative(
+                x,
+                0,
+                5,
+                1,
+                has_below,
+                up[low + n] + float(ROW[4, 4]) * x[0],
+                dn[at + n] + float(ROW[0, 0]) * x[20],
+            )
+            for n, x in enumerate((v[0], v[1], v[2], w[2]))
+        ]
         e_tt, g_rt, g_tz, div_w = q * vr, r_t - q * vt, z_t, r_w + q * wr + z_w
         if extra is not None:
             e_tt, g_rt, g_tz, div_w = e_tt + extra[1], g_rt + extra[0], g_tz + extra[2], div_w + extra[3]
@@ -428,15 +468,14 @@
 
     x0 = stresses(v1, w1, None)
     pack(8, x0["w"][4:20])
-    inner = slice(4, 25)
-    x1 = stresses(u, uw, [q * v1[0][inner], q * v1[1][inner], q * v1[2][inner], q * w1[1][inner]])
-    e2, dw2 = q * u[1][inner], q * uw[1][inner]
+    x1 = stresses(u, uw, [q * v1[0], q * v1[1], q * v1[2], q * w1[1]])
+    e2, dw2 = q * u[1], q * uw[1]
     total2 = bulk * e2 + couple * dw2
     x2 = dict(
         rr=mask21 * total2,
         zz=mask21 * total2,
-        rt=mask21 * (shear * (q * u[0][inner])),
-        tz=mask21 * (shear * (q * u[2][inner])),
+        rt=mask21 * (shear * (q * u[0])),
+        tz=mask21 * (shear * (q * u[2])),
         p=mask21 * (-(couple * e2 + modulus * dw2)),
     )
 
@@ -446,25 +485,25 @@
         hi, lo = [jnp.concatenate([items[h, NR * i : NR * i + NR] for i in slots], axis=0) for h in range(2)]
         return mm(stacked, hi, lo).reshape(-1, 8, NR)
 
-    def depth_items(fields, first):
+    def depth_items(fields):
         out = []
         for x in fields:
             if x is None:
                 out += [jnp.zeros((8, NR), F32)] * 2
             else:
-                out.append(x[first + 20])
-                out.append(has_below * below_partial(x[first : first + 4]))
+                out.append(x[20])
+                out.append(has_below * below_partial(x[:4]))
         return jnp.stack(out)
 
-    velocity_r = [v1[0][8:24], v1[1][8:24], v1[2][8:24], None] + [x[8:24] for x in (u[0], u[1], u[2], uw[0])]
-    pack(13, radius_items(velocity_r))
+    velocity_r = [v1[0], v1[1], v1[2], None, u[0], u[1], u[2], uw[0]]
+    pack(13, radius_items([None if x is None else x[4:20] for x in velocity_r]))
     names_r = ("rr", "rt", "rz", "p")
     pack(14, radius_items([x[n][4:20] for x in (x0, x1) for n in names_r]))
-    pack(15, depth_items([v1[0], v1[1], v1[2], None, u[0], u[1], u[2], uw[2]], 4))
+    pack(15, depth_items([v1[0], v1[1], v1[2], None, u[0], u[1], u[2], uw[2]]))
     names_z = ("rz", "tz", "zz", "p")
-    pack(16, depth_items([x[n] for x in (x0, x1) for n in names_z], 0))
+    pack(16, depth_items([x[n] for x in (x0, x1) for n in names_z]))
     second = [x2[n][4 + 8 * h : 12 + 8 * h] if n in x2 else None for h in range(2) for n in names_r]
-    pack(17, jnp.concatenate([radius_items(second), depth_items([x2.get(n) for n in names_z], 0)], axis=0))
+    pack(17, jnp.concatenate([radius_items(second), depth_items([x2.get(n) for n in names_z])], axis=0))
 
 
 def ring(recv, coef, mr, mz, dt_m, wr, wz, out):
@@ -728,28 +767,28 @@
     tables = [layer_ids, materials, jkd, source_depth]
     state, up, dn, ring_coef = call(
         prepare,
-        tables + [memory, velocity, stress],
-        [(COEF + FLAGS + 3, AZ, NR), (115, AZ, NR), (76, AZ, NR), (len(RING) + 1, 8, 256)],
-        hbm=range(7),
+        tables + [stress, memory, velocity, c["dr"]],
+        [(COEF + FLAGS + 3, AZ, NR), (UP_COEF + 7, AZ, NR), (DN_COEF + 7, AZ, NR), (len(RING) + 1, 8, 256)],
+        hbm=range(8),
         scratch=[pltpu.SMEM(x.shape, x.dtype) for x in tables]
-        + [pltpu.VMEM((n,) + block, F32) for n in (12, 6, 7)]
-        + [pltpu.SemaphoreType.DMA((7,))],
+        + [pltpu.VMEM((n,) + block, F32) for n in (7, 12, 6)]
+        + [pltpu.VMEM(c["dr"].shape, BF16), pltpu.SemaphoreType.DMA((8,))],
         vmem=VMEM_FULL,
     )
     up, dn = shift(up, 1), shift(dn, -1)
     staged = [c[n] for n in ("mr", "mz", "dt", "wr", "wz")]
     shapes = [x.shape[1:] if n < 2 else x.shape for n, x in enumerate(staged)]
-    *matrices, vw, t_part, coef = call(
+    *matrices, state, coef = call(
         stage,
         staged + [state],
-        shapes + [(96, AZ, NR), (48, AZ, NR), (FLAGS + 3, AZ, NR)],
-        types=[BF16] * 5 + [F32] * 3,
+        shapes + [(COEF, AZ, NR), (FLAGS + 3, AZ, NR)],
+        types=[BF16] * 5 + [F32] * 2,
         hbm=range(6),
-        scratch=[pltpu.SemaphoreType.DMA((8,))],
+        scratch=[pltpu.SemaphoreType.DMA((7,))],
     )
     packed, keep = call(
         launch,
-        [stress, vw, t_part, up, dn, coef, c["dr"], c["items"]],
+        [stress, state, up, dn, coef, c["dr"], c["items"]],
         [(8, 2 * FIELDS_IN, AZ, NR), (12,) + block],
         micros=4,
     )

time: 106 us -> 105 us (level)
  Pallas kernels: 12.8 us -> 14.7 us
  starting transfers between devices: 14.4 us -> 12.6 us
  waiting for transfers between devices: 11.8 us -> 10.1 us
  blocking collectives: 62.7 us -> 63.8 us
    pallas_call x7, Pallas kernels: 12.8 us -> 14.7 us  [call(): pl.pallas_call(body, out_shape=[jax.ShapeDtypeStruct(x, t) for x, t in zi...]
    ppermute x4, starting transfers between devices: 14.4 us -> 12.6 us  [shift(): lax.ppermute(value, 'depth', [(i, i + steps) for i in range(first, last)])]
    ppermute x4, waiting for transfers between devices: 11.8 us -> 10.1 us  [shift(): lax.ppermute(value, 'depth', [(i, i + steps) for i in range(first, last)])]
where the time goes in v4:
time: 105 us
  blocking collectives  63.8 us (61%)
  Pallas kernels  14.7 us (14%)
  starting transfers between devices  12.6 us (12%)
  waiting for transfers between devices  10.1 us (10%)
  local copies, waits for them, and re-layouts  1.96 us (2%)
  between operations  1.58 us (2%)
    all_to_all x1, blocking collectives, on_device(): lax.all_to_all(packed, 'az', split_axis=0, concat_axis=0, tiled=True)  37.4 us
    all_to_all x1, blocking collectives, on_device(): back = lax.all_to_all(back, 'az', split_axis=0, concat_axis=0, tiled=True)  26.4 us
    pallas_call x7, Pallas kernels, call(): pl.pallas_call(body, out_shape=[jax.ShapeDtypeStruct(x, t) for x, t in zi...  14.7 us
    ppermute x4, starting transfers between devices, shift(): lax.ppermute(value, 'depth', [(i, i + steps) for i in range(first, last)])  12.6 us
    ppermute x4, waiting for transfers between devices, shift(): lax.ppermute(value, 'depth', [(i, i + steps) for i in range(first, last)])  10.1 us
  transfers between devices with their start and end apart: 4, of which 2 were waited for; matrix products, arithmetic and copies ran while one was open for 0% of the time, Pallas kernels for 2%

profile of v4, /device:TPU:31, one launch (start us, length us, event | category | flops | bytes accessed | tf_op | source)
XLA Modules:
  0.0 104.8 jit_solution(1071456048432778215)
XLA Ops:
  0.6 0.0 copy-start.6
  0.6 0.0 copy-start.7
  0.7 0.0 copy-start.8
  0.7 0.0 copy-start.9
  1.4 3.0 %prepare.1 = (f32[209,8,128]{2,1,0:T(8,128)}, f32[59,8,128]{2,1,0:T(8,128)}, f32[27,8,128]{2,1,0:T(8,128)}, f32[9,8,256]{2,1,0:T(8,128)}) custom-call(s32[4,32]{1,0:T(4,128)} %lids_hbm.1, f32[8,8]{1,0:T(8,128)} %mat_hbm.1, f32[8,9]{1,0:T(8,128)} %jkd_hbm.1, s32[1]{0:T(128)S(6)} %copy.19.src_hbm, f32[7,16,8,128]{3,2,1,0:T(8,128)} %s.3, ...), custom_call_target="tpu_custom_call" | custom-call | bytes 3000000 | tf_op jit(solution)/shard_map/prepare/pallas_call | solution.py:745
  4.4 4.9 %collective-permute-start = (f32[59,8,128]{2,1,0:T(8,128)}, f32[59,8,128]{2,1,0:T(8,128)S(1)}, u32[]{:S(2)}, u32[]{:S(2)}) collective-permute-start(f32[59,8,128]{2,1,0:T(8,128)} %get-tuple-element.26), channel_id=1, source_target_pairs={{0,8},{8,16},{16,24},{24,32},{32,40},{40,48},{48,56},{56,64},{64,7... | collective-permute-start | bytes 725000 | tf_op jit(solution)/shard_map/ppermute | solution.py:761
  9.3 1.9 %collective-permute-start.1 = (f32[27,8,128]{2,1,0:T(8,128)}, f32[27,8,128]{2,1,0:T(8,128)S(1)}, u32[]{:S(2)}, u32[]{:S(2)}) collective-permute-start(f32[27,8,128]{2,1,0:T(8,128)} %get-tuple-element.27), channel_id=1, source_target_pairs={{8,0},{16,8},{24,16},{32,24},{40,32},{48,40},{56,48},{64,56},{72,6... | collective-permute-start | bytes 331784 | tf_op jit(solution)/shard_map/ppermute | solution.py:761
  11.2 0.0 copy-done.6
  11.2 0.0 copy-done.7
  11.3 0.0 copy-done.8
  11.3 0.0 copy-done.9
  11.3 0.0 copy-start.3
  11.3 1.1 %copy-done.3 = f32[209,8,128]{2,1,0:T(8,128)S(1)} copy-done((f32[209,8,128]{2,1,0:T(8,128)S(1)}, f32[209,8,128]{2,1,0:T(8,128)}, u32[]{:S(2)}) %copy-start.3) | copy-done | bytes 856088
  12.4 0.0 copy-start.11
  12.4 0.8 copy-done.11
  13.2 0.0 copy-start
  13.2 0.0 copy-start.4
  13.2 0.0 copy-start.5
  13.2 0.4 stage.1
  13.6 5.3 %collective-permute-done.1.dn = f32[27,8,128]{2,1,0:T(8,128)S(1)} collective-permute-done((f32[27,8,128]{2,1,0:T(8,128)}, f32[27,8,128]{2,1,0:T(8,128)S(1)}, u32[]{:S(2)}, u32[]{:S(2)}) %collective-permute-start.1) | collective-permute-done | bytes 110624 | tf_op jit(solution)/shard_map/ppermute | solution.py:761
  18.9 0.0 collective-permute-done.up
  18.9 0.0 copy-done
  18.9 0.0 copy-done.4
  18.9 0.0 copy-done.5
  18.9 4.5 %launch.1 = (f32[8,36,8,128]{3,2,1,0:T(8,128)S(1)}, f32[12,16,8,128]{3,2,1,0:T(8,128)S(1)}) custom-call(f32[7,16,8,128]{3,2,1,0:T(8,128)S(1)} %copy-done, f32[192,8,128]{2,1,0:T(8,128)S(1)} %get-tuple-element.25.state, f32[59,8,128]{2,1,0:T(8,128)S(1)} %collective-permute-done.up, f32[27,8,128]{2,1,0:T(8,128)S(1)} %collective-permute-done.1.dn, ...), custom_call_target="tpu_custom_call" | custom-call | bytes 12000000 | tf_op jit(solution)/shard_map/launch/pallas_call | solution.py:745
  23.5 0.0 copy-start.10
  23.5 37.4 %all_to_all.10.recv = f32[8,36,8,128]{3,2,1,0:T(8,128)S(1)} all-to-all(f32[8,36,8,128]{3,2,1,0:T(8,128)S(1)} %get-tuple-element.29), channel_id=1, replica_groups=mesh['depth'=64,'az'=8] {'az'}, dimensions={0} | all-to-all | bytes 2359296 | tf_op jit(solution)/shard_map/all_to_all | solution.py:795
  60.9 0.0 copy-done.10
  60.9 2.4 %ring.1 = f32[8,28,8,128]{3,2,1,0:T(8,128)S(1)} custom-call(f32[8,36,8,128]{3,2,1,0:T(8,128)S(1)} %all_to_all.10.recv, f32[9,8,256]{2,1,0:T(8,128)S(1)} %copy-done.10, bf16[2,128,128]{2,1,0:T(8,128)(2,1)S(1)} %get-tuple-element.31.mr, bf16[2,256,256]{2,1,0:T(8,128)(2,1)S(1)} %get-tuple-element.32.mz, bf16[2,64,64]{2,1,0:T(8,128)(2,1)S(1)} %get-tuple-element.33.dt_m, ...), custom_call_target="tpu_custom_call" | custom-call | bytes 9000000 | tf_op jit(solution)/shard_map/ring/pallas_call | solution.py:745
  63.3 26.4 %all_to_all.11.recv = f32[8,28,8,128]{3,2,1,0:T(8,128)S(1)} all-to-all(f32[8,28,8,128]{3,2,1,0:T(8,128)S(1)} %ring.1), channel_id=1, replica_groups=mesh['depth'=64,'az'=8] {'az'}, dimensions={0} | all-to-all | bytes 1835008 | tf_op jit(solution)/shard_map/all_to_all | solution.py:797
  89.7 0.0 copy-start.1
  89.7 0.0 copy-start.2
  89.7 2.1 %advance.1 = (f32[6,16,8,128]{3,2,1,0:T(8,128)S(1)}, f32[6,16,8,128]{3,2,1,0:T(8,128)S(1)}, f32[4,8,128]{2,1,0:T(8,128)S(1)}, f32[4,8,128]{2,1,0:T(8,128)S(1)}) custom-call(f32[8,28,8,128]{3,2,1,0:T(8,128)S(1)} %all_to_all.11.recv, f32[12,16,8,128]{3,2,1,0:T(8,128)S(1)} %get-tuple-element.36.keep, f32[17,8,128]{2,1,0:T(8,128)S(1)} %get-tuple-element.28.coef), custom_call_target="tpu_custom_call" | custom-call | bytes 3000000 | tf_op jit(solution)/shard_map/advance/pallas_call | solution.py:745
  91.8 3.9 %collective-permute-start.2 = (f32[4,8,128]{2,1,0:T(8,128)S(1)}, f32[4,8,128]{2,1,0:T(8,128)S(1)}, u32[]{:S(2)}, u32[]{:S(2)}) collective-permute-start(f32[4,8,128]{2,1,0:T(8,128)S(1)} %get-tuple-element.42), channel_id=1, source_target_pairs={{0,8},{8,16},{16,24},{24,32},{32,40},{40,48},{48,56},{56,64},{64,7... | collective-permute-start | bytes 49160 | tf_op jit(solution)/shard_map/ppermute | solution.py:761
  95.7 1.9 %collective-permute-start.3 = (f32[4,8,128]{2,1,0:T(8,128)S(1)}, f32[4,8,128]{2,1,0:T(8,128)S(1)}, u32[]{:S(2)}, u32[]{:S(2)}) collective-permute-start(f32[4,8,128]{2,1,0:T(8,128)S(1)} %get-tuple-element.43), channel_id=1, source_target_pairs={{8,0},{16,8},{24,16},{32,24},{40,32},{48,40},{56,48},{64,56},{72,6... | collective-permute-start | bytes 49160 | tf_op jit(solution)/shard_map/ppermute | solution.py:761
  97.6 0.0 copy-done.1
  97.6 0.0 copy-done.2
  97.6 1.6 %settle.1 = (f32[6,16,8,128]{3,2,1,0:T(8,128)}, f32[7,16,8,128]{3,2,1,0:T(8,128)}, f32[12,16,8,128]{3,2,1,0:T(8,128)}, f32[7,5,8,128]{3,2,1,0:T(8,128)S(1)}) custom-call(f32[8,28,8,128]{3,2,1,0:T(8,128)S(1)} %all_to_all.11.recv, f32[6,16,8,128]{3,2,1,0:T(8,128)S(1)} %get-tuple-element.37.v2, f32[6,16,8,128]{3,2,1,0:T(8,128)S(1)} %get-tuple-element.38.mid, ...), custom_call_target="tpu_custom_call" | custom-call | bytes 9000000 | tf_op jit(solution)/shard_map/settle/pallas_call | solution.py:745
  99.2 0.0 collective-permute-done.2.up
  99.2 4.8 %collective-permute-done.3.dn = f32[4,8,128]{2,1,0:T(8,128)S(1)} collective-permute-done((f32[4,8,128]{2,1,0:T(8,128)S(1)}, f32[4,8,128]{2,1,0:T(8,128)S(1)}, u32[]{:S(2)}, u32[]{:S(2)}) %collective-permute-start.3) | collective-permute-done | bytes 16416 | tf_op jit(solution)/shard_map/ppermute | solution.py:761
  104.1 0.7 close.1
Async XLA Ops:
  0.6 10.6 %copy-start.6 = (bf16[2,128,1024]{2,1,0:T(8,128)(2,1)S(1)}, bf16[2,128,1024]{2,1,0:T(8,128)(2,1)}, u32[]{:S(2)}) copy-start(bf16[2,128,1024]{2,1,0:T(8,128)(2,1)} %constant.19.clone.refs_4_) | copy-start | bytes 1572868
  0.6 10.6 %copy-start.7 = (bf16[2,2,128,512]{3,2,1,0:T(8,128)(2,1)S(1)}, bf16[2,2,128,512]{3,2,1,0:T(8,128)(2,1)}, u32[]{:S(2)}) copy-start(bf16[2,2,128,512]{3,2,1,0:T(8,128)(2,1)} %constant.18.clone.refs_3_) | copy-start | bytes 1572868
  0.7 10.6 %copy-start.8 = (bf16[2,2,256,256]{3,2,1,0:T(8,128)(2,1)S(1)}, bf16[2,2,256,256]{3,2,1,0:T(8,128)(2,1)}, u32[]{:S(2)}) copy-start(bf16[2,2,256,256]{3,2,1,0:T(8,128)(2,1)} %constant.16.clone.refs_1_) | copy-start | bytes 1572868
  0.7 10.6 %copy-start.9 = (bf16[2,2,128,128]{3,2,1,0:T(8,128)(2,1)S(1)}, bf16[2,2,128,128]{3,2,1,0:T(8,128)(2,1)}, u32[]{:S(2)}) copy-start(bf16[2,2,128,128]{3,2,1,0:T(8,128)(2,1)} %constant.15.clone.refs_0_) | copy-start | bytes 393220
  4.4 14.5 %collective-permute-start = (f32[59,8,128]{2,1,0:T(8,128)}, f32[59,8,128]{2,1,0:T(8,128)S(1)}, u32[]{:S(2)}, u32[]{:S(2)}) collective-permute-start(f32[59,8,128]{2,1,0:T(8,128)} %get-tuple-element.26), channel_id=1, source_target_pairs={{0,8},{8,16},{16,24},{24,32},{32,40},{40,48},{48,56},{56,64},{64,7... | collective-permute-start | bytes 725000 | tf_op jit(solution)/shard_map/ppermute | solution.py:761
  9.3 9.6 %collective-permute-start.1 = (f32[27,8,128]{2,1,0:T(8,128)}, f32[27,8,128]{2,1,0:T(8,128)S(1)}, u32[]{:S(2)}, u32[]{:S(2)}) collective-permute-start(f32[27,8,128]{2,1,0:T(8,128)} %get-tuple-element.27), channel_id=1, source_target_pairs={{8,0},{16,8},{24,16},{32,24},{40,32},{48,40},{56,48},{64,56},{72,6... | collective-permute-start | bytes 331784 | tf_op jit(solution)/shard_map/ppermute | solution.py:761
  11.3 1.2 %copy-start.3 = (f32[209,8,128]{2,1,0:T(8,128)S(1)}, f32[209,8,128]{2,1,0:T(8,128)}, u32[]{:S(2)}) copy-start(f32[209,8,128]{2,1,0:T(8,128)} %get-tuple-element.24.refs_5_) | copy-start | bytes 2568196
  12.4 0.8 copy-start.11
  13.2 5.7 %copy-start = (f32[7,16,8,128]{3,2,1,0:T(8,128)S(1)}, f32[7,16,8,128]{3,2,1,0:T(8,128)}, u32[]{:S(2)}) copy-start(f32[7,16,8,128]{3,2,1,0:T(8,128)} %s.3) | copy-start | bytes 1376260
  13.2 5.7 %copy-start.4 = (bf16[2,128,128]{2,1,0:T(8,128)(2,1)S(1)}, bf16[2,128,128]{2,1,0:T(8,128)(2,1)}, u32[]{:S(2)}) copy-start(bf16[2,128,128]{2,1,0:T(8,128)(2,1)} %constant.14.clone.dr_hbm.dr_m) | copy-start | bytes 196612
  13.2 5.7 %copy-start.5 = (bf16[2,1024,128]{2,1,0:T(8,128)(2,1)S(1)}, bf16[2,1024,128]{2,1,0:T(8,128)(2,1)}, u32[]{:S(2)}) copy-start(bf16[2,1024,128]{2,1,0:T(8,128)(2,1)} %constant.20.clone.items) | copy-start | bytes 1572868
  23.5 37.4 %copy-start.10 = (f32[9,8,256]{2,1,0:T(8,128)S(1)}, f32[9,8,256]{2,1,0:T(8,128)}, u32[]{:S(2)}) copy-start(f32[9,8,256]{2,1,0:T(8,128)} %get-tuple-element.30.coef) | copy-start | bytes 221188
  89.7 7.9 %copy-start.1 = (f32[12,16,8,128]{3,2,1,0:T(8,128)S(1)}, f32[12,16,8,128]{3,2,1,0:T(8,128)}, u32[]{:S(2)}) copy-start(f32[12,16,8,128]{3,2,1,0:T(8,128)} %psi.1) | copy-start | bytes 2359300
  89.7 7.9 %copy-start.2 = (f32[6,16,8,128]{3,2,1,0:T(8,128)S(1)}, f32[6,16,8,128]{3,2,1,0:T(8,128)}, u32[]{:S(2)}) copy-start(f32[6,16,8,128]{3,2,1,0:T(8,128)} %v.1) | copy-start | bytes 1179652
  91.8 7.4 %collective-permute-start.2 = (f32[4,8,128]{2,1,0:T(8,128)S(1)}, f32[4,8,128]{2,1,0:T(8,128)S(1)}, u32[]{:S(2)}, u32[]{:S(2)}) collective-permute-start(f32[4,8,128]{2,1,0:T(8,128)S(1)} %get-tuple-element.42), channel_id=1, source_target_pairs={{0,8},{8,16},{16,24},{24,32},{32,40},{40,48},{48,56},{56,64},{64,7... | collective-permute-start | bytes 49160 | tf_op jit(solution)/shard_map/ppermute | solution.py:761
  95.7 8.4 %collective-permute-start.3 = (f32[4,8,128]{2,1,0:T(8,128)S(1)}, f32[4,8,128]{2,1,0:T(8,128)S(1)}, u32[]{:S(2)}, u32[]{:S(2)}) collective-permute-start(f32[4,8,128]{2,1,0:T(8,128)S(1)} %get-tuple-element.43), channel_id=1, source_target_pairs={{8,0},{16,8},{24,16},{32,24},{40,32},{48,40},{56,48},{64,56},{72,6... | collective-permute-start | bytes 49160 | tf_op jit(solution)/shard_map/ppermute | solution.py:761

commit v5 on v4

--- a/solution.py
+++ b/solution.py
@@ -229,15 +229,15 @@
 
 def exchange_groups(x):
     groups = lane_groups()
-    rows = [x[j] for j in range(8)]
-    for s in (4, 2, 1):
-        low = (groups & s) == 0
-        for j in range(8):
-            if not j & s:
-                a, b = rows[j], rows[j + s]
-                rows[j] = jnp.where(low, a, roll(b, GROUP * s))
-                rows[j + s] = jnp.where(low, roll(a, -GROUP * s), b)
-    return rows
+    rows = [roll(x[j], GROUP * j) if j else x[j] for j in range(8)]
+    for s in (1, 2, 4):
+        stay = (groups & s) == 0
+        rows = [jnp.where(stay, rows[j], rows[(j + s) % 8]) for j in range(8)]
+    return [roll(rows[-k % 8], -GROUP * k) if k else rows[0] for k in range(8)]
+
+
+def for_each(count, body, unroll=4):
+    lax.fori_loop(0, count, lambda i, _: (body(i), 0)[1], 0, unroll=unroll)
 
 
 def flat(x):
@@ -245,18 +245,18 @@
 
 
 def prepare(
-    lids_hbm, mat_hbm, jkd_hbm, src_hbm, s_hbm, psi_hbm, v_hbm, dr_hbm,
+    lids_hbm, mat_hbm, jkd_hbm, s_hbm, psi_hbm, v_hbm, dr_hbm,
     state, up, dn, ring_coef,
-    lids, mat, jkd, src, s, psi, v, dr_m, sems,
+    lids, mat, jkd, s, psi, v, dr_m, sems,
 ):
     pairs = (
-        (lids_hbm, lids), (mat_hbm, mat), (jkd_hbm, jkd), (src_hbm, src), (s_hbm, s), (psi_hbm, psi),
+        (lids_hbm, lids), (mat_hbm, mat), (jkd_hbm, jkd), (s_hbm, s), (psi_hbm, psi),
         (v_hbm, v), (dr_hbm, dr_m),
     )
     copies = [pltpu.make_async_copy(a, b, sems.at[i]) for i, (a, b) in enumerate(pairs)]
     for copy in copies:
         copy.start()
-    for copy in copies[:4]:
+    for copy in copies[:3]:
         copy.wait()
     device = lax.axis_index("depth")
     rows = lax.broadcasted_iota(jnp.int32, (8, NR), 0)
@@ -264,10 +264,8 @@
     mine = (rows >= 2) & (rows < 6)
     for n, name in enumerate(OWN):
         state[COEF + n] = jnp.where(mine, c[name], 0.0)
-    source = (src[0] - PLANES * device).astype(F32)
     state[COEF + FLAGS] = jnp.full((8, NR), jnp.where(device > 0, 1.0, 0.0), F32)
     state[COEF + FLAGS + 1] = jnp.full((8, NR), jnp.where(device < lax.axis_size("depth") - 1, 1.0, 0.0), F32)
-    state[COEF + FLAGS + 2] = jnp.full((8, NR), source, F32)
     for n, name in enumerate(SHARED):
         swapped = pltpu.roll(c[name], 4, 0)
         up[UP_COEF + n] = jnp.where(rows < 2, swapped, 0.0)
@@ -280,7 +278,6 @@
     rc = coefficients(ids.astype(F32), (mat, jkd))
     for n, name in enumerate(RING):
         ring_coef[n] = rc[name]
-    ring_coef[len(RING)] = jnp.full((8, 256), source, F32)
 
     def sp(value):
         return spread_rows(value, 2, 4)
@@ -290,7 +287,7 @@
     cv, cf, cr, fric = [sp(c[n]) for n in ("cv", "cf", "cr", "fric")]
     weights = [sp(w) for w in c["weights"]]
     decayed = [sp(w * d) for w, d in zip(c["weights"], c["decay"])]
-    for copy in copies[4:]:
+    for copy in copies[3:]:
         copy.wait()
     rr, tt, zz, rt, rz, tz, p = [s[f] for f in range(7)]
     stacked = jnp.concatenate([flat(x) for x in (rr, rt, rz, p)], axis=0)
@@ -339,7 +336,7 @@
 
 
 def stage(*refs):
-    *pairs, sems = refs
+    src, *pairs, mark, sems = refs
     count = 6
     first_r = jnp.where(lax.axis_index("az") == 0, 1, 0)
     first_z = jnp.where(lax.axis_index("depth") == 0, 1, 0)
@@ -351,11 +348,12 @@
     copies = [pltpu.make_async_copy(a, b, sems.at[i]) for i, (a, b) in enumerate(zip(sources, pairs[count:]))]
     for copy in copies:
         copy.start()
+    mark[...] = jnp.full((8, 256), (src[0] - PLANES * lax.axis_index("depth")).astype(F32), F32)
     for copy in copies:
         copy.wait()
 
 
-def launch(s, state, up, dn, coef, dr_m, items, pk, keep):
+def launch(s, state, up, dn, coef, mark, dr_m, items, pk, keep, hold):
     has_below = coef[FLAGS]
     has_above = coef[FLAGS + 1]
     c = {name: coef[n] for n, name in enumerate(OWN)}
@@ -406,10 +404,8 @@
     uw = [-(cf * q_rt), -(cf * q_tt + cr * q_p), -(cf * q_tz)]
 
     def pack(f, planes):
-        for g in range(2):
-            chunks = exchange_groups(planes[8 * g : 8 * g + 8])
-            for k in range(8):
-                pk[k, 2 * f + g] = chunks[k]
+        hold[2 * f] = planes[:8]
+        hold[2 * f + 1] = planes[8:]
 
     for f, x in enumerate((3, 1, 5, 6)):
         pack(f, s[x])
@@ -432,7 +428,7 @@
     mask21 = jnp.where(lax.broadcasted_iota(jnp.int32, (21, 8, NR), 0) < 20, 1.0, has_above)
     plane21 = lax.broadcasted_iota(jnp.int32, (21, 8, NR), 0) - 4
     lane21 = lax.broadcasted_iota(jnp.int32, (21, 8, NR), 2)
-    source = jnp.where((plane21.astype(F32) == coef[FLAGS + 2]) & (lane21 < 4 * RB), SOURCE, 0.0)
+    source = jnp.where((plane21.astype(F32) == mark[:, :NR]) & (lane21 < 4 * RB), SOURCE, 0.0)
 
     def stresses(v, w, extra):
         at = 12 if extra is None else 16
@@ -505,8 +501,15 @@
     second = [x2[n][4 + 8 * h : 12 + 8 * h] if n in x2 else None for h in range(2) for n in names_r]
     pack(17, jnp.concatenate([radius_items(second), depth_items([x2.get(n) for n in names_z])], axis=0))
 
-
-def ring(recv, coef, mr, mz, dt_m, wr, wz, out):
+    def send(i):
+        chunks = exchange_groups(hold[i])
+        for k in range(8):
+            pk[k, i] = chunks[k]
+
+    for_each(2 * FIELDS_IN, send, unroll=9)
+
+
+def ring(recv, coef, mark, mr, mz, dt_m, wr, wz, out):
     group = lax.axis_index("az")
     c = {name: coef[n] for n, name in enumerate(RING)}
     q = inverse_radius(group, GROUP)
@@ -591,7 +594,7 @@
     total = c["bulk"] * div_v + c["couple"] * div_w
     shear = c["shear"]
     lanes = lax.broadcasted_iota(jnp.int32, (8, 256), 1) // GROUP
-    source = jnp.where(lanes.astype(F32) == coef[len(RING)], jnp.where(group == 0, SOURCE, 0.0), 0.0)
+    source = jnp.where(lanes.astype(F32) == mark[...], jnp.where(group == 0, SOURCE, 0.0), 0.0)
     n_rr = total + 2.0 * shear * r_r
     n_tt = total + 2.0 * shear * e_tt
     n_zz = total + 2.0 * shear * z_z
@@ -622,22 +625,26 @@
         out[:, 2 * f + 1] = x[:, :, 128:]
 
 
-def unpack(recv, f):
-    planes = []
-    for g in range(2):
-        planes += exchange_groups([recv[k, 2 * f + g] for k in range(8)])
-    return jnp.stack(planes)
-
-
-def advance(recv, keep, coef, new, mid, up, dn):
+def unpack(recv, hold, first, count):
+    def receive(i):
+        rows = exchange_groups([recv[k, 2 * first + i] for k in range(8)])
+        for j in range(8):
+            hold[i, j] = rows[j]
+
+    for_each(2 * count, receive)
+    return lambda f: jnp.concatenate([hold[2 * (f - first)], hold[2 * (f - first) + 1]], axis=0)
+
+
+def advance(recv, keep, coef, new, mid, up, dn, hold):
+    field = unpack(recv, hold, 0, 10)
     c = {name: coef[n] for n, name in enumerate(OWN)}
     q = inverse_radius(0, NR)
     cv, cf, cr = [spread_rows(c[n], 2, 4) for n in ("cv", "cf", "cr")]
-    q_rt, q_tt, q_tz, q_p = [q * unpack(recv, f) for f in range(4)]
+    q_rt, q_tt, q_tz, q_p = [q * field(f) for f in range(4)]
     dv = [cv * q_rt, cv * q_tt + cf * q_p, cv * q_tz]
     dw = [-(cf * q_rt), -(cf * q_tt + cr * q_p), -(cf * q_tz)]
     for i in range(3):
-        d, g = unpack(recv, 4 + i), unpack(recv, 7 + i)
+        d, g = field(4 + i), field(7 + i)
         v1 = keep[i] + dv[i]
         w1 = keep[3 + i] + dw[i]
         v2 = v1 + keep[6 + i] + cv * d + cf * g
@@ -655,7 +662,8 @@
             dn[3] = x[0]
 
 
-def settle(recv, v2, mid, v, s, psi, coef, dr_m, v_out, s_out, m_out, edge):
+def settle(recv, v2, mid, v, s, psi, coef, mark, dr_m, v_out, s_out, m_out, edge, hold):
+    field = unpack(recv, hold, 10, 4)
     v_out[...] = v2[...]
     has_below = coef[FLAGS]
     c = {name: coef[n] for n, name in enumerate(OWN)}
@@ -681,7 +689,7 @@
     stacked = jnp.concatenate([flat(x) for x in sums[:4]], axis=0)
     y = mm(stacked, dr_m[0], dr_m[1])
     r_r, r_t, r_z, r_w = [y[128 * i : 128 * i + 128].reshape(16, 8, NR) for i in range(4)]
-    a_r, a_t, a_z, a_w = [unpack(recv, 10 + i) for i in range(4)]
+    a_r, a_t, a_z, a_w = [field(10 + i) for i in range(4)]
     e_tt = q * (sums[0] + a_t)
     div_v = r_r + e_tt + z_z
     div_w = r_w + q * (sums[3] + a_w) + z_w
@@ -689,7 +697,7 @@
     total = sp(c["bulk"]) * div_v + couple * div_w
     plane = lax.broadcasted_iota(jnp.int32, (16, 8, NR), 0)
     lane = lax.broadcasted_iota(jnp.int32, (16, 8, NR), 2)
-    source = jnp.where((plane.astype(F32) == coef[FLAGS + 2]) & (lane < 4 * RB), SOURCE * (1.0 + math.cos(0.9)), 0.0)
+    source = jnp.where((plane.astype(F32) == mark[:, :NR]) & (lane < 4 * RB), SOURCE * (1.0 + math.cos(0.9)), 0.0)
     updates = [
         total + 2.0 * shear * r_r,
         total + 2.0 * shear * e_tt,
@@ -738,9 +746,9 @@
         copy.wait()
 
 
-def call(body, inputs, shapes, types=None, hbm=(), scratch=(), out_hbm=False, alias=None, micros=1, vmem=VMEM_LIMIT):
+def call(body, inputs, shapes, types=None, hbm=(), smem=(), scratch=(), out_hbm=False, alias=None, micros=1, vmem=VMEM_LIMIT):
     def space(i):
-        return pltpu.HBM if i in hbm else pltpu.VMEM
+        return pltpu.HBM if i in hbm else pltpu.SMEM if i in smem else pltpu.VMEM
 
     return pl.pallas_call(
         body,
@@ -764,47 +772,51 @@
 def on_device(velocity, stress, memory, layer_ids, materials, jkd, source_depth):
     c = constants()
     block = (PLANES, AZ, NR)
-    tables = [layer_ids, materials, jkd, source_depth]
+    tables = [layer_ids, materials, jkd]
     state, up, dn, ring_coef = call(
         prepare,
         tables + [stress, memory, velocity, c["dr"]],
-        [(COEF + FLAGS + 3, AZ, NR), (UP_COEF + 7, AZ, NR), (DN_COEF + 7, AZ, NR), (len(RING) + 1, 8, 256)],
-        hbm=range(8),
+        [(COEF + FLAGS + 2, AZ, NR), (UP_COEF + 7, AZ, NR), (DN_COEF + 7, AZ, NR), (len(RING), 8, 256)],
+        hbm=range(7),
         scratch=[pltpu.SMEM(x.shape, x.dtype) for x in tables]
         + [pltpu.VMEM((n,) + block, F32) for n in (7, 12, 6)]
-        + [pltpu.VMEM(c["dr"].shape, BF16), pltpu.SemaphoreType.DMA((8,))],
+        + [pltpu.VMEM(c["dr"].shape, BF16), pltpu.SemaphoreType.DMA((7,))],
         vmem=VMEM_FULL,
     )
     up, dn = shift(up, 1), shift(dn, -1)
     staged = [c[n] for n in ("mr", "mz", "dt", "wr", "wz")]
     shapes = [x.shape[1:] if n < 2 else x.shape for n, x in enumerate(staged)]
-    *matrices, state, coef = call(
+    *matrices, state, coef, mark = call(
         stage,
-        staged + [state],
-        shapes + [(COEF, AZ, NR), (FLAGS + 3, AZ, NR)],
-        types=[BF16] * 5 + [F32] * 2,
-        hbm=range(6),
+        [source_depth] + staged + [state],
+        shapes + [(COEF, AZ, NR), (FLAGS + 2, AZ, NR), (8, 256)],
+        types=[BF16] * 5 + [F32] * 3,
+        hbm=range(1, 7),
+        smem=(0,),
         scratch=[pltpu.SemaphoreType.DMA((7,))],
     )
     packed, keep = call(
         launch,
-        [stress, state, up, dn, coef, c["dr"], c["items"]],
+        [stress, state, up, dn, coef, mark, c["dr"], c["items"]],
         [(8, 2 * FIELDS_IN, AZ, NR), (12,) + block],
+        scratch=[pltpu.VMEM((2 * FIELDS_IN, 8, AZ, NR), F32)],
         micros=4,
     )
     packed = lax.all_to_all(packed, "az", split_axis=0, concat_axis=0, tiled=True)
-    (back,) = call(ring, [packed, ring_coef] + matrices, [(8, 2 * FIELDS_OUT, AZ, NR)], micros=3)
+    (back,) = call(ring, [packed, ring_coef, mark] + matrices, [(8, 2 * FIELDS_OUT, AZ, NR)], micros=3)
     back = lax.all_to_all(back, "az", split_axis=0, concat_axis=0, tiled=True)
     new, mid, up, dn = call(
         advance,
         [back, keep, coef],
         [(6,) + block, (6,) + block, (4, AZ, NR), (4, AZ, NR)],
+        scratch=[pltpu.VMEM((20, 8, AZ, NR), F32)],
     )
     up, dn = shift(up, 1), shift(dn, -1)
     v_out, s_part, m_out, edge = call(
         settle,
-        [back, new, mid, velocity, stress, memory, coef, c["dr"]],
+        [back, new, mid, velocity, stress, memory, coef, mark, c["dr"]],
         [(6,) + block, (7,) + block, (12,) + block, (7, 5, AZ, NR)],
+        scratch=[pltpu.VMEM((8, 8, AZ, NR), F32)],
         micros=3,
     )
     (s_out,) = call(

time: 105 us -> 101 us (0.962)
  the two profiles are of different devices: /device:TPU:31 before, /device:TPU:47 now
where the time goes in v5:
time: 101 us
  blocking collectives  70.4 us (70%)
  Pallas kernels  11.8 us (12%)
  starting transfers between devices  9.03 us (9%)
  waiting for transfers between devices  6.4 us (6%)
  local copies, waits for them, and re-layouts  1.96 us (2%)
  between operations  1.46 us (1%)
    all_to_all x1, blocking collectives, on_device(): lax.all_to_all(packed, 'az', split_axis=0, concat_axis=0, tiled=True)  41.6 us
    all_to_all x1, blocking collectives, on_device(): back = lax.all_to_all(back, 'az', split_axis=0, concat_axis=0, tiled=True)  28.8 us
    pallas_call x7, Pallas kernels, call(): pl.pallas_call(body, out_shape=[jax.ShapeDtypeStruct(x, t) for x, t in zi...  11.8 us
    ppermute x4, starting transfers between devices, shift(): lax.ppermute(value, 'depth', [(i, i + steps) for i in range(first, last)])  9.03 us
    ppermute x4, waiting for transfers between devices, shift(): lax.ppermute(value, 'depth', [(i, i + steps) for i in range(first, last)])  6.4 us
  transfers between devices with their start and end apart: 4, of which 2 were waited for; matrix products, arithmetic and copies ran while one was open for 0% of the time, Pallas kernels for 2%

profile of v5, /device:TPU:47, one launch (start us, length us, event | category | flops | bytes accessed | tf_op | source)
XLA Modules:
  0.0 101.0 jit_solution(11104903809135007321)
XLA Ops:
  0.6 0.0 copy-start.6
  0.6 0.0 copy-start.7
  0.7 0.0 copy-start.8
  0.7 0.0 copy-start.9
  0.7 3.1 %prepare.1 = (f32[208,8,128]{2,1,0:T(8,128)}, f32[59,8,128]{2,1,0:T(8,128)}, f32[27,8,128]{2,1,0:T(8,128)}, f32[8,8,256]{2,1,0:T(8,128)}) custom-call(s32[4,32]{1,0:T(4,128)} %lids_hbm.1, f32[8,8]{1,0:T(8,128)} %mat_hbm.1, f32[8,9]{1,0:T(8,128)} %jkd_hbm.1, f32[7,16,8,128]{3,2,1,0:T(8,128)} %s.3, f32[12,16,8,128]{3,2,1,0:T(8,128)} %psi.1, ...), custom_call_target="tpu_custom_call" | custom-call | bytes 3000000 | tf_op jit(solution)/shard_map/prepare/pallas_call | solution.py:753
  3.7 2.8 %collective-permute-start = (f32[59,8,128]{2,1,0:T(8,128)}, f32[59,8,128]{2,1,0:T(8,128)S(1)}, u32[]{:S(2)}, u32[]{:S(2)}) collective-permute-start(f32[59,8,128]{2,1,0:T(8,128)} %get-tuple-element.27), channel_id=1, source_target_pairs={{0,8},{8,16},{16,24},{24,32},{32,40},{40,48},{48,56},{56,64},{64,7... | collective-permute-start | bytes 725000 | tf_op jit(solution)/shard_map/ppermute | solution.py:769
  6.5 1.9 %collective-permute-start.1 = (f32[27,8,128]{2,1,0:T(8,128)}, f32[27,8,128]{2,1,0:T(8,128)S(1)}, u32[]{:S(2)}, u32[]{:S(2)}) collective-permute-start(f32[27,8,128]{2,1,0:T(8,128)} %get-tuple-element.28), channel_id=1, source_target_pairs={{8,0},{16,8},{24,16},{32,24},{40,32},{48,40},{56,48},{64,56},{72,6... | collective-permute-start | bytes 331784 | tf_op jit(solution)/shard_map/ppermute | solution.py:769
  9.1 0.0 copy-done.6
  9.1 0.0 copy-done.7
  9.1 0.0 copy-done.8
  9.1 0.0 copy-done.9
  9.2 0.0 copy-start.3
  9.2 1.1 %copy-done.3 = f32[208,8,128]{2,1,0:T(8,128)S(1)} copy-done((f32[208,8,128]{2,1,0:T(8,128)S(1)}, f32[208,8,128]{2,1,0:T(8,128)}, u32[]{:S(2)}) %copy-start.3) | copy-done | bytes 851992
  10.3 0.0 copy-start.11
  10.3 0.8 copy-done.11
  11.1 0.0 copy-start
  11.1 0.0 copy-start.4
  11.1 0.0 copy-start.5
  11.1 0.4 stage.1
  11.5 3.4 %collective-permute-done.1.dn = f32[27,8,128]{2,1,0:T(8,128)S(1)} collective-permute-done((f32[27,8,128]{2,1,0:T(8,128)}, f32[27,8,128]{2,1,0:T(8,128)S(1)}, u32[]{:S(2)}, u32[]{:S(2)}) %collective-permute-start.1) | collective-permute-done | bytes 110624 | tf_op jit(solution)/shard_map/ppermute | solution.py:769
  14.9 0.0 collective-permute-done.up
  14.9 0.0 copy-done
  14.9 0.0 copy-done.4
  14.9 0.0 copy-done.5
  14.9 2.4 %launch.1 = (f32[8,36,8,128]{3,2,1,0:T(8,128)S(1)}, f32[12,16,8,128]{3,2,1,0:T(8,128)S(1)}) custom-call(f32[7,16,8,128]{3,2,1,0:T(8,128)S(1)} %copy-done, f32[192,8,128]{2,1,0:T(8,128)S(1)} %get-tuple-element.26.state, f32[59,8,128]{2,1,0:T(8,128)S(1)} %collective-permute-done.up, f32[27,8,128]{2,1,0:T(8,128)S(1)} %collective-permute-done.1.dn, ...), custom_call_target="tpu_custom_call" | custom-call | bytes 12000000 | tf_op jit(solution)/shard_map/launch/pallas_call | solution.py:753
  17.4 0.0 copy-start.10
  17.4 41.6 %all_to_all.10.recv = f32[8,36,8,128]{3,2,1,0:T(8,128)S(1)} all-to-all(f32[8,36,8,128]{3,2,1,0:T(8,128)S(1)} %get-tuple-element.31), channel_id=1, replica_groups=mesh['depth'=64,'az'=8] {'az'}, dimensions={0} | all-to-all | bytes 2359296 | tf_op jit(solution)/shard_map/all_to_all | solution.py:805
  59.0 0.0 copy-done.10
  59.0 2.4 %ring.1 = f32[8,28,8,128]{3,2,1,0:T(8,128)S(1)} custom-call(f32[8,36,8,128]{3,2,1,0:T(8,128)S(1)} %all_to_all.10.recv, f32[8,8,256]{2,1,0:T(8,128)S(1)} %copy-done.10, f32[8,256]{1,0:T(8,128)S(1)} %get-tuple-element.30.mark, bf16[2,128,128]{2,1,0:T(8,128)(2,1)S(1)} %get-tuple-element.33.mr, bf16[2,256,256]{2,1,0:T(8,128)(2,1)S(1)} %get-tuple-element.34.mz, ...), custom_call_target="tpu_custom_call" | custom-call | bytes 9000000 | tf_op jit(solution)/shard_map/ring/pallas_call | solution.py:753
  61.4 28.8 %all_to_all.11.recv = f32[8,28,8,128]{3,2,1,0:T(8,128)S(1)} all-to-all(f32[8,28,8,128]{3,2,1,0:T(8,128)S(1)} %ring.1), channel_id=1, replica_groups=mesh['depth'=64,'az'=8] {'az'}, dimensions={0} | all-to-all | bytes 1835008 | tf_op jit(solution)/shard_map/all_to_all | solution.py:807
  90.2 0.0 copy-start.1
  90.2 0.0 copy-start.2
  90.2 1.0 %advance.1 = (f32[6,16,8,128]{3,2,1,0:T(8,128)S(1)}, f32[6,16,8,128]{3,2,1,0:T(8,128)S(1)}, f32[4,8,128]{2,1,0:T(8,128)S(1)}, f32[4,8,128]{2,1,0:T(8,128)S(1)}) custom-call(f32[8,28,8,128]{3,2,1,0:T(8,128)S(1)} %all_to_all.11.recv, f32[12,16,8,128]{3,2,1,0:T(8,128)S(1)} %get-tuple-element.38.keep, f32[16,8,128]{2,1,0:T(8,128)S(1)} %get-tuple-element.29.coef), custom_call_target="tpu_custom_call" | custom-call | bytes 3000000 | tf_op jit(solution)/shard_map/advance/pallas_call | solution.py:753
  91.2 1.9 %collective-permute-start.2 = (f32[4,8,128]{2,1,0:T(8,128)S(1)}, f32[4,8,128]{2,1,0:T(8,128)S(1)}, u32[]{:S(2)}, u32[]{:S(2)}) collective-permute-start(f32[4,8,128]{2,1,0:T(8,128)S(1)} %get-tuple-element.44), channel_id=1, source_target_pairs={{0,8},{8,16},{16,24},{24,32},{32,40},{40,48},{48,56},{56,64},{64,7... | collective-permute-start | bytes 49160 | tf_op jit(solution)/shard_map/ppermute | solution.py:769
  93.1 2.4 %collective-permute-start.3 = (f32[4,8,128]{2,1,0:T(8,128)S(1)}, f32[4,8,128]{2,1,0:T(8,128)S(1)}, u32[]{:S(2)}, u32[]{:S(2)}) collective-permute-start(f32[4,8,128]{2,1,0:T(8,128)S(1)} %get-tuple-element.45), channel_id=1, source_target_pairs={{8,0},{16,8},{24,16},{32,24},{40,32},{48,40},{56,48},{64,56},{72,6... | collective-permute-start | bytes 49160 | tf_op jit(solution)/shard_map/ppermute | solution.py:769
  95.6 0.0 copy-done.1
  95.6 0.0 copy-done.2
  95.6 1.7 %settle.1 = (f32[6,16,8,128]{3,2,1,0:T(8,128)}, f32[7,16,8,128]{3,2,1,0:T(8,128)}, f32[12,16,8,128]{3,2,1,0:T(8,128)}, f32[7,5,8,128]{3,2,1,0:T(8,128)S(1)}) custom-call(f32[8,28,8,128]{3,2,1,0:T(8,128)S(1)} %all_to_all.11.recv, f32[6,16,8,128]{3,2,1,0:T(8,128)S(1)} %get-tuple-element.39.v2, f32[6,16,8,128]{3,2,1,0:T(8,128)S(1)} %get-tuple-element.40.mid, ...), custom_call_target="tpu_custom_call" | custom-call | bytes 9000000 | tf_op jit(solution)/shard_map/settle/pallas_call | solution.py:753
  97.3 0.0 collective-permute-done.2.up
  97.3 3.0 %collective-permute-done.3.dn = f32[4,8,128]{2,1,0:T(8,128)S(1)} collective-permute-done((f32[4,8,128]{2,1,0:T(8,128)S(1)}, f32[4,8,128]{2,1,0:T(8,128)S(1)}, u32[]{:S(2)}, u32[]{:S(2)}) %collective-permute-start.3) | collective-permute-done | bytes 16416 | tf_op jit(solution)/shard_map/ppermute | solution.py:769
  100.3 0.7 close.1
Async XLA Ops:
  0.6 8.5 %copy-start.6 = (bf16[2,128,1024]{2,1,0:T(8,128)(2,1)S(1)}, bf16[2,128,1024]{2,1,0:T(8,128)(2,1)}, u32[]{:S(2)}) copy-start(bf16[2,128,1024]{2,1,0:T(8,128)(2,1)} %constant.19.clone.refs_5_) | copy-start | bytes 1572868
  0.6 8.5 %copy-start.7 = (bf16[2,2,128,512]{3,2,1,0:T(8,128)(2,1)S(1)}, bf16[2,2,128,512]{3,2,1,0:T(8,128)(2,1)}, u32[]{:S(2)}) copy-start(bf16[2,2,128,512]{3,2,1,0:T(8,128)(2,1)} %constant.18.clone.refs_4_) | copy-start | bytes 1572868
  0.7 8.5 %copy-start.8 = (bf16[2,2,256,256]{3,2,1,0:T(8,128)(2,1)S(1)}, bf16[2,2,256,256]{3,2,1,0:T(8,128)(2,1)}, u32[]{:S(2)}) copy-start(bf16[2,2,256,256]{3,2,1,0:T(8,128)(2,1)} %constant.16.clone.refs_2_) | copy-start | bytes 1572868
  0.7 8.5 %copy-start.9 = (bf16[2,2,128,128]{3,2,1,0:T(8,128)(2,1)S(1)}, bf16[2,2,128,128]{3,2,1,0:T(8,128)(2,1)}, u32[]{:S(2)}) copy-start(bf16[2,2,128,128]{3,2,1,0:T(8,128)(2,1)} %constant.15.clone.refs_1_) | copy-start | bytes 393220
  3.7 11.2 %collective-permute-start = (f32[59,8,128]{2,1,0:T(8,128)}, f32[59,8,128]{2,1,0:T(8,128)S(1)}, u32[]{:S(2)}, u32[]{:S(2)}) collective-permute-start(f32[59,8,128]{2,1,0:T(8,128)} %get-tuple-element.27), channel_id=1, source_target_pairs={{0,8},{8,16},{16,24},{24,32},{32,40},{40,48},{48,56},{56,64},{64,7... | collective-permute-start | bytes 725000 | tf_op jit(solution)/shard_map/ppermute | solution.py:769
  6.5 8.4 %collective-permute-start.1 = (f32[27,8,128]{2,1,0:T(8,128)}, f32[27,8,128]{2,1,0:T(8,128)S(1)}, u32[]{:S(2)}, u32[]{:S(2)}) collective-permute-start(f32[27,8,128]{2,1,0:T(8,128)} %get-tuple-element.28), channel_id=1, source_target_pairs={{8,0},{16,8},{24,16},{32,24},{40,32},{48,40},{56,48},{64,56},{72,6... | collective-permute-start | bytes 331784 | tf_op jit(solution)/shard_map/ppermute | solution.py:769
  9.2 1.2 %copy-start.3 = (f32[208,8,128]{2,1,0:T(8,128)S(1)}, f32[208,8,128]{2,1,0:T(8,128)}, u32[]{:S(2)}) copy-start(f32[208,8,128]{2,1,0:T(8,128)} %get-tuple-element.25.refs_6_) | copy-start | bytes 2555908
  10.3 0.8 copy-start.11
  11.1 3.9 %copy-start = (f32[7,16,8,128]{3,2,1,0:T(8,128)S(1)}, f32[7,16,8,128]{3,2,1,0:T(8,128)}, u32[]{:S(2)}) copy-start(f32[7,16,8,128]{3,2,1,0:T(8,128)} %s.3) | copy-start | bytes 1376260
  11.1 3.9 %copy-start.4 = (bf16[2,128,128]{2,1,0:T(8,128)(2,1)S(1)}, bf16[2,128,128]{2,1,0:T(8,128)(2,1)}, u32[]{:S(2)}) copy-start(bf16[2,128,128]{2,1,0:T(8,128)(2,1)} %constant.14.clone.dr_hbm.dr_m) | copy-start | bytes 196612
  11.1 3.9 %copy-start.5 = (bf16[2,1024,128]{2,1,0:T(8,128)(2,1)S(1)}, bf16[2,1024,128]{2,1,0:T(8,128)(2,1)}, u32[]{:S(2)}) copy-start(bf16[2,1024,128]{2,1,0:T(8,128)(2,1)} %constant.20.clone.items) | copy-start | bytes 1572868
  17.4 41.6 %copy-start.10 = (f32[8,8,256]{2,1,0:T(8,128)S(1)}, f32[8,8,256]{2,1,0:T(8,128)}, u32[]{:S(2)}) copy-start(f32[8,8,256]{2,1,0:T(8,128)} %get-tuple-element.32.coef) | copy-start | bytes 196612
  90.2 5.4 %copy-start.1 = (f32[12,16,8,128]{3,2,1,0:T(8,128)S(1)}, f32[12,16,8,128]{3,2,1,0:T(8,128)}, u32[]{:S(2)}) copy-start(f32[12,16,8,128]{3,2,1,0:T(8,128)} %psi.1) | copy-start | bytes 2359300
  90.2 5.4 %copy-start.2 = (f32[6,16,8,128]{3,2,1,0:T(8,128)S(1)}, f32[6,16,8,128]{3,2,1,0:T(8,128)}, u32[]{:S(2)}) copy-start(f32[6,16,8,128]{3,2,1,0:T(8,128)} %v.1) | copy-start | bytes 1179652
  91.2 6.1 %collective-permute-start.2 = (f32[4,8,128]{2,1,0:T(8,128)S(1)}, f32[4,8,128]{2,1,0:T(8,128)S(1)}, u32[]{:S(2)}, u32[]{:S(2)}) collective-permute-start(f32[4,8,128]{2,1,0:T(8,128)S(1)} %get-tuple-element.44), channel_id=1, source_target_pairs={{0,8},{8,16},{16,24},{24,32},{32,40},{40,48},{48,56},{56,64},{64,7... | collective-permute-start | bytes 49160 | tf_op jit(solution)/shard_map/ppermute | solution.py:769
  93.1 7.2 %collective-permute-start.3 = (f32[4,8,128]{2,1,0:T(8,128)S(1)}, f32[4,8,128]{2,1,0:T(8,128)S(1)}, u32[]{:S(2)}, u32[]{:S(2)}) collective-permute-start(f32[4,8,128]{2,1,0:T(8,128)S(1)} %get-tuple-element.45), channel_id=1, source_target_pairs={{8,0},{16,8},{24,16},{32,24},{40,32},{48,40},{56,48},{64,56},{72,6... | collective-permute-start | bytes 49160 | tf_op jit(solution)/shard_map/ppermute | solution.py:769

commit v6 on v5

--- a/solution.py
+++ b/solution.py
@@ -246,8 +246,8 @@
 
 def prepare(
     lids_hbm, mat_hbm, jkd_hbm, s_hbm, psi_hbm, v_hbm, dr_hbm,
-    state, up, dn, ring_coef,
-    lids, mat, jkd, s, psi, v, dr_m, sems,
+    state, far, near, ring_coef,
+    up, dn, lids, mat, jkd, s, psi, v, dr_m, sems,
 ):
     pairs = (
         (lids_hbm, lids), (mat_hbm, mat), (jkd_hbm, jkd), (s_hbm, s), (psi_hbm, psi),
@@ -333,6 +333,24 @@
         dn[6 + i] = x[0]
     for i, x in enumerate((rz, tz, zz, p)):
         up[48 + i] = below_partial(x[12:])
+    dn[DN_COEF + 7 :] = jnp.zeros((UP_COEF - DN_COEF, 8, NR), F32)
+    outgoing(up[...], dn[...], near, far)
+
+
+def is_even():
+    return lax.axis_index("depth") % 2 == 0
+
+
+def outgoing(up, dn, near, far):
+    even = is_even()
+    near[...] = jnp.where(even, up, dn)
+    far[...] = jnp.where(even, dn, up)
+
+
+def incoming(near, far):
+    even = is_even()
+    x, y = near[...], far[...]
+    return jnp.where(even, y, x), jnp.where(even, x, y)
 
 
 def stage(*refs):
@@ -353,9 +371,10 @@
         copy.wait()
 
 
-def launch(s, state, up, dn, coef, mark, dr_m, items, pk, keep, hold):
+def launch(s, state, far, near, coef, mark, dr_m, items, pk, keep, hold):
     has_below = coef[FLAGS]
     has_above = coef[FLAGS + 1]
+    up, dn = incoming(near, far)
     c = {name: coef[n] for n, name in enumerate(OWN)}
     for n, name in enumerate(SHARED):
         c[name] = c[name] + up[UP_COEF + n] + dn[DN_COEF + n]
@@ -635,7 +654,8 @@
     return lambda f: jnp.concatenate([hold[2 * (f - first)], hold[2 * (f - first) + 1]], axis=0)
 
 
-def advance(recv, keep, coef, new, mid, up, dn, hold):
+def advance(recv, keep, coef, new, mid, far, near, hold):
+    up, dn = [], []
     field = unpack(recv, hold, 0, 10)
     c = {name: coef[n] for n, name in enumerate(OWN)}
     q = inverse_radius(0, NR)
@@ -654,12 +674,13 @@
         mid[i] = v1
         mid[3 + i] = w1
         x = v1 + v2
-        up[i] = below_partial(x[12:])
-        dn[i] = x[0]
+        up.append(below_partial(x[12:]))
+        dn.append(x[0])
         if i == 2:
             x = w1 + w2
-            up[3] = below_partial(x[12:])
-            dn[3] = x[0]
+            up.append(below_partial(x[12:]))
+            dn.append(x[0])
+    outgoing(jnp.stack(up), jnp.stack(dn), near, far)
 
 
 def settle(recv, v2, mid, v, s, psi, coef, mark, dr_m, v_out, s_out, m_out, edge, hold):
@@ -714,7 +735,8 @@
         edge[f, 1:] = x[12:]
 
 
-def close(s_in, edge, up, dn, coef, s_out, new, sems):
+def close(s_in, edge, far, near, coef, s_out, new, sems):
+    up, dn = incoming(near, far)
     has_below = coef[FLAGS]
     c = {name: coef[n] for n, name in enumerate(OWN)}
 
@@ -763,27 +785,32 @@
     )(*inputs)
 
 
-def shift(value, steps):
-    count = lax.axis_size("depth")
-    first, last = max(0, -steps), min(count, count - steps)
-    return lax.ppermute(value, "depth", [(i, i + steps) for i in range(first, last)])
+def swap(value, first):
+    lows = range(first, lax.axis_size("depth") - 1, 2)
+    return lax.ppermute(value, "depth", [p for i in lows for p in ((i, i + 1), (i + 1, i))])
+
+
+def neighbours(near, far):
+    far = swap(far, 1)
+    return swap(near, 0), far
 
 
 def on_device(velocity, stress, memory, layer_ids, materials, jkd, source_depth):
     c = constants()
     block = (PLANES, AZ, NR)
     tables = [layer_ids, materials, jkd]
-    state, up, dn, ring_coef = call(
+    state, far, near, ring_coef = call(
         prepare,
         tables + [stress, memory, velocity, c["dr"]],
-        [(COEF + FLAGS + 2, AZ, NR), (UP_COEF + 7, AZ, NR), (DN_COEF + 7, AZ, NR), (len(RING), 8, 256)],
+        [(COEF + FLAGS + 2, AZ, NR), (UP_COEF + 7, AZ, NR), (UP_COEF + 7, AZ, NR), (len(RING), 8, 256)],
         hbm=range(7),
-        scratch=[pltpu.SMEM(x.shape, x.dtype) for x in tables]
+        scratch=[pltpu.VMEM((UP_COEF + 7, AZ, NR), F32)] * 2
+        + [pltpu.SMEM(x.shape, x.dtype) for x in tables]
         + [pltpu.VMEM((n,) + block, F32) for n in (7, 12, 6)]
         + [pltpu.VMEM(c["dr"].shape, BF16), pltpu.SemaphoreType.DMA((7,))],
         vmem=VMEM_FULL,
     )
-    up, dn = shift(up, 1), shift(dn, -1)
+    near, far = neighbours(near, far)
     staged = [c[n] for n in ("mr", "mz", "dt", "wr", "wz")]
     shapes = [x.shape[1:] if n < 2 else x.shape for n, x in enumerate(staged)]
     *matrices, state, coef, mark = call(
@@ -797,7 +824,7 @@
     )
     packed, keep = call(
         launch,
-        [stress, state, up, dn, coef, mark, c["dr"], c["items"]],
+        [stress, state, far, near, coef, mark, c["dr"], c["items"]],
         [(8, 2 * FIELDS_IN, AZ, NR), (12,) + block],
         scratch=[pltpu.VMEM((2 * FIELDS_IN, 8, AZ, NR), F32)],
         micros=4,
@@ -805,13 +832,13 @@
     packed = lax.all_to_all(packed, "az", split_axis=0, concat_axis=0, tiled=True)
     (back,) = call(ring, [packed, ring_coef, mark] + matrices, [(8, 2 * FIELDS_OUT, AZ, NR)], micros=3)
     back = lax.all_to_all(back, "az", split_axis=0, concat_axis=0, tiled=True)
-    new, mid, up, dn = call(
+    new, mid, far, near = call(
         advance,
         [back, keep, coef],
         [(6,) + block, (6,) + block, (4, AZ, NR), (4, AZ, NR)],
         scratch=[pltpu.VMEM((20, 8, AZ, NR), F32)],
     )
-    up, dn = shift(up, 1), shift(dn, -1)
+    near, far = neighbours(near, far)
     v_out, s_part, m_out, edge = call(
         settle,
         [back, new, mid, velocity, stress, memory, coef, mark, c["dr"]],
@@ -821,7 +848,7 @@
     )
     (s_out,) = call(
         close,
-        [s_part, edge, up, dn, coef],
+        [s_part, edge, far, near, coef],
         [(7,) + block],
         hbm=(0,),
         scratch=[pltpu.VMEM((7, 5, AZ, NR), F32), pltpu.SemaphoreType.DMA((2,))],

time: 101 us -> 101 us (level)
  the two profiles are of different devices: /device:TPU:47 before, /device:TPU:49 now
where the time goes in v6:
time: 101 us; the launch traced here: 100 us
  blocking collectives  70.7 us (70%)
  starting transfers between devices  13.5 us (13%)
  Pallas kernels  11.8 us (12%)
  local copies, waits for them, and re-layouts  2.7 us (3%)
  between operations  1.46 us (1%)
    all_to_all x1, blocking collectives, on_device(): lax.all_to_all(packed, 'az', split_axis=0, concat_axis=0, tiled=True)  42 us
    all_to_all x1, blocking collectives, on_device(): back = lax.all_to_all(back, 'az', split_axis=0, concat_axis=0, tiled=True)  28.7 us
    ppermute x4, starting transfers between devices, swap(): lax.ppermute(value, 'depth', [p for i in lows for p in ((i, i + 1), (i +...  13.5 us
    pallas_call x7, Pallas kernels, call(): pl.pallas_call(body, out_shape=[jax.ShapeDtypeStruct(x, t) for x, t in zi...  11.8 us
    unnamed x24, local copies, waits for them, and re-layouts  2.7 us
  transfers between devices with their start and end apart: 4, of which 0 were waited for; matrix products, arithmetic and copies ran while one was open for 0% of the time, Pallas kernels for 2%

profile of v6, /device:TPU:49, one launch (start us, length us, event | category | flops | bytes accessed | tf_op | source)
XLA Modules:
  0.0 100.2 jit_solution(13525190100106272761)
XLA Ops:
  0.6 0.0 copy-start.6
  0.6 0.0 copy-start.7
  0.7 0.0 copy-start.8
  0.7 0.0 copy-start.9
  0.7 3.1 %prepare.1 = (f32[208,8,128]{2,1,0:T(8,128)}, f32[59,8,128]{2,1,0:T(8,128)}, f32[59,8,128]{2,1,0:T(8,128)}, f32[8,8,256]{2,1,0:T(8,128)}) custom-call(s32[4,32]{1,0:T(4,128)} %lids_hbm.1, f32[8,8]{1,0:T(8,128)} %mat_hbm.1, f32[8,9]{1,0:T(8,128)} %jkd_hbm.1, f32[7,16,8,128]{3,2,1,0:T(8,128)} %s.3, f32[12,16,8,128]{3,2,1,0:T(8,128)} %psi.1, ...), custom_call_target="tpu_custom_call" | custom-call | bytes 3000000 | tf_op jit(solution)/shard_map/prepare/pallas_call | solution.py:775
  3.8 3.7 %collective-permute-start = (f32[59,8,128]{2,1,0:T(8,128)}, f32[59,8,128]{2,1,0:T(8,128)S(1)}, u32[]{:S(2)}, u32[]{:S(2)}) collective-permute-start(f32[59,8,128]{2,1,0:T(8,128)} %get-tuple-element.27), channel_id=1, source_target_pairs={{8,16},{16,8},{24,32},{32,24},{40,48},{48,40},{56,64},{64,56},{72,... | collective-permute-start | bytes 725000 | tf_op jit(solution)/shard_map/ppermute | solution.py:790
  7.5 3.8 %collective-permute-start.1 = (f32[59,8,128]{2,1,0:T(8,128)}, f32[59,8,128]{2,1,0:T(8,128)S(1)}, u32[]{:S(2)}, u32[]{:S(2)}) collective-permute-start(f32[59,8,128]{2,1,0:T(8,128)} %get-tuple-element.28), channel_id=1, source_target_pairs={{0,8},{8,0},{16,24},{24,16},{32,40},{40,32},{48,56},{56,48},{64,72... | collective-permute-start | bytes 725000 | tf_op jit(solution)/shard_map/ppermute | solution.py:790
  11.9 0.0 copy-done.6
  12.0 0.0 copy-done.7
  12.0 0.0 copy-done.8
  12.0 0.0 copy-done.9
  12.0 0.0 copy-start.3
  12.0 1.1 %copy-done.3 = f32[208,8,128]{2,1,0:T(8,128)S(1)} copy-done((f32[208,8,128]{2,1,0:T(8,128)S(1)}, f32[208,8,128]{2,1,0:T(8,128)}, u32[]{:S(2)}) %copy-start.3) | copy-done | bytes 851992
  13.1 0.0 copy-start.11
  13.1 0.8 copy-done.11
  13.9 0.0 copy-start
  13.9 0.0 copy-start.4
  13.9 0.0 copy-start.5
  13.9 0.4 stage.1
  14.3 0.0 collective-permute-done.far
  14.3 0.0 collective-permute-done.1.near
  14.4 0.6 copy-done
  14.9 0.0 copy-done.4
  14.9 0.2 copy-done.5
  15.1 2.4 %launch.1 = (f32[8,36,8,128]{3,2,1,0:T(8,128)S(1)}, f32[12,16,8,128]{3,2,1,0:T(8,128)S(1)}) custom-call(f32[7,16,8,128]{3,2,1,0:T(8,128)S(1)} %copy-done, f32[192,8,128]{2,1,0:T(8,128)S(1)} %get-tuple-element.26.state, f32[59,8,128]{2,1,0:T(8,128)S(1)} %collective-permute-done.far, f32[59,8,128]{2,1,0:T(8,128)S(1)} %collective-permute-done.1.near, ...), custom_call_target="tpu_custom_call" | custom-call | bytes 12000000 | tf_op jit(solution)/shard_map/launch/pallas_call | solution.py:775
  17.5 0.0 copy-start.10
  17.5 42.0 %all_to_all.10.recv = f32[8,36,8,128]{3,2,1,0:T(8,128)S(1)} all-to-all(f32[8,36,8,128]{3,2,1,0:T(8,128)S(1)} %get-tuple-element.31), channel_id=1, replica_groups=mesh['depth'=64,'az'=8] {'az'}, dimensions={0} | all-to-all | bytes 2359296 | tf_op jit(solution)/shard_map/all_to_all | solution.py:832
  59.5 0.0 copy-done.10
  59.5 2.4 %ring.1 = f32[8,28,8,128]{3,2,1,0:T(8,128)S(1)} custom-call(f32[8,36,8,128]{3,2,1,0:T(8,128)S(1)} %all_to_all.10.recv, f32[8,8,256]{2,1,0:T(8,128)S(1)} %copy-done.10, f32[8,256]{1,0:T(8,128)S(1)} %get-tuple-element.30.mark, bf16[2,128,128]{2,1,0:T(8,128)(2,1)S(1)} %get-tuple-element.33.mr, bf16[2,256,256]{2,1,0:T(8,128)(2,1)S(1)} %get-tuple-element.34.mz, ...), custom_call_target="tpu_custom_call" | custom-call | bytes 9000000 | tf_op jit(solution)/shard_map/ring/pallas_call | solution.py:775
  61.9 28.7 %all_to_all.11.recv = f32[8,28,8,128]{3,2,1,0:T(8,128)S(1)} all-to-all(f32[8,28,8,128]{3,2,1,0:T(8,128)S(1)} %ring.1), channel_id=1, replica_groups=mesh['depth'=64,'az'=8] {'az'}, dimensions={0} | all-to-all | bytes 1835008 | tf_op jit(solution)/shard_map/all_to_all | solution.py:834
  90.6 0.0 copy-start.1
  90.6 0.0 copy-start.2
  90.6 1.0 %advance.1 = (f32[6,16,8,128]{3,2,1,0:T(8,128)S(1)}, f32[6,16,8,128]{3,2,1,0:T(8,128)S(1)}, f32[4,8,128]{2,1,0:T(8,128)S(1)}, f32[4,8,128]{2,1,0:T(8,128)S(1)}) custom-call(f32[8,28,8,128]{3,2,1,0:T(8,128)S(1)} %all_to_all.11.recv, f32[12,16,8,128]{3,2,1,0:T(8,128)S(1)} %get-tuple-element.38.keep, f32[16,8,128]{2,1,0:T(8,128)S(1)} %get-tuple-element.29.coef), custom_call_target="tpu_custom_call" | custom-call | bytes 3000000 | tf_op jit(solution)/shard_map/advance/pallas_call | solution.py:775
  91.7 1.9 %collective-permute-start.2 = (f32[4,8,128]{2,1,0:T(8,128)S(1)}, f32[4,8,128]{2,1,0:T(8,128)S(1)}, u32[]{:S(2)}, u32[]{:S(2)}) collective-permute-start(f32[4,8,128]{2,1,0:T(8,128)S(1)} %get-tuple-element.44), channel_id=1, source_target_pairs={{8,16},{16,8},{24,32},{32,24},{40,48},{48,40},{56,64},{64,56},{72,... | collective-permute-start | bytes 49160 | tf_op jit(solution)/shard_map/ppermute | solution.py:790
  93.6 4.1 %collective-permute-start.3 = (f32[4,8,128]{2,1,0:T(8,128)S(1)}, f32[4,8,128]{2,1,0:T(8,128)S(1)}, u32[]{:S(2)}, u32[]{:S(2)}) collective-permute-start(f32[4,8,128]{2,1,0:T(8,128)S(1)} %get-tuple-element.45), channel_id=1, source_target_pairs={{0,8},{8,0},{16,24},{24,16},{32,40},{40,32},{48,56},{56,48},{64,72... | collective-permute-start | bytes 49160 | tf_op jit(solution)/shard_map/ppermute | solution.py:790
  97.8 0.0 copy-done.1
  97.8 0.0 copy-done.2
  97.8 1.7 %settle.1 = (f32[6,16,8,128]{3,2,1,0:T(8,128)}, f32[7,16,8,128]{3,2,1,0:T(8,128)}, f32[12,16,8,128]{3,2,1,0:T(8,128)}, f32[7,5,8,128]{3,2,1,0:T(8,128)S(1)}) custom-call(f32[8,28,8,128]{3,2,1,0:T(8,128)S(1)} %all_to_all.11.recv, f32[6,16,8,128]{3,2,1,0:T(8,128)S(1)} %get-tuple-element.39.v2, f32[6,16,8,128]{3,2,1,0:T(8,128)S(1)} %get-tuple-element.40.mid, ...), custom_call_target="tpu_custom_call" | custom-call | bytes 9000000 | tf_op jit(solution)/shard_map/settle/pallas_call | solution.py:775
  99.5 0.0 collective-permute-done.2.far
  99.5 0.0 collective-permute-done.3.near
  99.5 0.7 close.1
Async XLA Ops:
  0.6 11.3 %copy-start.6 = (bf16[2,128,1024]{2,1,0:T(8,128)(2,1)S(1)}, bf16[2,128,1024]{2,1,0:T(8,128)(2,1)}, u32[]{:S(2)}) copy-start(bf16[2,128,1024]{2,1,0:T(8,128)(2,1)} %constant.19.clone.refs_5_) | copy-start | bytes 1572868
  0.6 11.3 %copy-start.7 = (bf16[2,2,128,512]{3,2,1,0:T(8,128)(2,1)S(1)}, bf16[2,2,128,512]{3,2,1,0:T(8,128)(2,1)}, u32[]{:S(2)}) copy-start(bf16[2,2,128,512]{3,2,1,0:T(8,128)(2,1)} %constant.18.clone.refs_4_) | copy-start | bytes 1572868
  0.7 11.3 %copy-start.8 = (bf16[2,2,256,256]{3,2,1,0:T(8,128)(2,1)S(1)}, bf16[2,2,256,256]{3,2,1,0:T(8,128)(2,1)}, u32[]{:S(2)}) copy-start(bf16[2,2,256,256]{3,2,1,0:T(8,128)(2,1)} %constant.16.clone.refs_2_) | copy-start | bytes 1572868
  0.7 11.3 %copy-start.9 = (bf16[2,2,128,128]{3,2,1,0:T(8,128)(2,1)S(1)}, bf16[2,2,128,128]{3,2,1,0:T(8,128)(2,1)}, u32[]{:S(2)}) copy-start(bf16[2,2,128,128]{3,2,1,0:T(8,128)(2,1)} %constant.15.clone.refs_1_) | copy-start | bytes 393220
  3.8 10.5 %collective-permute-start = (f32[59,8,128]{2,1,0:T(8,128)}, f32[59,8,128]{2,1,0:T(8,128)S(1)}, u32[]{:S(2)}, u32[]{:S(2)}) collective-permute-start(f32[59,8,128]{2,1,0:T(8,128)} %get-tuple-element.27), channel_id=1, source_target_pairs={{8,16},{16,8},{24,32},{32,24},{40,48},{48,40},{56,64},{64,56},{72,... | collective-permute-start | bytes 725000 | tf_op jit(solution)/shard_map/ppermute | solution.py:790
  7.5 6.9 %collective-permute-start.1 = (f32[59,8,128]{2,1,0:T(8,128)}, f32[59,8,128]{2,1,0:T(8,128)S(1)}, u32[]{:S(2)}, u32[]{:S(2)}) collective-permute-start(f32[59,8,128]{2,1,0:T(8,128)} %get-tuple-element.28), channel_id=1, source_target_pairs={{0,8},{8,0},{16,24},{24,16},{32,40},{40,32},{48,56},{56,48},{64,72... | collective-permute-start | bytes 725000 | tf_op jit(solution)/shard_map/ppermute | solution.py:790
  12.0 1.2 %copy-start.3 = (f32[208,8,128]{2,1,0:T(8,128)S(1)}, f32[208,8,128]{2,1,0:T(8,128)}, u32[]{:S(2)}) copy-start(f32[208,8,128]{2,1,0:T(8,128)} %get-tuple-element.25.refs_6_) | copy-start | bytes 2555908
  13.1 0.8 copy-start.11
  13.9 1.0 %copy-start = (f32[7,16,8,128]{3,2,1,0:T(8,128)S(1)}, f32[7,16,8,128]{3,2,1,0:T(8,128)}, u32[]{:S(2)}) copy-start(f32[7,16,8,128]{3,2,1,0:T(8,128)} %s.3) | copy-start | bytes 1376260
  13.9 1.0 %copy-start.4 = (bf16[2,128,128]{2,1,0:T(8,128)(2,1)S(1)}, bf16[2,128,128]{2,1,0:T(8,128)(2,1)}, u32[]{:S(2)}) copy-start(bf16[2,128,128]{2,1,0:T(8,128)(2,1)} %constant.14.clone.dr_hbm.dr_m) | copy-start | bytes 196612
  13.9 1.2 %copy-start.5 = (bf16[2,1024,128]{2,1,0:T(8,128)(2,1)S(1)}, bf16[2,1024,128]{2,1,0:T(8,128)(2,1)}, u32[]{:S(2)}) copy-start(bf16[2,1024,128]{2,1,0:T(8,128)(2,1)} %constant.20.clone.items) | copy-start | bytes 1572868
  17.5 42.0 %copy-start.10 = (f32[8,8,256]{2,1,0:T(8,128)S(1)}, f32[8,8,256]{2,1,0:T(8,128)}, u32[]{:S(2)}) copy-start(f32[8,8,256]{2,1,0:T(8,128)} %get-tuple-element.32.coef) | copy-start | bytes 196612
  90.6 7.1 %copy-start.1 = (f32[12,16,8,128]{3,2,1,0:T(8,128)S(1)}, f32[12,16,8,128]{3,2,1,0:T(8,128)}, u32[]{:S(2)}) copy-start(f32[12,16,8,128]{3,2,1,0:T(8,128)} %psi.1) | copy-start | bytes 2359300
  90.6 7.1 %copy-start.2 = (f32[6,16,8,128]{3,2,1,0:T(8,128)S(1)}, f32[6,16,8,128]{3,2,1,0:T(8,128)}, u32[]{:S(2)}) copy-start(f32[6,16,8,128]{3,2,1,0:T(8,128)} %v.1) | copy-start | bytes 1179652
  91.7 7.9 %collective-permute-start.2 = (f32[4,8,128]{2,1,0:T(8,128)S(1)}, f32[4,8,128]{2,1,0:T(8,128)S(1)}, u32[]{:S(2)}, u32[]{:S(2)}) collective-permute-start(f32[4,8,128]{2,1,0:T(8,128)S(1)} %get-tuple-element.44), channel_id=1, source_target_pairs={{8,16},{16,8},{24,32},{32,24},{40,48},{48,40},{56,64},{64,56},{72,... | collective-permute-start | bytes 49160 | tf_op jit(solution)/shard_map/ppermute | solution.py:790
  93.6 5.9 %collective-permute-start.3 = (f32[4,8,128]{2,1,0:T(8,128)S(1)}, f32[4,8,128]{2,1,0:T(8,128)S(1)}, u32[]{:S(2)}, u32[]{:S(2)}) collective-permute-start(f32[4,8,128]{2,1,0:T(8,128)S(1)} %get-tuple-element.45), channel_id=1, source_target_pairs={{0,8},{8,0},{16,24},{24,16},{32,40},{40,32},{48,56},{56,48},{64,72... | collective-permute-start | bytes 49160 | tf_op jit(solution)/shard_map/ppermute | solution.py:790

commit v7 on v6

--- a/solution.py
+++ b/solution.py
@@ -88,8 +88,10 @@
             if k:
                 items[s, GROUP * k - 4 : GROUP * k, k, 2 * s + 1] = ROW[4, :4]
     c["items"] = halves(items.reshape(8 * NR, 128))
-    c["dt"] = halves(azimuth_operator())
-    c["mr"] = np.stack([halves(np.kron(np.eye(8), line_operator(16, first).T)) for first in (False, True)])
+    azimuth = np.zeros((128, 128))
+    azimuth[:NT, :NT] = azimuth_operator()
+    small = [np.kron(np.eye(8), line_operator(16, first).T) for first in (False, True)] + [azimuth]
+    c["mr"] = np.stack([halves(m) for m in small])
     c["mz"] = np.stack([halves(np.kron(line_operator(16, first).T, np.eye(16))) for first in (False, True)])
     spread = np.zeros((2, 16))
     spread[0, 12:] = ROW[:4, 4]
@@ -245,13 +247,13 @@
 
 
 def prepare(
-    lids_hbm, mat_hbm, jkd_hbm, s_hbm, psi_hbm, v_hbm, dr_hbm,
+    lids_hbm, mat_hbm, jkd_hbm, s_hbm, dr_hbm, v_hbm, psi_hbm,
     state, far, near, ring_coef,
-    up, dn, lids, mat, jkd, s, psi, v, dr_m, sems,
+    up, dn, lids, mat, jkd, s, dr_m, v, psi, sems,
 ):
     pairs = (
-        (lids_hbm, lids), (mat_hbm, mat), (jkd_hbm, jkd), (s_hbm, s), (psi_hbm, psi),
-        (v_hbm, v), (dr_hbm, dr_m),
+        (lids_hbm, lids), (mat_hbm, mat), (jkd_hbm, jkd), (s_hbm, s), (dr_hbm, dr_m),
+        (v_hbm, v), (psi_hbm, psi),
     )
     copies = [pltpu.make_async_copy(a, b, sems.at[i]) for i, (a, b) in enumerate(pairs)]
     for copy in copies:
@@ -287,7 +289,7 @@
     cv, cf, cr, fric = [sp(c[n]) for n in ("cv", "cf", "cr", "fric")]
     weights = [sp(w) for w in c["weights"]]
     decayed = [sp(w * d) for w, d in zip(c["weights"], c["decay"])]
-    for copy in copies[3:]:
+    for copy in copies[3:5]:
         copy.wait()
     rr, tt, zz, rt, rz, tz, p = [s[f] for f in range(7)]
     stacked = jnp.concatenate([flat(x) for x in (rr, rt, rz, p)], axis=0)
@@ -300,7 +302,8 @@
     ]
     div = [r_rr + z_rz + q * (rr - tt), r_rt + z_tz + 2.0 * q * rt, r_rz + z_zz + q * rz]
     grads = (r_p, None, z_p)
-    new = []
+    for copy in copies[5:]:
+        copy.wait()
     for i in range(3):
         memory = [psi[3 * l + i] for l in range(4)]
         total = sum(w * m for w, m in zip(weights, memory))
@@ -353,20 +356,21 @@
     return jnp.where(even, y, x), jnp.where(even, x, y)
 
 
-def stage(*refs):
-    src, *pairs, mark, sems = refs
-    count = 6
-    first_r = jnp.where(lax.axis_index("az") == 0, 1, 0)
-    first_z = jnp.where(lax.axis_index("depth") == 0, 1, 0)
-    sources = list(pairs[:count])
-    sources[0] = sources[0].at[first_r]
-    sources[1] = sources[1].at[first_z]
-    state = sources.pop()
-    sources += [state.at[0:COEF], state.at[COEF:]]
-    copies = [pltpu.make_async_copy(a, b, sems.at[i]) for i, (a, b) in enumerate(zip(sources, pairs[count:]))]
+def stage(src, mr_in, mz_in, wr_in, wz_in, state_in, mr, mz, dt_m, wr, wz, state, coef, mark, sems):
+    device = lax.axis_index("depth")
+    pairs = (
+        (state_in.at[0:COEF], state),
+        (state_in.at[COEF:], coef),
+        (mr_in.at[jnp.where(lax.axis_index("az") == 0, 1, 0)], mr),
+        (mz_in.at[jnp.where(device == 0, 1, 0)], mz),
+        (mr_in.at[2], dt_m),
+        (wr_in, wr),
+        (wz_in, wz),
+    )
+    copies = [pltpu.make_async_copy(a, b, sems.at[i]) for i, (a, b) in enumerate(pairs)]
     for copy in copies:
         copy.start()
-    mark[...] = jnp.full((8, 256), (src[0] - PLANES * lax.axis_index("depth")).astype(F32), F32)
+    mark[...] = jnp.full((8, 256), (src[0] - PLANES * device).astype(F32), F32)
     for copy in copies:
         copy.wait()
 
@@ -536,10 +540,12 @@
     def field(f):
         return jnp.concatenate([recv[:, 2 * f], recv[:, 2 * f + 1]], axis=-1)
 
+    dt_h, dt_l = dt_m[0, :NT, :NT], dt_m[1, :NT, :NT]
+
     def az(fields):
         x = jnp.concatenate([y.reshape(NT, -1) for y in fields], axis=1)
         xh, xl = parts(x)
-        y = dot(dt_m[0], xh) + dot(dt_m[0], xl) + dot(dt_m[1], xh)
+        y = dot(dt_h, xh) + dot(dt_h, xl) + dot(dt_l, xh)
         res, at = [], 0
         for f in fields:
             n = f.shape[-1]
@@ -683,9 +689,13 @@
     outgoing(jnp.stack(up), jnp.stack(dn), near, far)
 
 
-def settle(recv, v2, mid, v, s, psi, coef, mark, dr_m, v_out, s_out, m_out, edge, hold):
+def settle(recv, v2, mid, v, s, psi, coef, mark, dr_m, v_hbm, s_hbm, m_hbm, edge, hold, s_out, m_out, sems):
+    copies = [
+        pltpu.make_async_copy(a, b, sems.at[i])
+        for i, (a, b) in enumerate(((v2, v_hbm), (m_out, m_hbm), (s_out, s_hbm)))
+    ]
+    copies[0].start()
     field = unpack(recv, hold, 10, 4)
-    v_out[...] = v2[...]
     has_below = coef[FLAGS]
     c = {name: coef[n] for n, name in enumerate(OWN)}
     q = inverse_radius(0, NR)
@@ -701,6 +711,7 @@
         second = w2 - w1 + omega * w2
         for l in range(4):
             m_out[3 * l + i] = decay[l] * (decay[l] * (psi[3 * l + i] + first) + second)
+    copies[1].start()
     sums = [mid[i] + v2[i] for i in range(6)]
     zero = jnp.zeros((1, 8, NR), F32)
     z_r, z_t, z_z, z_w = [
@@ -733,6 +744,9 @@
         s_out[f] = x
         edge[f, 0] = x[0]
         edge[f, 1:] = x[12:]
+    copies[2].start()
+    for copy in copies:
+        copy.wait()
 
 
 def close(s_in, edge, far, near, coef, s_out, new, sems):
@@ -768,7 +782,7 @@
         copy.wait()
 
 
-def call(body, inputs, shapes, types=None, hbm=(), smem=(), scratch=(), out_hbm=False, alias=None, micros=1, vmem=VMEM_LIMIT):
+def call(body, inputs, shapes, types=None, hbm=(), smem=(), scratch=(), out_hbm=(), alias=None, micros=1, vmem=VMEM_LIMIT):
     def space(i):
         return pltpu.HBM if i in hbm else pltpu.SMEM if i in smem else pltpu.VMEM
 
@@ -776,7 +790,7 @@
         body,
         out_shape=[jax.ShapeDtypeStruct(x, t) for x, t in zip(shapes, types or [F32] * len(shapes))],
         in_specs=[pl.BlockSpec(memory_space=space(i)) for i in range(len(inputs))],
-        out_specs=[pl.BlockSpec(memory_space=pltpu.HBM if out_hbm else pltpu.VMEM) for _ in shapes],
+        out_specs=[pl.BlockSpec(memory_space=pltpu.HBM if i in out_hbm else pltpu.VMEM) for i in range(len(shapes))],
         scratch_shapes=list(scratch),
         input_output_aliases=alias or {},
         compiler_params=pltpu.CompilerParams(vmem_limit_bytes=vmem),
@@ -801,24 +815,25 @@
     tables = [layer_ids, materials, jkd]
     state, far, near, ring_coef = call(
         prepare,
-        tables + [stress, memory, velocity, c["dr"]],
+        tables + [stress, c["dr"], velocity, memory],
         [(COEF + FLAGS + 2, AZ, NR), (UP_COEF + 7, AZ, NR), (UP_COEF + 7, AZ, NR), (len(RING), 8, 256)],
         hbm=range(7),
         scratch=[pltpu.VMEM((UP_COEF + 7, AZ, NR), F32)] * 2
         + [pltpu.SMEM(x.shape, x.dtype) for x in tables]
-        + [pltpu.VMEM((n,) + block, F32) for n in (7, 12, 6)]
-        + [pltpu.VMEM(c["dr"].shape, BF16), pltpu.SemaphoreType.DMA((7,))],
+        + [pltpu.VMEM((7,) + block, F32), pltpu.VMEM(c["dr"].shape, BF16)]
+        + [pltpu.VMEM((n,) + block, F32) for n in (6, 12)]
+        + [pltpu.SemaphoreType.DMA((7,))],
         vmem=VMEM_FULL,
     )
     near, far = neighbours(near, far)
-    staged = [c[n] for n in ("mr", "mz", "dt", "wr", "wz")]
-    shapes = [x.shape[1:] if n < 2 else x.shape for n, x in enumerate(staged)]
+    staged = [c[n] for n in ("mr", "mz", "wr", "wz")]
+    shapes = [c[n].shape[1:] for n in ("mr", "mz", "mr")] + [c["wr"].shape, c["wz"].shape]
     *matrices, state, coef, mark = call(
         stage,
         [source_depth] + staged + [state],
         shapes + [(COEF, AZ, NR), (FLAGS + 2, AZ, NR), (8, 256)],
         types=[BF16] * 5 + [F32] * 3,
-        hbm=range(1, 7),
+        hbm=range(1, 6),
         smem=(0,),
         scratch=[pltpu.SemaphoreType.DMA((7,))],
     )
@@ -843,7 +858,10 @@
         settle,
         [back, new, mid, velocity, stress, memory, coef, mark, c["dr"]],
         [(6,) + block, (7,) + block, (12,) + block, (7, 5, AZ, NR)],
-        scratch=[pltpu.VMEM((8, 8, AZ, NR), F32)],
+        scratch=[pltpu.VMEM((8, 8, AZ, NR), F32)]
+        + [pltpu.VMEM((n,) + block, F32) for n in (7, 12)]
+        + [pltpu.SemaphoreType.DMA((3,))],
+        out_hbm=range(3),
         micros=3,
     )
     (s_out,) = call(
@@ -852,7 +870,7 @@
         [(7,) + block],
         hbm=(0,),
         scratch=[pltpu.VMEM((7, 5, AZ, NR), F32), pltpu.SemaphoreType.DMA((2,))],
-        out_hbm=True,
+        out_hbm=(0,),
         alias={0: 0},
     )
     return v_out, s_out, m_out

time: 101 us -> 101 us (level)
  the two profiles are of different devices: /device:TPU:49 before, /device:TPU:41 now
where the time goes in v7:
time: 101 us; the launch traced here: 100 us
  blocking collectives  70 us (69%)
  starting transfers between devices  14.1 us (14%)
  Pallas kernels  11.7 us (12%)
  local copies, waits for them, and re-layouts  2.82 us (3%)
  between operations  1.47 us (1%)
    all_to_all x1, blocking collectives, on_device(): lax.all_to_all(packed, 'az', split_axis=0, concat_axis=0, tiled=True)  42 us
    all_to_all x1, blocking collectives, on_device(): back = lax.all_to_all(back, 'az', split_axis=0, concat_axis=0, tiled=True)  28 us
    ppermute x4, starting transfers between devices, swap(): lax.ppermute(value, 'depth', [p for i in lows for p in ((i, i + 1), (i +...  14.1 us
    pallas_call x7, Pallas kernels, call(): pl.pallas_call(body, out_shape=[jax.ShapeDtypeStruct(x, t) for x, t in zi...  11.7 us
    unnamed x22, local copies, waits for them, and re-layouts  2.82 us
  transfers between devices with their start and end apart: 4, of which 0 were waited for; matrix products, arithmetic and copies ran while one was open for 0% of the time, Pallas kernels for 2%

profile of v7, /device:TPU:41, one launch (start us, length us, event | category | flops | bytes accessed | tf_op | source)
XLA Modules:
  0.0 100.1 jit_solution(2477089814707613439)
XLA Ops:
  0.6 0.0 copy-start.6
  0.6 0.0 copy-start.7
  0.7 0.0 copy-start.8
  0.7 2.8 %prepare.1 = (f32[208,8,128]{2,1,0:T(8,128)}, f32[59,8,128]{2,1,0:T(8,128)}, f32[59,8,128]{2,1,0:T(8,128)}, f32[8,8,256]{2,1,0:T(8,128)}) custom-call(s32[4,32]{1,0:T(4,128)} %lids_hbm.1, f32[8,8]{1,0:T(8,128)} %mat_hbm.1, f32[8,9]{1,0:T(8,128)} %jkd_hbm.1, f32[7,16,8,128]{3,2,1,0:T(8,128)} %s.3, bf16[2,128,128]{2,1,0:T(8,128)(2,1)} %constant.12.clone.dr_hbm.dr_m, ...), custom_call_target="tpu_custom_call" | custom-call | bytes 3000000 | tf_op jit(solution)/shard_map/prepare/pallas_call | solution.py:789
  3.5 3.7 %collective-permute-start = (f32[59,8,128]{2,1,0:T(8,128)}, f32[59,8,128]{2,1,0:T(8,128)S(1)}, u32[]{:S(2)}, u32[]{:S(2)}) collective-permute-start(f32[59,8,128]{2,1,0:T(8,128)} %get-tuple-element.27), channel_id=1, source_target_pairs={{8,16},{16,8},{24,32},{32,24},{40,48},{48,40},{56,64},{64,56},{72,... | collective-permute-start | bytes 725000 | tf_op jit(solution)/shard_map/ppermute | solution.py:804
  7.2 3.8 %collective-permute-start.1 = (f32[59,8,128]{2,1,0:T(8,128)}, f32[59,8,128]{2,1,0:T(8,128)S(1)}, u32[]{:S(2)}, u32[]{:S(2)}) collective-permute-start(f32[59,8,128]{2,1,0:T(8,128)} %get-tuple-element.28), channel_id=1, source_target_pairs={{0,8},{8,0},{16,24},{24,16},{32,40},{40,32},{48,56},{56,48},{64,72... | collective-permute-start | bytes 725000 | tf_op jit(solution)/shard_map/ppermute | solution.py:804
  11.7 0.0 copy-done.6
  11.7 0.0 copy-done.7
  11.7 0.0 copy-done.8
  11.7 0.0 copy-start.3
  11.7 1.1 %copy-done.3 = f32[208,8,128]{2,1,0:T(8,128)S(1)} copy-done((f32[208,8,128]{2,1,0:T(8,128)S(1)}, f32[208,8,128]{2,1,0:T(8,128)}, u32[]{:S(2)}) %copy-start.3) | copy-done | bytes 851992
  12.8 0.0 copy-start.9
  12.9 0.9 copy-done.9
  13.8 0.0 copy-start
  13.8 0.0 copy-start.4
  13.8 0.0 copy-start.5
  13.8 0.5 stage.1
  14.3 0.0 collective-permute-done.far
  14.3 0.0 collective-permute-done.1.near
  14.3 0.5 copy-done
  14.8 0.0 copy-done.4
  14.8 0.2 copy-done.5
  15.0 2.4 %launch.1 = (f32[8,36,8,128]{3,2,1,0:T(8,128)S(1)}, f32[12,16,8,128]{3,2,1,0:T(8,128)S(1)}) custom-call(f32[7,16,8,128]{3,2,1,0:T(8,128)S(1)} %copy-done, f32[192,8,128]{2,1,0:T(8,128)S(1)} %get-tuple-element.26.state, f32[59,8,128]{2,1,0:T(8,128)S(1)} %collective-permute-done.far, f32[59,8,128]{2,1,0:T(8,128)S(1)} %collective-permute-done.1.near, ...), custom_call_target="tpu_custom_call" | custom-call | bytes 12000000 | tf_op jit(solution)/shard_map/launch/pallas_call | solution.py:789
  17.4 0.0 copy-start.10
  17.4 42.0 %all_to_all.10.recv = f32[8,36,8,128]{3,2,1,0:T(8,128)S(1)} all-to-all(f32[8,36,8,128]{3,2,1,0:T(8,128)S(1)} %get-tuple-element.31), channel_id=1, replica_groups=mesh['depth'=64,'az'=8] {'az'}, dimensions={0} | all-to-all | bytes 2359296 | tf_op jit(solution)/shard_map/all_to_all | solution.py:847
  59.4 0.0 copy-done.10
  59.4 2.4 %ring.1 = f32[8,28,8,128]{3,2,1,0:T(8,128)S(1)} custom-call(f32[8,36,8,128]{3,2,1,0:T(8,128)S(1)} %all_to_all.10.recv, f32[8,8,256]{2,1,0:T(8,128)S(1)} %copy-done.10, f32[8,256]{1,0:T(8,128)S(1)} %get-tuple-element.30.mark, bf16[2,128,128]{2,1,0:T(8,128)(2,1)S(1)} %get-tuple-element.33.mr, bf16[2,256,256]{2,1,0:T(8,128)(2,1)S(1)} %get-tuple-element.34.mz, ...), custom_call_target="tpu_custom_call" | custom-call | bytes 9000000 | tf_op jit(solution)/shard_map/ring/pallas_call | solution.py:789
  61.8 28.0 %all_to_all.11.recv = f32[8,28,8,128]{3,2,1,0:T(8,128)S(1)} all-to-all(f32[8,28,8,128]{3,2,1,0:T(8,128)S(1)} %ring.1), channel_id=1, replica_groups=mesh['depth'=64,'az'=8] {'az'}, dimensions={0} | all-to-all | bytes 1835008 | tf_op jit(solution)/shard_map/all_to_all | solution.py:849
  89.8 0.0 copy-start.1
  89.8 0.0 copy-start.2
  89.8 1.0 %advance.1 = (f32[6,16,8,128]{3,2,1,0:T(8,128)S(1)}, f32[6,16,8,128]{3,2,1,0:T(8,128)S(1)}, f32[4,8,128]{2,1,0:T(8,128)S(1)}, f32[4,8,128]{2,1,0:T(8,128)S(1)}) custom-call(f32[8,28,8,128]{3,2,1,0:T(8,128)S(1)} %all_to_all.11.recv, f32[12,16,8,128]{3,2,1,0:T(8,128)S(1)} %get-tuple-element.38.keep, f32[16,8,128]{2,1,0:T(8,128)S(1)} %get-tuple-element.29.coef), custom_call_target="tpu_custom_call" | custom-call | bytes 3000000 | tf_op jit(solution)/shard_map/advance/pallas_call | solution.py:789
  90.8 1.9 %collective-permute-start.2 = (f32[4,8,128]{2,1,0:T(8,128)S(1)}, f32[4,8,128]{2,1,0:T(8,128)S(1)}, u32[]{:S(2)}, u32[]{:S(2)}) collective-permute-start(f32[4,8,128]{2,1,0:T(8,128)S(1)} %get-tuple-element.44), channel_id=1, source_target_pairs={{8,16},{16,8},{24,32},{32,24},{40,48},{48,40},{56,64},{64,56},{72,... | collective-permute-start | bytes 49160 | tf_op jit(solution)/shard_map/ppermute | solution.py:804
  92.8 4.7 %collective-permute-start.3 = (f32[4,8,128]{2,1,0:T(8,128)S(1)}, f32[4,8,128]{2,1,0:T(8,128)S(1)}, u32[]{:S(2)}, u32[]{:S(2)}) collective-permute-start(f32[4,8,128]{2,1,0:T(8,128)S(1)} %get-tuple-element.45), channel_id=1, source_target_pairs={{0,8},{8,0},{16,24},{24,16},{32,40},{40,32},{48,56},{56,48},{64,72... | collective-permute-start | bytes 49160 | tf_op jit(solution)/shard_map/ppermute | solution.py:804
  97.5 0.0 copy-done.1
  97.5 0.0 copy-done.2
  97.5 1.9 %settle.1 = (f32[6,16,8,128]{3,2,1,0:T(8,128)}, f32[7,16,8,128]{3,2,1,0:T(8,128)}, f32[12,16,8,128]{3,2,1,0:T(8,128)}, f32[7,5,8,128]{3,2,1,0:T(8,128)S(1)}) custom-call(f32[8,28,8,128]{3,2,1,0:T(8,128)S(1)} %all_to_all.11.recv, f32[6,16,8,128]{3,2,1,0:T(8,128)S(1)} %get-tuple-element.39.v2, f32[6,16,8,128]{3,2,1,0:T(8,128)S(1)} %get-tuple-element.40.mid, ...), custom_call_target="tpu_custom_call" | custom-call | bytes 9000000 | tf_op jit(solution)/shard_map/settle/pallas_call | solution.py:789
  99.4 0.0 collective-permute-done.2.far
  99.4 0.0 collective-permute-done.3.near
  99.4 0.7 close.1
Async XLA Ops:
  0.6 11.0 %copy-start.6 = (bf16[2,128,1024]{2,1,0:T(8,128)(2,1)S(1)}, bf16[2,128,1024]{2,1,0:T(8,128)(2,1)}, u32[]{:S(2)}) copy-start(bf16[2,128,1024]{2,1,0:T(8,128)(2,1)} %constant.16.clone.wz_in) | copy-start | bytes 1572868
  0.6 11.0 %copy-start.7 = (bf16[2,2,128,512]{3,2,1,0:T(8,128)(2,1)S(1)}, bf16[2,2,128,512]{3,2,1,0:T(8,128)(2,1)}, u32[]{:S(2)}) copy-start(bf16[2,2,128,512]{3,2,1,0:T(8,128)(2,1)} %constant.15.clone.wr_in) | copy-start | bytes 1572868
  0.7 11.0 %copy-start.8 = (bf16[2,2,256,256]{3,2,1,0:T(8,128)(2,1)S(1)}, bf16[2,2,256,256]{3,2,1,0:T(8,128)(2,1)}, u32[]{:S(2)}) copy-start(bf16[2,2,256,256]{3,2,1,0:T(8,128)(2,1)} %constant.14.clone.mz_in) | copy-start | bytes 1572868
  3.5 10.7 %collective-permute-start = (f32[59,8,128]{2,1,0:T(8,128)}, f32[59,8,128]{2,1,0:T(8,128)S(1)}, u32[]{:S(2)}, u32[]{:S(2)}) collective-permute-start(f32[59,8,128]{2,1,0:T(8,128)} %get-tuple-element.27), channel_id=1, source_target_pairs={{8,16},{16,8},{24,32},{32,24},{40,48},{48,40},{56,64},{64,56},{72,... | collective-permute-start | bytes 725000 | tf_op jit(solution)/shard_map/ppermute | solution.py:804
  7.2 7.1 %collective-permute-start.1 = (f32[59,8,128]{2,1,0:T(8,128)}, f32[59,8,128]{2,1,0:T(8,128)S(1)}, u32[]{:S(2)}, u32[]{:S(2)}) collective-permute-start(f32[59,8,128]{2,1,0:T(8,128)} %get-tuple-element.28), channel_id=1, source_target_pairs={{0,8},{8,0},{16,24},{24,16},{32,40},{40,32},{48,56},{56,48},{64,72... | collective-permute-start | bytes 725000 | tf_op jit(solution)/shard_map/ppermute | solution.py:804
  11.7 1.2 %copy-start.3 = (f32[208,8,128]{2,1,0:T(8,128)S(1)}, f32[208,8,128]{2,1,0:T(8,128)}, u32[]{:S(2)}) copy-start(f32[208,8,128]{2,1,0:T(8,128)} %get-tuple-element.25.state_in) | copy-start | bytes 2555908
  12.8 0.9 copy-start.9
  13.8 1.0 %copy-start = (f32[7,16,8,128]{3,2,1,0:T(8,128)S(1)}, f32[7,16,8,128]{3,2,1,0:T(8,128)}, u32[]{:S(2)}) copy-start(f32[7,16,8,128]{3,2,1,0:T(8,128)} %s.3) | copy-start | bytes 1376260
  13.8 1.0 %copy-start.4 = (bf16[2,128,128]{2,1,0:T(8,128)(2,1)S(1)}, bf16[2,128,128]{2,1,0:T(8,128)(2,1)}, u32[]{:S(2)}) copy-start(bf16[2,128,128]{2,1,0:T(8,128)(2,1)} %constant.12.clone.dr_hbm.dr_m) | copy-start | bytes 196612
  13.8 1.2 %copy-start.5 = (bf16[2,1024,128]{2,1,0:T(8,128)(2,1)S(1)}, bf16[2,1024,128]{2,1,0:T(8,128)(2,1)}, u32[]{:S(2)}) copy-start(bf16[2,1024,128]{2,1,0:T(8,128)(2,1)} %constant.17.clone.items) | copy-start | bytes 1572868
  17.4 42.0 %copy-start.10 = (f32[8,8,256]{2,1,0:T(8,128)S(1)}, f32[8,8,256]{2,1,0:T(8,128)}, u32[]{:S(2)}) copy-start(f32[8,8,256]{2,1,0:T(8,128)} %get-tuple-element.32.coef) | copy-start | bytes 196612
  89.8 7.7 %copy-start.1 = (f32[12,16,8,128]{3,2,1,0:T(8,128)S(1)}, f32[12,16,8,128]{3,2,1,0:T(8,128)}, u32[]{:S(2)}) copy-start(f32[12,16,8,128]{3,2,1,0:T(8,128)} %psi.1) | copy-start | bytes 2359300
  89.8 7.7 %copy-start.2 = (f32[6,16,8,128]{3,2,1,0:T(8,128)S(1)}, f32[6,16,8,128]{3,2,1,0:T(8,128)}, u32[]{:S(2)}) copy-start(f32[6,16,8,128]{3,2,1,0:T(8,128)} %v.1) | copy-start | bytes 1179652
  90.8 8.6 %collective-permute-start.2 = (f32[4,8,128]{2,1,0:T(8,128)S(1)}, f32[4,8,128]{2,1,0:T(8,128)S(1)}, u32[]{:S(2)}, u32[]{:S(2)}) collective-permute-start(f32[4,8,128]{2,1,0:T(8,128)S(1)} %get-tuple-element.44), channel_id=1, source_target_pairs={{8,16},{16,8},{24,32},{32,24},{40,48},{48,40},{56,64},{64,56},{72,... | collective-permute-start | bytes 49160 | tf_op jit(solution)/shard_map/ppermute | solution.py:804
  92.8 6.6 %collective-permute-start.3 = (f32[4,8,128]{2,1,0:T(8,128)S(1)}, f32[4,8,128]{2,1,0:T(8,128)S(1)}, u32[]{:S(2)}, u32[]{:S(2)}) collective-permute-start(f32[4,8,128]{2,1,0:T(8,128)S(1)} %get-tuple-element.45), channel_id=1, source_target_pairs={{0,8},{8,0},{16,24},{24,16},{32,40},{40,32},{48,56},{56,48},{64,72... | collective-permute-start | bytes 49160 | tf_op jit(solution)/shard_map/ppermute | solution.py:804

commit v8 on v7

--- a/solution.py
+++ b/solution.py
@@ -689,10 +689,10 @@
     outgoing(jnp.stack(up), jnp.stack(dn), near, far)
 
 
-def settle(recv, v2, mid, v, s, psi, coef, mark, dr_m, v_hbm, s_hbm, m_hbm, edge, hold, s_out, m_out, sems):
+def settle(recv, v2, mid, v, s, psi, coef, mark, dr_m, v_hbm, m_hbm, s_out, hold, m_out, sems):
     copies = [
         pltpu.make_async_copy(a, b, sems.at[i])
-        for i, (a, b) in enumerate(((v2, v_hbm), (m_out, m_hbm), (s_out, s_hbm)))
+        for i, (a, b) in enumerate(((v2, v_hbm), (m_out, m_hbm)))
     ]
     copies[0].start()
     field = unpack(recv, hold, 10, 4)
@@ -740,49 +740,47 @@
         source - (couple * div_v + sp(c["modulus"]) * div_w),
     ]
     for f, x in enumerate(updates):
-        x = s[f] + x
-        s_out[f] = x
-        edge[f, 0] = x[0]
-        edge[f, 1:] = x[12:]
-    copies[2].start()
+        s_out[f] = s[f] + x
     for copy in copies:
         copy.wait()
 
 
-def close(s_in, edge, far, near, coef, s_out, new, sems):
+def close(s, far, near, coef, s_out, new, sems):
+    inner = pltpu.make_async_copy(s.at[:, 1:12], s_out.at[:, 1:12], sems.at[2])
+    inner.start()
     up, dn = incoming(near, far)
     has_below = coef[FLAGS]
     c = {name: coef[n] for n, name in enumerate(OWN)}
 
-    def update(slot, row, z_r, z_t, z_z, z_w):
+    def update(slot, row, plane, z_r, z_t, z_z, z_w):
         def at(name):
             return jnp.broadcast_to(c[name][row : row + 1, :], (8, NR))
 
         bulk, couple, modulus, shear = at("bulk"), at("couple"), at("modulus"), at("shear")
         total = bulk * z_z + couple * z_w
-        new[0, slot] = edge[0, slot] + total
-        new[1, slot] = edge[1, slot] + total
-        new[2, slot] = edge[2, slot] + total + 2.0 * shear * z_z
-        new[3, slot] = edge[3, slot]
-        new[4, slot] = edge[4, slot] + shear * z_r
-        new[5, slot] = edge[5, slot] + shear * z_t
-        new[6, slot] = edge[6, slot] - (couple * z_z + modulus * z_w)
-
-    update(0, 2, *[has_below * up[i] for i in range(4)])
+        new[0, slot] = s[0, plane] + total
+        new[1, slot] = s[1, plane] + total
+        new[2, slot] = s[2, plane] + total + 2.0 * shear * z_z
+        new[3, slot] = s[3, plane]
+        new[4, slot] = s[4, plane] + shear * z_r
+        new[5, slot] = s[5, plane] + shear * z_t
+        new[6, slot] = s[6, plane] - (couple * z_z + modulus * z_w)
+
+    update(0, 2, 0, *[has_below * up[i] for i in range(4)])
     for slot in range(1, 5):
         weight = float(ROW[slot - 1, 4])
-        update(slot, 5, *[weight * dn[i] for i in range(4)])
+        update(slot, 5, 11 + slot, *[weight * dn[i] for i in range(4)])
     copies = [
         pltpu.make_async_copy(new.at[:, 0:1], s_out.at[:, 0:1], sems.at[0]),
         pltpu.make_async_copy(new.at[:, 1:5], s_out.at[:, 12:16], sems.at[1]),
     ]
     for copy in copies:
         copy.start()
-    for copy in copies:
+    for copy in copies + [inner]:
         copy.wait()
 
 
-def call(body, inputs, shapes, types=None, hbm=(), smem=(), scratch=(), out_hbm=(), alias=None, micros=1, vmem=VMEM_LIMIT):
+def call(body, inputs, shapes, types=None, hbm=(), smem=(), scratch=(), out_hbm=(), micros=1, vmem=VMEM_LIMIT):
     def space(i):
         return pltpu.HBM if i in hbm else pltpu.SMEM if i in smem else pltpu.VMEM
 
@@ -792,7 +790,6 @@
         in_specs=[pl.BlockSpec(memory_space=space(i)) for i in range(len(inputs))],
         out_specs=[pl.BlockSpec(memory_space=pltpu.HBM if i in out_hbm else pltpu.VMEM) for i in range(len(shapes))],
         scratch_shapes=list(scratch),
-        input_output_aliases=alias or {},
         compiler_params=pltpu.CompilerParams(vmem_limit_bytes=vmem),
         cost_estimate=pl.CostEstimate(flops=0, bytes_accessed=3 * 10**6 * micros, transcendentals=0),
         name=body.__name__,
@@ -854,24 +851,22 @@
         scratch=[pltpu.VMEM((20, 8, AZ, NR), F32)],
     )
     near, far = neighbours(near, far)
-    v_out, s_part, m_out, edge = call(
+    v_out, m_out, s_part = call(
         settle,
         [back, new, mid, velocity, stress, memory, coef, mark, c["dr"]],
-        [(6,) + block, (7,) + block, (12,) + block, (7, 5, AZ, NR)],
+        [(6,) + block, (12,) + block, (7,) + block],
         scratch=[pltpu.VMEM((8, 8, AZ, NR), F32)]
-        + [pltpu.VMEM((n,) + block, F32) for n in (7, 12)]
-        + [pltpu.SemaphoreType.DMA((3,))],
-        out_hbm=range(3),
+        + [pltpu.VMEM((n,) + block, F32) for n in (12,)]
+        + [pltpu.SemaphoreType.DMA((2,))],
+        out_hbm=range(2),
         micros=3,
     )
     (s_out,) = call(
         close,
-        [s_part, edge, far, near, coef],
+        [s_part, far, near, coef],
         [(7,) + block],
-        hbm=(0,),
-        scratch=[pltpu.VMEM((7, 5, AZ, NR), F32), pltpu.SemaphoreType.DMA((2,))],
+        scratch=[pltpu.VMEM((7, 5, AZ, NR), F32), pltpu.SemaphoreType.DMA((3,))],
         out_hbm=(0,),
-        alias={0: 0},
     )
     return v_out, s_out, m_out
 

time: 101 us -> 100 us (0.990)
  no operation moved by 1% of the time
where the time goes in v8:
time: 100 us
  blocking collectives  70 us (70%)
  starting transfers between devices  14.1 us (14%)
  Pallas kernels  11.6 us (12%)
  local copies, waits for them, and re-layouts  2.82 us (3%)
  between operations  1.47 us (1%)
    all_to_all x1, blocking collectives, on_device(): lax.all_to_all(packed, 'az', split_axis=0, concat_axis=0, tiled=True)  42 us
    all_to_all x1, blocking collectives, on_device(): back = lax.all_to_all(back, 'az', split_axis=0, concat_axis=0, tiled=True)  28 us
    ppermute x4, starting transfers between devices, swap(): lax.ppermute(value, 'depth', [p for i in lows for p in ((i, i + 1), (i +...  14.1 us
    pallas_call x7, Pallas kernels, call(): pl.pallas_call(body, out_shape=[jax.ShapeDtypeStruct(x, t) for x, t in zi...  11.6 us
    unnamed x22, local copies, waits for them, and re-layouts  2.82 us
  transfers between devices with their start and end apart: 4, of which 0 were waited for; matrix products, arithmetic and copies ran while one was open for 0% of the time, Pallas kernels for 2%

profile of v8, /device:TPU:41, one launch (start us, length us, event | category | flops | bytes accessed | tf_op | source)
XLA Modules:
  0.0 100.1 jit_solution(17264577721679197704)
XLA Ops:
  0.6 0.0 copy-start.6
  0.6 0.0 copy-start.7
  0.7 0.0 copy-start.8
  0.7 2.8 %prepare.1 = (f32[208,8,128]{2,1,0:T(8,128)}, f32[59,8,128]{2,1,0:T(8,128)}, f32[59,8,128]{2,1,0:T(8,128)}, f32[8,8,256]{2,1,0:T(8,128)}) custom-call(s32[4,32]{1,0:T(4,128)} %lids_hbm.1, f32[8,8]{1,0:T(8,128)} %mat_hbm.1, f32[8,9]{1,0:T(8,128)} %jkd_hbm.1, f32[7,16,8,128]{3,2,1,0:T(8,128)} %s.3, bf16[2,128,128]{2,1,0:T(8,128)(2,1)} %constant.12.clone.dr_hbm.dr_m, ...), custom_call_target="tpu_custom_call" | custom-call | bytes 3000000 | tf_op jit(solution)/shard_map/prepare/pallas_call | solution.py:787
  3.5 3.7 %collective-permute-start = (f32[59,8,128]{2,1,0:T(8,128)}, f32[59,8,128]{2,1,0:T(8,128)S(1)}, u32[]{:S(2)}, u32[]{:S(2)}) collective-permute-start(f32[59,8,128]{2,1,0:T(8,128)} %get-tuple-element.26), channel_id=1, source_target_pairs={{8,16},{16,8},{24,32},{32,24},{40,48},{48,40},{56,64},{64,56},{72,... | collective-permute-start | bytes 725000 | tf_op jit(solution)/shard_map/ppermute | solution.py:801
  7.2 3.8 %collective-permute-start.1 = (f32[59,8,128]{2,1,0:T(8,128)}, f32[59,8,128]{2,1,0:T(8,128)S(1)}, u32[]{:S(2)}, u32[]{:S(2)}) collective-permute-start(f32[59,8,128]{2,1,0:T(8,128)} %get-tuple-element.27), channel_id=1, source_target_pairs={{0,8},{8,0},{16,24},{24,16},{32,40},{40,32},{48,56},{56,48},{64,72... | collective-permute-start | bytes 725000 | tf_op jit(solution)/shard_map/ppermute | solution.py:801
  11.7 0.0 copy-done.6
  11.7 0.0 copy-done.7
  11.7 0.0 copy-done.8
  11.7 0.0 copy-start.3
  11.7 1.1 %copy-done.3 = f32[208,8,128]{2,1,0:T(8,128)S(1)} copy-done((f32[208,8,128]{2,1,0:T(8,128)S(1)}, f32[208,8,128]{2,1,0:T(8,128)}, u32[]{:S(2)}) %copy-start.3) | copy-done | bytes 851992
  12.8 0.0 copy-start.9
  12.9 0.9 copy-done.9
  13.8 0.0 copy-start
  13.8 0.0 copy-start.4
  13.8 0.0 copy-start.5
  13.8 0.5 stage.1
  14.3 0.0 collective-permute-done.far
  14.3 0.0 collective-permute-done.1.near
  14.3 0.5 copy-done
  14.8 0.0 copy-done.4
  14.8 0.2 copy-done.5
  15.0 2.4 %launch.1 = (f32[8,36,8,128]{3,2,1,0:T(8,128)S(1)}, f32[12,16,8,128]{3,2,1,0:T(8,128)S(1)}) custom-call(f32[7,16,8,128]{3,2,1,0:T(8,128)S(1)} %copy-done, f32[192,8,128]{2,1,0:T(8,128)S(1)} %get-tuple-element.25.state, f32[59,8,128]{2,1,0:T(8,128)S(1)} %collective-permute-done.far, f32[59,8,128]{2,1,0:T(8,128)S(1)} %collective-permute-done.1.near, ...), custom_call_target="tpu_custom_call" | custom-call | bytes 12000000 | tf_op jit(solution)/shard_map/launch/pallas_call | solution.py:787
  17.4 0.0 copy-start.10
  17.4 42.0 %all_to_all.10.recv = f32[8,36,8,128]{3,2,1,0:T(8,128)S(1)} all-to-all(f32[8,36,8,128]{3,2,1,0:T(8,128)S(1)} %get-tuple-element.30), channel_id=1, replica_groups=mesh['depth'=64,'az'=8] {'az'}, dimensions={0} | all-to-all | bytes 2359296 | tf_op jit(solution)/shard_map/all_to_all | solution.py:844
  59.4 0.0 copy-done.10
  59.4 2.4 %ring.1 = f32[8,28,8,128]{3,2,1,0:T(8,128)S(1)} custom-call(f32[8,36,8,128]{3,2,1,0:T(8,128)S(1)} %all_to_all.10.recv, f32[8,8,256]{2,1,0:T(8,128)S(1)} %copy-done.10, f32[8,256]{1,0:T(8,128)S(1)} %get-tuple-element.29.mark, bf16[2,128,128]{2,1,0:T(8,128)(2,1)S(1)} %get-tuple-element.32.mr, bf16[2,256,256]{2,1,0:T(8,128)(2,1)S(1)} %get-tuple-element.33.mz, ...), custom_call_target="tpu_custom_call" | custom-call | bytes 9000000 | tf_op jit(solution)/shard_map/ring/pallas_call | solution.py:787
  61.8 28.0 %all_to_all.11.recv = f32[8,28,8,128]{3,2,1,0:T(8,128)S(1)} all-to-all(f32[8,28,8,128]{3,2,1,0:T(8,128)S(1)} %ring.1), channel_id=1, replica_groups=mesh['depth'=64,'az'=8] {'az'}, dimensions={0} | all-to-all | bytes 1835008 | tf_op jit(solution)/shard_map/all_to_all | solution.py:846
  89.8 0.0 copy-start.1
  89.8 0.0 copy-start.2
  89.8 1.0 %advance.1 = (f32[6,16,8,128]{3,2,1,0:T(8,128)S(1)}, f32[6,16,8,128]{3,2,1,0:T(8,128)S(1)}, f32[4,8,128]{2,1,0:T(8,128)S(1)}, f32[4,8,128]{2,1,0:T(8,128)S(1)}) custom-call(f32[8,28,8,128]{3,2,1,0:T(8,128)S(1)} %all_to_all.11.recv, f32[12,16,8,128]{3,2,1,0:T(8,128)S(1)} %get-tuple-element.37.keep, f32[16,8,128]{2,1,0:T(8,128)S(1)} %get-tuple-element.28.coef), custom_call_target="tpu_custom_call" | custom-call | bytes 3000000 | tf_op jit(solution)/shard_map/advance/pallas_call | solution.py:787
  90.9 1.9 %collective-permute-start.2 = (f32[4,8,128]{2,1,0:T(8,128)S(1)}, f32[4,8,128]{2,1,0:T(8,128)S(1)}, u32[]{:S(2)}, u32[]{:S(2)}) collective-permute-start(f32[4,8,128]{2,1,0:T(8,128)S(1)} %get-tuple-element.42), channel_id=1, source_target_pairs={{8,16},{16,8},{24,32},{32,24},{40,48},{48,40},{56,64},{64,56},{72,... | collective-permute-start | bytes 49160 | tf_op jit(solution)/shard_map/ppermute | solution.py:801
  92.8 4.7 %collective-permute-start.3 = (f32[4,8,128]{2,1,0:T(8,128)S(1)}, f32[4,8,128]{2,1,0:T(8,128)S(1)}, u32[]{:S(2)}, u32[]{:S(2)}) collective-permute-start(f32[4,8,128]{2,1,0:T(8,128)S(1)} %get-tuple-element.43), channel_id=1, source_target_pairs={{0,8},{8,0},{16,24},{24,16},{32,40},{40,32},{48,56},{56,48},{64,72... | collective-permute-start | bytes 49160 | tf_op jit(solution)/shard_map/ppermute | solution.py:801
  97.5 0.0 copy-done.1
  97.5 0.0 copy-done.2
  97.5 1.7 %settle.1 = (f32[6,16,8,128]{3,2,1,0:T(8,128)}, f32[12,16,8,128]{3,2,1,0:T(8,128)}, f32[7,16,8,128]{3,2,1,0:T(8,128)S(1)}) custom-call(f32[8,28,8,128]{3,2,1,0:T(8,128)S(1)} %all_to_all.11.recv, f32[6,16,8,128]{3,2,1,0:T(8,128)S(1)} %get-tuple-element.38.v2, f32[6,16,8,128]{3,2,1,0:T(8,128)S(1)} %get-tuple-element.39.mid, f32[6,16,8,128]{3,2,1,0:T(8,128)S(1)} %copy-done.2, ...), custom_call_target="tpu_custom_call" | custom-call | bytes 9000000 | tf_op jit(solution)/shard_map/settle/pallas_call | solution.py:787
  99.3 0.0 collective-permute-done.2.far
  99.3 0.0 collective-permute-done.3.near
  99.3 0.8 close.1
Async XLA Ops:
  0.6 11.0 %copy-start.6 = (bf16[2,128,1024]{2,1,0:T(8,128)(2,1)S(1)}, bf16[2,128,1024]{2,1,0:T(8,128)(2,1)}, u32[]{:S(2)}) copy-start(bf16[2,128,1024]{2,1,0:T(8,128)(2,1)} %constant.16.clone.wz_in) | copy-start | bytes 1572868
  0.6 11.0 %copy-start.7 = (bf16[2,2,128,512]{3,2,1,0:T(8,128)(2,1)S(1)}, bf16[2,2,128,512]{3,2,1,0:T(8,128)(2,1)}, u32[]{:S(2)}) copy-start(bf16[2,2,128,512]{3,2,1,0:T(8,128)(2,1)} %constant.15.clone.wr_in) | copy-start | bytes 1572868
  0.7 11.0 %copy-start.8 = (bf16[2,2,256,256]{3,2,1,0:T(8,128)(2,1)S(1)}, bf16[2,2,256,256]{3,2,1,0:T(8,128)(2,1)}, u32[]{:S(2)}) copy-start(bf16[2,2,256,256]{3,2,1,0:T(8,128)(2,1)} %constant.14.clone.mz_in) | copy-start | bytes 1572868
  3.5 10.7 %collective-permute-start = (f32[59,8,128]{2,1,0:T(8,128)}, f32[59,8,128]{2,1,0:T(8,128)S(1)}, u32[]{:S(2)}, u32[]{:S(2)}) collective-permute-start(f32[59,8,128]{2,1,0:T(8,128)} %get-tuple-element.26), channel_id=1, source_target_pairs={{8,16},{16,8},{24,32},{32,24},{40,48},{48,40},{56,64},{64,56},{72,... | collective-permute-start | bytes 725000 | tf_op jit(solution)/shard_map/ppermute | solution.py:801
  7.2 7.1 %collective-permute-start.1 = (f32[59,8,128]{2,1,0:T(8,128)}, f32[59,8,128]{2,1,0:T(8,128)S(1)}, u32[]{:S(2)}, u32[]{:S(2)}) collective-permute-start(f32[59,8,128]{2,1,0:T(8,128)} %get-tuple-element.27), channel_id=1, source_target_pairs={{0,8},{8,0},{16,24},{24,16},{32,40},{40,32},{48,56},{56,48},{64,72... | collective-permute-start | bytes 725000 | tf_op jit(solution)/shard_map/ppermute | solution.py:801
  11.7 1.2 %copy-start.3 = (f32[208,8,128]{2,1,0:T(8,128)S(1)}, f32[208,8,128]{2,1,0:T(8,128)}, u32[]{:S(2)}) copy-start(f32[208,8,128]{2,1,0:T(8,128)} %get-tuple-element.24.state_in) | copy-start | bytes 2555908
  12.8 0.9 copy-start.9
  13.8 1.0 %copy-start = (f32[7,16,8,128]{3,2,1,0:T(8,128)S(1)}, f32[7,16,8,128]{3,2,1,0:T(8,128)}, u32[]{:S(2)}) copy-start(f32[7,16,8,128]{3,2,1,0:T(8,128)} %s.3) | copy-start | bytes 1376260
  13.8 1.0 %copy-start.4 = (bf16[2,128,128]{2,1,0:T(8,128)(2,1)S(1)}, bf16[2,128,128]{2,1,0:T(8,128)(2,1)}, u32[]{:S(2)}) copy-start(bf16[2,128,128]{2,1,0:T(8,128)(2,1)} %constant.12.clone.dr_hbm.dr_m) | copy-start | bytes 196612
  13.8 1.2 %copy-start.5 = (bf16[2,1024,128]{2,1,0:T(8,128)(2,1)S(1)}, bf16[2,1024,128]{2,1,0:T(8,128)(2,1)}, u32[]{:S(2)}) copy-start(bf16[2,1024,128]{2,1,0:T(8,128)(2,1)} %constant.17.clone.items) | copy-start | bytes 1572868
  17.4 42.0 %copy-start.10 = (f32[8,8,256]{2,1,0:T(8,128)S(1)}, f32[8,8,256]{2,1,0:T(8,128)}, u32[]{:S(2)}) copy-start(f32[8,8,256]{2,1,0:T(8,128)} %get-tuple-element.31.coef) | copy-start | bytes 196612
  89.8 7.7 %copy-start.1 = (f32[12,16,8,128]{3,2,1,0:T(8,128)S(1)}, f32[12,16,8,128]{3,2,1,0:T(8,128)}, u32[]{:S(2)}) copy-start(f32[12,16,8,128]{3,2,1,0:T(8,128)} %psi.1) | copy-start | bytes 2359300
  89.8 7.7 %copy-start.2 = (f32[6,16,8,128]{3,2,1,0:T(8,128)S(1)}, f32[6,16,8,128]{3,2,1,0:T(8,128)}, u32[]{:S(2)}) copy-start(f32[6,16,8,128]{3,2,1,0:T(8,128)} %v.1) | copy-start | bytes 1179652
  90.9 8.4 %collective-permute-start.2 = (f32[4,8,128]{2,1,0:T(8,128)S(1)}, f32[4,8,128]{2,1,0:T(8,128)S(1)}, u32[]{:S(2)}, u32[]{:S(2)}) collective-permute-start(f32[4,8,128]{2,1,0:T(8,128)S(1)} %get-tuple-element.42), channel_id=1, source_target_pairs={{8,16},{16,8},{24,32},{32,24},{40,48},{48,40},{56,64},{64,56},{72,... | collective-permute-start | bytes 49160 | tf_op jit(solution)/shard_map/ppermute | solution.py:801
  92.8 6.5 %collective-permute-start.3 = (f32[4,8,128]{2,1,0:T(8,128)S(1)}, f32[4,8,128]{2,1,0:T(8,128)S(1)}, u32[]{:S(2)}, u32[]{:S(2)}) collective-permute-start(f32[4,8,128]{2,1,0:T(8,128)S(1)} %get-tuple-element.43), channel_id=1, source_target_pairs={{0,8},{8,0},{16,24},{24,16},{32,40},{40,32},{48,56},{56,48},{64,72... | collective-permute-start | bytes 49160 | tf_op jit(solution)/shard_map/ppermute | solution.py:801
